TPU v7x, 128 devices: a whole 4x4x4 slice. The times are simulated.
128 devices in a mesh: grp: 2 (over x_lo), gr: 8 (over z, x_hi), gc: 8 (over y, core).
Axes of the slice: x: 4 (x_hi: 2, x_lo: 2; x = x_hi * 2 + x_lo), y: 4, z: 4, core: 2. Of those that a mesh axis runs over, the one named last changes fastest.
Arguments:
- embeddings: bfloat16 [131072, 768], P(('grp', 'gr', 'gc')), parts along dimension 0, may hold values from -2000 to 2000
- sorted_slot: int32 [131072], P(('grp', 'gr', 'gc')), parts along dimension 0, may hold values from 0 to 65535, as said below
- cluster_ids: int32 [131072], P(('grp', 'gr', 'gc')), parts along dimension 0, may hold values from 0 to 31, never falling along the last dimension, each value on 1 to 5120 neighbouring positions
- block_list: int32 [128, 4], P(('grp', 'gr', 'gc')), parts along dimension 0, may hold values 0 or 1
Outputs:
- dedup_weight: float32 [131072], P(('grp', 'gr', 'gc')), parts along dimension 0
There are 2 independent parts, one for each index of `grp`. A program takes and returns all parts, laid end to end along the dimension named above; each array names one. Nothing has to cross between parts.
Inputs may be any that keep to these rules, and one draw needn't show every extreme that they name: `sorted_slot`: a permutation; the 1024 encoder-order rows of each block hold exactly 16 positions in each block of cluster-sorted rows. `cluster_ids`: ids never fall along the cluster-sorted rows.
All inputs are finite; a program needn't handle non-finite values. No bound on the sum of `block_list` on one device may be relied on, other than what follows from the above.
Results may differ from a plain program's by a relative error of at most 0.00044.
Values may be sent and summed in bfloat16 or wider, within the bound.
No kernel may reach another device: no remote copies, remote signals or barrier semaphores. Data moves between devices by JAX's collectives and lax.ppermute only.
A program may use at most 64 MiB of HBM per device.

v0:
```python
import math

import jax
import jax.numpy as jnp
from jax import lax
from jax.sharding import PartitionSpec as P

SHIFTS = 4


sharpness = 20.0
threshold = 0.8


def passed_along(value, axis, steps):
    count = lax.axis_size(axis)
    first, last = (max(0, -steps), min(count, count - steps))
    return lax.ppermute(value, axis, [(source, source + steps) for source in range(first, last)])


def normalize(sorted_rows):
    values = sorted_rows.astype(jnp.float32)
    inverse = lax.rsqrt(jnp.mean(values * values, axis=-1, keepdims=True) + 1e-06) / math.sqrt(
        sorted_rows.shape[-1]
    )
    return (values * inverse).astype(jnp.bfloat16)


def similarity(my_rows, their_rows, my_ids, their_ids):
    cosine = lax.dot_general(
        my_rows, their_rows, (((1,), (1,)), ((), ())), preferred_element_type=jnp.float32
    )
    kinship = jnp.where(my_ids[:, None] == their_ids[None, :], 1.0, 0.5)
    return kinship * jax.nn.sigmoid(sharpness * (cosine - threshold))


def row_sums(my_rows, their_rows, my_ids, their_ids, weight_now):
    return jnp.sum(similarity(my_rows, their_rows, my_ids, their_ids), axis=1) * weight_now


def relay_rows(embeddings, sorted_slot):
    rows_here = embeddings.shape[0]
    sending = jnp.argsort(sorted_slot)
    outgoing = embeddings[sending]
    targets = sorted_slot[sending]
    arrived, landing = (
        lax.all_to_all(outgoing, ("gr", "gc"), split_axis=0, concat_axis=0, tiled=True),
        lax.all_to_all(targets, ("gr", "gc"), split_axis=0, concat_axis=0, tiled=True),
    )
    return jnp.zeros_like(embeddings).at[landing % rows_here].set(arrived)


def local(embeddings, sorted_slot, cluster_ids, block_list):
    unit_rows = normalize(relay_rows(embeddings, sorted_slot))
    rows_here = unit_rows.shape[0]
    position = lax.axis_index(("gr", "gc"))
    devices = lax.axis_size(("gr", "gc"))
    listed = block_list.astype(jnp.float32)
    own_terms = similarity(unit_rows, unit_rows, cluster_ids, cluster_ids)
    row_iota = lax.broadcasted_iota(jnp.int32, (rows_here, rows_here), 0)
    col_iota = lax.broadcasted_iota(jnp.int32, (rows_here, rows_here), 1)
    dup_load = jnp.sum(jnp.where(row_iota == col_iota, 0.0, own_terms), axis=1)
    for offset in range(1, SHIFTS + 1):
        ahead_ok = (position + offset < devices).astype(jnp.float32)
        far_rows, far_ids = passed_along((unit_rows, cluster_ids), ("gr", "gc"), -offset)
        dup_load = dup_load + row_sums(
            unit_rows, far_rows, cluster_ids, far_ids, listed[0, offset - 1] * ahead_ok
        )
        near_rows, near_ids, near_list = passed_along(
            (unit_rows, cluster_ids, block_list), ("gr", "gc"), offset
        )
        near_flag = near_list.astype(jnp.float32)[0, offset - 1]
        dup_load = dup_load + row_sums(unit_rows, near_rows, cluster_ids, near_ids, near_flag)
    return 1.0 / (1.0 + dup_load)


def solution(mesh):
    in_specs = (
        P(("grp", "gr", "gc"), None),
        P(("grp", "gr", "gc")),
        P(("grp", "gr", "gc")),
        P(("grp", "gr", "gc"), None),
    )
    out_specs = P(("grp", "gr", "gc"))
    return jax.shard_map(local, mesh=mesh, in_specs=in_specs, out_specs=out_specs, check_vma=False)
```

profile of v0, /device:TPU:34, one launch (start us, length us, event | category | flops | bytes accessed | tf_op | source)
XLA Modules:
  0.0 336.4 jit_solution(1428782948806836032)
XLA Ops:
  0.0 5.2 %sort.17 = (s32[1024]{0:T(1024)}, s32[1024]{0:T(1024)S(1)}) sort(s32[1024]{0:T(1024)} %param.5, s32[1024]{0:T(1024)S(1)} %iota.16), dimensions={0}, to_apply=%region_0.0 | sort | flops 10240 | bytes 16384 | tf_op jit(solution)/shard_map/jit(argsort)/sort | solution.py:43
  5.2 4.5 %gather_fusion = s32[1024]{0:T(1024)S(1)} fusion(s32[1024]{0:T(1024)S(1)} %copy-done.1, s32[1024]{0:T(1024)S(1)} %fusion.4), kind=kCustom, calls=%fused_computation | custom fusion | bytes 12288 | tf_op jit(solution)/shard_map/gather | solution.py:45
  9.7 0.7 all_to_all.16
  10.4 10.2 %all-to-all-start = ((s32[64,16,1]{1,2,0:T(1,128)}), s32[64,16,1]{1,2,0:T(1,128)S(1)}, u32[]{:S(2)}, u32[]{:S(2)}) async-start(s32[64,16,1]{1,2,0:T(1,128)} %bitcast), calls=%async_computation | async-start | bytes 65536 | tf_op jit(solution)/shard_map/all_to_all | solution.py:48
  20.6 5.2 %gather_fusion.1 = bf16[1024,768]{1,0:T(8,128)(2,1)} fusion(bf16[1024,768]{1,0:T(8,128)(2,1)S(1)} %copy-done, s32[1024]{0:T(1024)S(1)} %fusion.4), kind=kCustom, calls=%fused_computation.1 | custom fusion | bytes 3149824 | tf_op jit(solution)/shard_map/gather | solution.py:44
  25.8 3.3 all-to-all-done
  29.1 7.0 %all-to-all-start.1 = ((bf16[64,16,768]{2,1,0:T(8,128)(2,1)}), bf16[64,16,768]{2,1,0:T(8,128)(2,1)S(1)}, u32[]{:S(2)}, u32[]{:S(2)}) async-start(bf16[64,16,768]{2,1,0:T(8,128)(2,1)} %bitcast.2), calls=%async_computation.1 | async-start | bytes 3145728 | tf_op jit(solution)/shard_map/all_to_all | solution.py:47
  36.2 0.5 broadcast.147
  36.7 0.7 reduce.3
  37.4 0.1 all_to_all.18
  37.5 22.5 %all-to-all-done.1 = bf16[64,16,768]{2,1,0:T(8,128)(2,1)S(1)} async-done(((bf16[64,16,768]{2,1,0:T(8,128)(2,1)}), bf16[64,16,768]{2,1,0:T(8,128)(2,1)S(1)}, u32[]{:S(2)}, u32[]{:S(2)}) %all-to-all-start.1) | async-done | bytes 1572896 | tf_op jit(solution)/shard_map/all_to_all | solution.py:47
  60.0 1.2 copy-done.2
  61.2 6.2 %scatter_custom_fusion = bf16[1024,768]{1,0:T(8,128)(2,1)S(1)} fusion(s32[1024]{0:T(1024)S(1)} %bitcast.33, bf16[1024,768]{1,0:T(8,128)(2,1)} %bitcast.32, bf16[]{:T(256)} %constant.54.clone.1), kind=kCustom, calls=%fused_computation.17 | custom fusion | bytes 1573376 | tf_op jit(solution)/shard_map/scatter | solution.py:50
  67.4 0.4 fusion
  67.8 0.0 copy-start.3
  67.8 0.0 copy-start.4
  67.8 1.5 fusion.1
  69.3 3.0 collective-permute-start.8
  72.3 1.9 collective-permute-start.7
  74.2 8.4 %collective-permute-start.5 = (s32[1024]{0:T(1024)S(1)}, s32[1024]{0:T(1024)S(1)}, u32[]{:S(2)}, u32[]{:S(2)}) collective-permute-start(s32[1024]{0:T(1024)S(1)} %copy-done.3), channel_id=1, source_target_pairs={{2,0},{3,1},{4,2},{5,3},{6,4},{7,5},{8,6},{9,7},{10,8},{11,9},{12,... | collective-permute-start | bytes 12296 | tf_op jit(solution)/shard_map/ppermute | solution.py:18
  82.7 1.9 collective-permute-start.2
  84.6 1.9 collective-permute-start.19
  86.6 0.7 fusion.6
  89.8 16.2 %collective-permute-done.19 = s32[1,4]{1,0:T(1,128)S(1)} collective-permute-done((s32[1,4]{1,0:T(1,128)S(1)}, s32[1,4]{1,0:T(1,128)S(1)}, u32[]{:S(2)}, u32[]{:S(2)}) %collective-permute-start.19) | collective-permute-done | bytes 48 | tf_op jit(solution)/shard_map/ppermute | solution.py:18
  106.0 9.4 %collective-permute-start.9 = (s32[1,4]{1,0:T(1,128)S(1)}, s32[1,4]{1,0:T(1,128)S(1)}, u32[]{:S(2)}, u32[]{:S(2)}) collective-permute-start(s32[1,4]{1,0:T(1,128)S(1)} %copy-done.4), channel_id=1, source_target_pairs={{0,2},{1,3},{2,4},{3,5},{4,6},{5,7},{6,8},{7,9},{8,10},{9,11},{10,... | collective-permute-start | bytes 56 | tf_op jit(solution)/shard_map/ppermute | solution.py:18
  115.4 0.6 slice.31
  116.0 0.7 collective-permute-done.9
  116.6 1.9 collective-permute-start.14
  118.6 0.6 slice.27
  119.2 7.1 %collective-permute-done.14 = s32[1,4]{1,0:T(1,128)S(1)} collective-permute-done((s32[1,4]{1,0:T(1,128)S(1)}, s32[1,4]{1,0:T(1,128)S(1)}, u32[]{:S(2)}, u32[]{:S(2)}) %collective-permute-start.14) | collective-permute-done | bytes 48 | tf_op jit(solution)/shard_map/ppermute | solution.py:18
  126.3 1.9 collective-permute-start.4
  128.2 0.7 slice.29
  128.9 6.8 %collective-permute-done.4 = s32[1,4]{1,0:T(1,128)S(1)} collective-permute-done((s32[1,4]{1,0:T(1,128)S(1)}, s32[1,4]{1,0:T(1,128)S(1)}, u32[]{:S(2)}, u32[]{:S(2)}) %collective-permute-start.4) | collective-permute-done | bytes 48 | tf_op jit(solution)/shard_map/ppermute | solution.py:18
  135.6 1.9 collective-permute-start.6
  137.6 4.5 %select_reduce_fusion = f32[1024]{0:T(1024)S(1)} fusion(s32[1024]{0:T(1024)S(1)} %copy-done.3, bf16[1024,768]{1,0:T(8,128)(2,1)} %fusion.1), kind=kOutput, calls=%fused_computation.11 | convolution fusion | flops 1622146048 | bytes 1581056 | tf_op jit(solution)/shard_map/dot_general | solution.py:30
  142.0 0.0 collective-permute-done.7
  142.0 1.9 collective-permute-start
  144.0 0.0 collective-permute-done.8
  144.0 2.4 collective-permute-start.3
  146.4 4.2 %multiply_reduce_fusion.4 = f32[1024]{0:T(1024)S(1)} fusion(s32[1024]{0:T(1024)S(1)} %copy-done.3, s32[1024]{0:T(1024)S(1)} %collective-permute-done.7, bf16[1024,768]{1,0:T(8,128)(2,1)} %fusion.1, bf16[1024,768]{1,0:T(8,128)(2,1)S(1)} %collective-permute-done.8), kind=kOutput, calls=%fused_computation.7 | convolution fusion | flops 1620048896 | bytes 3158016 | tf_op jit(solution)/shard_map/dot_general | solution.py:30
  150.6 0.0 collective-permute-done.5
  150.6 1.9 collective-permute-start.10
  152.5 19.1 %collective-permute-done.6 = bf16[1024,768]{1,0:T(8,128)(2,1)S(1)} collective-permute-done((bf16[1024,768]{1,0:T(8,128)(2,1)}, bf16[1024,768]{1,0:T(8,128)(2,1)S(1)}, u32[]{:S(2)}, u32[]{:S(2)}) %collective-permute-start.6) | collective-permute-done | bytes 1572896 | tf_op jit(solution)/shard_map/ppermute | solution.py:18
  171.6 7.5 %collective-permute-start.1 = (bf16[1024,768]{1,0:T(8,128)(2,1)}, bf16[1024,768]{1,0:T(8,128)(2,1)S(1)}, u32[]{:S(2)}, u32[]{:S(2)}) collective-permute-start(bf16[1024,768]{1,0:T(8,128)(2,1)} %fusion.1), channel_id=1, source_target_pairs={{1,0},{2,1},{3,2},{4,3},{5,4},{6,5},{7,6},{8,7},{9,8},{10,9},{11,1... | collective-permute-start | bytes 4718600 | tf_op jit(solution)/shard_map/ppermute | solution.py:18
  179.2 4.2 %multiply_reduce_fusion.5 = f32[1024]{0:T(1024)S(1)} fusion(s32[1024]{0:T(1024)S(1)} %copy-done.3, s32[1024]{0:T(1024)S(1)} %collective-permute-done.5, bf16[1024,768]{1,0:T(8,128)(2,1)} %fusion.1, bf16[1024,768]{1,0:T(8,128)(2,1)S(1)} %collective-permute-done.6), kind=kOutput, calls=%fused_computation.8 | convolution fusion | flops 1620048896 | bytes 3158016 | tf_op jit(solution)/shard_map/dot_general | solution.py:30
  183.3 0.0 collective-permute-done.2
  183.3 1.9 collective-permute-start.12
  185.3 8.4 %collective-permute-start.11 = (bf16[1024,768]{1,0:T(8,128)(2,1)}, bf16[1024,768]{1,0:T(8,128)(2,1)S(1)}, u32[]{:S(2)}, u32[]{:S(2)}) collective-permute-start(bf16[1024,768]{1,0:T(8,128)(2,1)} %fusion.1), channel_id=1, source_target_pairs={{3,0},{4,1},{5,2},{6,3},{7,4},{8,5},{9,6},{10,7},{11,8},{12,9},{13... | collective-permute-start | bytes 4718600 | tf_op jit(solution)/shard_map/ppermute | solution.py:18
  193.7 4.2 %multiply_reduce_fusion.6 = f32[1024]{0:T(1024)S(1)} fusion(s32[1024]{0:T(1024)S(1)} %copy-done.3, s32[1024]{0:T(1024)S(1)} %collective-permute-done.2, bf16[1024,768]{1,0:T(8,128)(2,1)} %fusion.1, bf16[1024,768]{1,0:T(8,128)(2,1)S(1)} %collective-permute-done.3), kind=kOutput, calls=%fused_computation.9 | convolution fusion | flops 1620048896 | bytes 3158016 | tf_op jit(solution)/shard_map/dot_general | solution.py:30
  198.0 1.9 collective-permute-start.15
  199.9 15.6 %collective-permute-done.1 = bf16[1024,768]{1,0:T(8,128)(2,1)S(1)} collective-permute-done((bf16[1024,768]{1,0:T(8,128)(2,1)}, bf16[1024,768]{1,0:T(8,128)(2,1)S(1)}, u32[]{:S(2)}, u32[]{:S(2)}) %collective-permute-start.1) | collective-permute-done | bytes 1572896 | tf_op jit(solution)/shard_map/ppermute | solution.py:18
  215.5 1.9 collective-permute-start.13
  217.4 4.2 %multiply_reduce_fusion.7 = f32[1024]{0:T(1024)S(1)} fusion(s32[1024]{0:T(1024)S(1)} %copy-done.3, s32[1024]{0:T(1024)S(1)} %collective-permute-done, bf16[1024,768]{1,0:T(8,128)(2,1)} %fusion.1, bf16[1024,768]{1,0:T(8,128)(2,1)S(1)} %collective-permute-done.1), kind=kOutput, calls=%fused_computation.10 | convolution fusion | flops 1620048896 | bytes 3158016 | tf_op jit(solution)/shard_map/dot_general | solution.py:30
  221.6 8.8 %collective-permute-start.17 = (s32[1024]{0:T(1024)S(1)}, s32[1024]{0:T(1024)S(1)}, u32[]{:S(2)}, u32[]{:S(2)}) collective-permute-start(s32[1024]{0:T(1024)S(1)} %copy-done.3), channel_id=1, source_target_pairs={{0,4},{1,5},{2,6},{3,7},{4,8},{5,9},{6,10},{7,11},{8,12},{9,13},{1... | collective-permute-start | bytes 12296 | tf_op jit(solution)/shard_map/ppermute | solution.py:18
  230.5 12.4 %collective-permute-done.11 = bf16[1024,768]{1,0:T(8,128)(2,1)S(1)} collective-permute-done((bf16[1024,768]{1,0:T(8,128)(2,1)}, bf16[1024,768]{1,0:T(8,128)(2,1)S(1)}, u32[]{:S(2)}, u32[]{:S(2)}) %collective-permute-start.11) | collective-permute-done | bytes 1572896 | tf_op jit(solution)/shard_map/ppermute | solution.py:18
  242.9 1.9 collective-permute-start.16
  244.8 4.2 %multiply_reduce_fusion.3 = f32[1024]{0:T(1024)S(1)} fusion(s32[1024]{0:T(1024)S(1)} %copy-done.3, s32[1024]{0:T(1024)S(1)} %collective-permute-done.10, bf16[1024,768]{1,0:T(8,128)(2,1)} %fusion.1, bf16[1024,768]{1,0:T(8,128)(2,1)S(1)} %collective-permute-done.11), kind=kOutput, calls=%fused_computation.6 | convolution fusion | flops 1620048896 | bytes 3158016 | tf_op jit(solution)/shard_map/dot_general | solution.py:30
  249.0 5.4 %collective-permute-start.18 = (bf16[1024,768]{1,0:T(8,128)(2,1)}, bf16[1024,768]{1,0:T(8,128)(2,1)S(1)}, u32[]{:S(2)}, u32[]{:S(2)}) collective-permute-start(bf16[1024,768]{1,0:T(8,128)(2,1)} %fusion.1), channel_id=1, source_target_pairs={{0,4},{1,5},{2,6},{3,7},{4,8},{5,9},{6,10},{7,11},{8,12},{9,13},{1... | collective-permute-start | bytes 4718600 | tf_op jit(solution)/shard_map/ppermute | solution.py:18
  254.4 47.8 %collective-permute-done.13 = bf16[1024,768]{1,0:T(8,128)(2,1)S(1)} collective-permute-done((bf16[1024,768]{1,0:T(8,128)(2,1)}, bf16[1024,768]{1,0:T(8,128)(2,1)S(1)}, u32[]{:S(2)}, u32[]{:S(2)}) %collective-permute-start.13) | collective-permute-done | bytes 1572896 | tf_op jit(solution)/shard_map/ppermute | solution.py:18
  302.3 4.2 %multiply_reduce_fusion.2 = f32[1024]{0:T(1024)S(1)} fusion(s32[1024]{0:T(1024)S(1)} %copy-done.3, s32[1024]{0:T(1024)S(1)} %collective-permute-done.12, bf16[1024,768]{1,0:T(8,128)(2,1)} %fusion.1, bf16[1024,768]{1,0:T(8,128)(2,1)S(1)} %collective-permute-done.13), kind=kOutput, calls=%fused_computation.5 | convolution fusion | flops 1620048896 | bytes 3158016 | tf_op jit(solution)/shard_map/dot_general | solution.py:30
  306.5 19.1 %collective-permute-done.16 = bf16[1024,768]{1,0:T(8,128)(2,1)S(1)} collective-permute-done((bf16[1024,768]{1,0:T(8,128)(2,1)}, bf16[1024,768]{1,0:T(8,128)(2,1)S(1)}, u32[]{:S(2)}, u32[]{:S(2)}) %collective-permute-start.16) | collective-permute-done | bytes 1572896 | tf_op jit(solution)/shard_map/ppermute | solution.py:18
  325.5 4.2 %multiply_reduce_fusion.1 = f32[1024]{0:T(1024)S(1)} fusion(s32[1024]{0:T(1024)S(1)} %copy-done.3, s32[1024]{0:T(1024)S(1)} %collective-permute-done.15, bf16[1024,768]{1,0:T(8,128)(2,1)} %fusion.1, bf16[1024,768]{1,0:T(8,128)(2,1)S(1)} %collective-permute-done.16), kind=kOutput, calls=%fused_computation.4 | convolution fusion | flops 1620048896 | bytes 3158016 | tf_op jit(solution)/shard_map/dot_general | solution.py:30
  329.7 4.2 %multiply_reduce_fusion = f32[1024]{0:T(1024)S(1)} fusion(s32[1024]{0:T(1024)S(1)} %copy-done.3, s32[1024]{0:T(1024)S(1)} %collective-permute-done.17, bf16[1024,768]{1,0:T(8,128)(2,1)} %fusion.1, bf16[1024,768]{1,0:T(8,128)(2,1)S(1)} %collective-permute-done.18), kind=kOutput, calls=%fused_computation.3 | convolution fusion | flops 1620048896 | bytes 3158016 | tf_op jit(solution)/shard_map/dot_general | solution.py:30
  333.9 2.5 add_divide_fusion
  (23 shorter events, 0.1 us)
Async XLA Ops:
  0.0 20.6 %copy-start = (bf16[1024,768]{1,0:T(8,128)(2,1)S(1)}, bf16[1024,768]{1,0:T(8,128)(2,1)}, u32[]{:S(2)}) copy-start(bf16[1024,768]{1,0:T(8,128)(2,1)} %param.4) | copy-start | bytes 4718596
  0.0 5.2 %copy-start.1 = (s32[1024]{0:T(1024)S(1)}, s32[1024]{0:T(1024)}, u32[]{:S(2)}) copy-start(s32[1024]{0:T(1024)} %param.5) | copy-start | bytes 12292
  10.4 18.7 %all-to-all-start = ((s32[64,16,1]{1,2,0:T(1,128)}), s32[64,16,1]{1,2,0:T(1,128)S(1)}, u32[]{:S(2)}, u32[]{:S(2)}) async-start(s32[64,16,1]{1,2,0:T(1,128)} %bitcast), calls=%async_computation | async-start | bytes 65536 | tf_op jit(solution)/shard_map/all_to_all | solution.py:48
  29.1 30.9 %all-to-all-start.1 = ((bf16[64,16,768]{2,1,0:T(8,128)(2,1)}), bf16[64,16,768]{2,1,0:T(8,128)(2,1)S(1)}, u32[]{:S(2)}, u32[]{:S(2)}) async-start(bf16[64,16,768]{2,1,0:T(8,128)(2,1)} %bitcast.2), calls=%async_computation.1 | async-start | bytes 3145728 | tf_op jit(solution)/shard_map/all_to_all | solution.py:47
  60.0 1.2 copy-start.2
  67.8 4.5 %copy-start.3 = (s32[1024]{0:T(1024)S(1)}, s32[1024]{0:T(1024)}, u32[]{:S(2)}) copy-start(s32[1024]{0:T(1024)} %param.6) | copy-start | bytes 12292
  67.8 16.8 %copy-start.4 = (s32[1,4]{1,0:T(1,128)S(1)}, s32[1,4]{1,0:T(1,128)}, u32[]{:S(2)}) copy-start(s32[1,4]{1,0:T(1,128)} %param.7) | copy-start | bytes 52
  69.3 74.7 %collective-permute-start.8 = (bf16[1024,768]{1,0:T(8,128)(2,1)}, bf16[1024,768]{1,0:T(8,128)(2,1)S(1)}, u32[]{:S(2)}, u32[]{:S(2)}) collective-permute-start(bf16[1024,768]{1,0:T(8,128)(2,1)} %fusion.1), channel_id=1, source_target_pairs={{0,2},{1,3},{2,4},{3,5},{4,6},{5,7},{6,8},{7,9},{8,10},{9,11},{10,... | collective-permute-start | bytes 4718600 | tf_op jit(solution)/shard_map/ppermute | solution.py:18
  72.3 69.7 %collective-permute-start.7 = (s32[1024]{0:T(1024)S(1)}, s32[1024]{0:T(1024)S(1)}, u32[]{:S(2)}, u32[]{:S(2)}) collective-permute-start(s32[1024]{0:T(1024)S(1)} %copy-done.3), channel_id=1, source_target_pairs={{0,2},{1,3},{2,4},{3,5},{4,6},{5,7},{6,8},{7,9},{8,10},{9,11},{10,... | collective-permute-start | bytes 12296 | tf_op jit(solution)/shard_map/ppermute | solution.py:18
  74.2 76.3 %collective-permute-start.5 = (s32[1024]{0:T(1024)S(1)}, s32[1024]{0:T(1024)S(1)}, u32[]{:S(2)}, u32[]{:S(2)}) collective-permute-start(s32[1024]{0:T(1024)S(1)} %copy-done.3), channel_id=1, source_target_pairs={{2,0},{3,1},{4,2},{5,3},{6,4},{7,5},{8,6},{9,7},{10,8},{11,9},{12,... | collective-permute-start | bytes 12296 | tf_op jit(solution)/shard_map/ppermute | solution.py:18
  82.7 100.7 %collective-permute-start.2 = (s32[1024]{0:T(1024)S(1)}, s32[1024]{0:T(1024)S(1)}, u32[]{:S(2)}, u32[]{:S(2)}) collective-permute-start(s32[1024]{0:T(1024)S(1)} %copy-done.3), channel_id=1, source_target_pairs={{0,1},{1,2},{2,3},{3,4},{4,5},{5,6},{6,7},{7,8},{8,9},{9,10},{10,1... | collective-permute-start | bytes 12296 | tf_op jit(solution)/shard_map/ppermute | solution.py:18
  84.6 21.4 %collective-permute-start.19 = (s32[1,4]{1,0:T(1,128)S(1)}, s32[1,4]{1,0:T(1,128)S(1)}, u32[]{:S(2)}, u32[]{:S(2)}) collective-permute-start(s32[1,4]{1,0:T(1,128)S(1)} %copy-done.4), channel_id=1, source_target_pairs={{0,4},{1,5},{2,6},{3,7},{4,8},{5,9},{6,10},{7,11},{8,12},{9,13},{1... | collective-permute-start | bytes 56 | tf_op jit(solution)/shard_map/ppermute | solution.py:18
  106.0 10.7 %collective-permute-start.9 = (s32[1,4]{1,0:T(1,128)S(1)}, s32[1,4]{1,0:T(1,128)S(1)}, u32[]{:S(2)}, u32[]{:S(2)}) collective-permute-start(s32[1,4]{1,0:T(1,128)S(1)} %copy-done.4), channel_id=1, source_target_pairs={{0,2},{1,3},{2,4},{3,5},{4,6},{5,7},{6,8},{7,9},{8,10},{9,11},{10,... | collective-permute-start | bytes 56 | tf_op jit(solution)/shard_map/ppermute | solution.py:18
  116.6 9.7 %collective-permute-start.14 = (s32[1,4]{1,0:T(1,128)S(1)}, s32[1,4]{1,0:T(1,128)S(1)}, u32[]{:S(2)}, u32[]{:S(2)}) collective-permute-start(s32[1,4]{1,0:T(1,128)S(1)} %copy-done.4), channel_id=1, source_target_pairs={{0,3},{1,4},{2,5},{3,6},{4,7},{5,8},{6,9},{7,10},{8,11},{9,12},{10... | collective-permute-start | bytes 56 | tf_op jit(solution)/shard_map/ppermute | solution.py:18
  126.3 9.4 %collective-permute-start.4 = (s32[1,4]{1,0:T(1,128)S(1)}, s32[1,4]{1,0:T(1,128)S(1)}, u32[]{:S(2)}, u32[]{:S(2)}) collective-permute-start(s32[1,4]{1,0:T(1,128)S(1)} %copy-done.4), channel_id=1, source_target_pairs={{0,1},{1,2},{2,3},{3,4},{4,5},{5,6},{6,7},{7,8},{8,9},{9,10},{10,1... | collective-permute-start | bytes 56 | tf_op jit(solution)/shard_map/ppermute | solution.py:18
  135.6 36.0 %collective-permute-start.6 = (bf16[1024,768]{1,0:T(8,128)(2,1)}, bf16[1024,768]{1,0:T(8,128)(2,1)S(1)}, u32[]{:S(2)}, u32[]{:S(2)}) collective-permute-start(bf16[1024,768]{1,0:T(8,128)(2,1)} %fusion.1), channel_id=1, source_target_pairs={{2,0},{3,1},{4,2},{5,3},{6,4},{7,5},{8,6},{9,7},{10,8},{11,9},{12,... | collective-permute-start | bytes 4718600 | tf_op jit(solution)/shard_map/ppermute | solution.py:18
  142.0 55.9 %collective-permute-start = (s32[1024]{0:T(1024)S(1)}, s32[1024]{0:T(1024)S(1)}, u32[]{:S(2)}, u32[]{:S(2)}) collective-permute-start(s32[1024]{0:T(1024)S(1)} %copy-done.3), channel_id=1, source_target_pairs={{1,0},{2,1},{3,2},{4,3},{5,4},{6,5},{7,6},{8,7},{9,8},{10,9},{11,1... | collective-permute-start | bytes 12296 | tf_op jit(solution)/shard_map/ppermute | solution.py:18
  144.0 41.3 %collective-permute-start.3 = (bf16[1024,768]{1,0:T(8,128)(2,1)}, bf16[1024,768]{1,0:T(8,128)(2,1)S(1)}, u32[]{:S(2)}, u32[]{:S(2)}) collective-permute-start(bf16[1024,768]{1,0:T(8,128)(2,1)} %fusion.1), channel_id=1, source_target_pairs={{0,1},{1,2},{2,3},{3,4},{4,5},{5,6},{6,7},{7,8},{8,9},{9,10},{10,1... | collective-permute-start | bytes 4718600 | tf_op jit(solution)/shard_map/ppermute | solution.py:18
  150.6 71.1 %collective-permute-start.10 = (s32[1024]{0:T(1024)S(1)}, s32[1024]{0:T(1024)S(1)}, u32[]{:S(2)}, u32[]{:S(2)}) collective-permute-start(s32[1024]{0:T(1024)S(1)} %copy-done.3), channel_id=1, source_target_pairs={{3,0},{4,1},{5,2},{6,3},{7,4},{8,5},{9,6},{10,7},{11,8},{12,9},{13... | collective-permute-start | bytes 12296 | tf_op jit(solution)/shard_map/ppermute | solution.py:18
  171.6 43.9 %collective-permute-start.1 = (bf16[1024,768]{1,0:T(8,128)(2,1)}, bf16[1024,768]{1,0:T(8,128)(2,1)S(1)}, u32[]{:S(2)}, u32[]{:S(2)}) collective-permute-start(bf16[1024,768]{1,0:T(8,128)(2,1)} %fusion.1), channel_id=1, source_target_pairs={{1,0},{2,1},{3,2},{4,3},{5,4},{6,5},{7,6},{8,7},{9,8},{10,9},{11,1... | collective-permute-start | bytes 4718600 | tf_op jit(solution)/shard_map/ppermute | solution.py:18
  183.3 65.7 %collective-permute-start.12 = (s32[1024]{0:T(1024)S(1)}, s32[1024]{0:T(1024)S(1)}, u32[]{:S(2)}, u32[]{:S(2)}) collective-permute-start(s32[1024]{0:T(1024)S(1)} %copy-done.3), channel_id=1, source_target_pairs={{0,3},{1,4},{2,5},{3,6},{4,7},{5,8},{6,9},{7,10},{8,11},{9,12},{10... | collective-permute-start | bytes 12296 | tf_op jit(solution)/shard_map/ppermute | solution.py:18
  185.3 57.6 %collective-permute-start.11 = (bf16[1024,768]{1,0:T(8,128)(2,1)}, bf16[1024,768]{1,0:T(8,128)(2,1)S(1)}, u32[]{:S(2)}, u32[]{:S(2)}) collective-permute-start(bf16[1024,768]{1,0:T(8,128)(2,1)} %fusion.1), channel_id=1, source_target_pairs={{3,0},{4,1},{5,2},{6,3},{7,4},{8,5},{9,6},{10,7},{11,8},{12,9},{13... | collective-permute-start | bytes 4718600 | tf_op jit(solution)/shard_map/ppermute | solution.py:18
  198.0 108.5 %collective-permute-start.15 = (s32[1024]{0:T(1024)S(1)}, s32[1024]{0:T(1024)S(1)}, u32[]{:S(2)}, u32[]{:S(2)}) collective-permute-start(s32[1024]{0:T(1024)S(1)} %copy-done.3), channel_id=1, source_target_pairs={{4,0},{5,1},{6,2},{7,3},{8,4},{9,5},{10,6},{11,7},{12,8},{13,9},{1... | collective-permute-start | bytes 12296 | tf_op jit(solution)/shard_map/ppermute | solution.py:18
  215.5 86.8 %collective-permute-start.13 = (bf16[1024,768]{1,0:T(8,128)(2,1)}, bf16[1024,768]{1,0:T(8,128)(2,1)S(1)}, u32[]{:S(2)}, u32[]{:S(2)}) collective-permute-start(bf16[1024,768]{1,0:T(8,128)(2,1)} %fusion.1), channel_id=1, source_target_pairs={{0,3},{1,4},{2,5},{3,6},{4,7},{5,8},{6,9},{7,10},{8,11},{9,12},{10... | collective-permute-start | bytes 4718600 | tf_op jit(solution)/shard_map/ppermute | solution.py:18
  221.6 108.0 %collective-permute-start.17 = (s32[1024]{0:T(1024)S(1)}, s32[1024]{0:T(1024)S(1)}, u32[]{:S(2)}, u32[]{:S(2)}) collective-permute-start(s32[1024]{0:T(1024)S(1)} %copy-done.3), channel_id=1, source_target_pairs={{0,4},{1,5},{2,6},{3,7},{4,8},{5,9},{6,10},{7,11},{8,12},{9,13},{1... | collective-permute-start | bytes 12296 | tf_op jit(solution)/shard_map/ppermute | solution.py:18
  242.9 82.6 %collective-permute-start.16 = (bf16[1024,768]{1,0:T(8,128)(2,1)}, bf16[1024,768]{1,0:T(8,128)(2,1)S(1)}, u32[]{:S(2)}, u32[]{:S(2)}) collective-permute-start(bf16[1024,768]{1,0:T(8,128)(2,1)} %fusion.1), channel_id=1, source_target_pairs={{4,0},{5,1},{6,2},{7,3},{8,4},{9,5},{10,6},{11,7},{12,8},{13,9},{1... | collective-permute-start | bytes 4718600 | tf_op jit(solution)/shard_map/ppermute | solution.py:18
  249.0 80.7 %collective-permute-start.18 = (bf16[1024,768]{1,0:T(8,128)(2,1)}, bf16[1024,768]{1,0:T(8,128)(2,1)S(1)}, u32[]{:S(2)}, u32[]{:S(2)}) collective-permute-start(bf16[1024,768]{1,0:T(8,128)(2,1)} %fusion.1), channel_id=1, source_target_pairs={{0,4},{1,5},{2,6},{3,7},{4,8},{5,9},{6,10},{7,11},{8,12},{9,13},{1... | collective-permute-start | bytes 4718600 | tf_op jit(solution)/shard_map/ppermute | solution.py:18
where the time goes:
time: 339 us; the launch traced here: 336 us
  waiting for transfers between devices  171 us (50%)
  starting transfers between devices  93.7 us (28%)
  matrix products  37.9 us (11%)
  local copies, waits for them, and re-layouts  20.9 us (6%)
  other arithmetic  10.3 us (3%)
    ppermute x20, waiting for transfers between devices, passed_along(): lax.ppermute(value, axis, [(source, source + steps) for source in range(f...  145 us
    ppermute x20, starting transfers between devices, passed_along(): lax.ppermute(value, axis, [(source, source + steps) for source in range(f...  76.4 us
    dot_general x9, matrix products, similarity(): lax.dot_general(my_rows, their_rows, (((1,), (1,)), ((), ())), preferred_...  37.9 us
    all_to_all x1, waiting for transfers between devices, relay_rows(): lax.all_to_all(outgoing, ('gr', 'gc'), split_axis=0, concat_axis=0, tiled...  22.5 us
    all_to_all x1, starting transfers between devices, relay_rows(): lax.all_to_all(targets, ('gr', 'gc'), split_axis=0, concat_axis=0, tiled=...  10.2 us
    all_to_all x1, starting transfers between devices, relay_rows(): lax.all_to_all(outgoing, ('gr', 'gc'), split_axis=0, concat_axis=0, tiled...  7.05 us
  transfers between devices with their start and end apart: 22, of which 11 were waited for; matrix products, arithmetic and copies ran while one was open for 13% of the time, Pallas kernels for 0%

commit v1 on v0

v1 whole, which is shorter than its diff:
```python
import functools
import math

import jax
import jax.numpy as jnp
from jax import lax
from jax.experimental import pallas as pl
from jax.experimental.pallas import tpu as pltpu
from jax.sharding import PartitionSpec as P

SHIFTS = 4
ROWS = 1024
WIDTH = 768
LANES = 128
CHUNKS = 2
PART = ROWS // CHUNKS
AXES = ("gr", "gc")

sharpness = 20.0
threshold = 0.8

F32 = jnp.float32
BF16 = jnp.bfloat16
VMEM = pl.BlockSpec(memory_space=pltpu.VMEM)
ANY = pl.BlockSpec(memory_space=pl.ANY)


def iota(shape, axis):
    return lax.broadcasted_iota(jnp.int32, shape, axis)


def one_hot(rows, first, wanted):
    hit = iota((rows, wanted.shape[1]), 0) + first == wanted
    return jnp.where(hit, 1.0, 0.0).astype(BF16)


def nt(a, b):
    return lax.dot_general(a, b, (((1,), (1,)), ((), ())), preferred_element_type=F32)


def front_kernel(devices, emb_ref, slot_ref, out_ref, land_ref, unit_ref):
    per_pair = ROWS // devices
    for step in range(4):
        part = pl.ds(step * 256, 256)
        values = emb_ref[part, :].astype(F32)
        mean = jnp.sum(values * values, axis=1, keepdims=True) * (1.0 / WIDTH)
        inverse = lax.rsqrt(mean + 1e-06) * (1.0 / math.sqrt(WIDTH))
        unit_ref[part, :] = (values * inverse).astype(BF16)
    slot = slot_ref[...]
    target = slot // ROWS
    low = slot - target * ROWS
    goes = iota((devices, ROWS), 0) == target
    goes_b = jnp.where(goes, 1.0, 0.0).astype(BF16)
    before = jnp.where(iota((ROWS, ROWS), 0) < iota((ROWS, ROWS), 1), 1.0, 0.0).astype(BF16)
    count = jnp.dot(goes_b, before, preferred_element_type=F32)
    rank = jnp.sum(jnp.where(goes, count, 0.0), axis=0, keepdims=True)
    dest = target * per_pair + rank.astype(jnp.int32)
    low_hi = low // 32
    low_lo = low - low_hi * 32
    which = iota((8, ROWS), 0)
    digits = jnp.where(which == 0, low_hi.astype(F32), jnp.where(which == 1, low_lo.astype(F32), 0.0)).astype(BF16)
    for step in range(4):
        part = pl.ds(step * 256, 256)
        place = one_hot(256, step * 256, dest)
        out_ref[part, :] = jnp.dot(place, unit_ref[...], preferred_element_type=F32).astype(BF16)
        sent = nt(digits, place)
        land_ref[:, part] = (sent[0:1, :] * 32.0 + sent[1:2, :]).astype(jnp.int32)


def meta_kernel(land_ref, ids_ref, list_ref, out_ref):
    ids = jnp.broadcast_to(ids_ref[...].astype(F32), (8, ROWS)).astype(BF16)
    arrived = jnp.zeros((8, ROWS), F32)
    for step in range(4):
        place = one_hot(256, step * 256, land_ref[...])
        arrived = arrived + jnp.dot(ids[:, step * 256:(step + 1) * 256], place, preferred_element_type=F32)
    out_ref[:, 0:ROWS] = arrived[0:1, :].astype(jnp.int32)
    out_ref[:, ROWS:ROWS + LANES] = list_ref[...]


def weight_of(meta_ref, shift):
    entries = meta_ref[:, ROWS:ROWS + LANES].astype(F32)
    return jnp.sum(jnp.where(iota((1, LANES), 1) == shift - 1, entries, 0.0), axis=1, keepdims=True)


def ids_row(meta_ref, part=None):
    where = slice(0, ROWS) if part is None else slice(part * PART, (part + 1) * PART)
    return meta_ref[:, where].astype(F32)


def as_column(row):
    return jnp.transpose(jnp.broadcast_to(row, (LANES, row.shape[1])))


def tile_terms(scores, id_col, id_row, masked):
    rows, cols = scores.shape
    over_cols, over_rows = None, []
    for lane in range(cols // LANES):
        cut = slice(lane * LANES, (lane + 1) * LANES)
        half = jnp.tanh(scores[:, cut] * (0.5 * sharpness) - 0.5 * sharpness * threshold)
        factor = jnp.where(id_col == id_row[:, cut], 0.5, 0.25)
        term = factor * (1.0 + half)
        if masked:
            term = jnp.where(iota(term.shape, 0) == iota(term.shape, 1) + lane * LANES, 0.0, term)
        over_cols = term if over_cols is None else over_cols + term
        over_rows.append(jnp.sum(term.reshape(rows // 8, 8, LANES), axis=0))
    return over_cols, jnp.concatenate(over_rows, axis=1)


def pair(a_ref, a_base, a_rows, a_col, b_ref, b_base, b_rows, b_row, weight, row_acc, row_base, col_acc, col_base):
    height, breadth = 256, 512

    def step(i, carry):
        a_at = pl.multiple_of(i * height, height)
        a = a_ref[pl.ds(a_base + a_at, height), :]
        col = a_col[pl.ds(a_at, height), :]
        total = None
        for j in range(b_rows // breadth):
            scores = nt(a, b_ref[pl.ds(b_base + j * breadth, breadth), :])
            by_row, by_col = tile_terms(scores, col, b_row[:, j * breadth:(j + 1) * breadth], False)
            total = by_row if total is None else total + by_row
            at = pl.ds(col_base + j * breadth, breadth)
            col_acc[:, at] = col_acc[:, at] + weight * by_col
        at = pl.ds(row_base + a_at, height)
        row_acc[at, :] = row_acc[at, :] + weight * total
        return carry

    lax.fori_loop(0, a_rows // height, step, 0)


def own_pair(ref, col_ref, row, row_acc, col_acc):
    size = 256
    for i in range(ROWS // size):
        a = ref[i * size:(i + 1) * size, :]
        col = col_ref[i * size:(i + 1) * size, :]
        for j in range(i, ROWS // size):
            cut = slice(j * size, (j + 1) * size)
            by_row, by_col = tile_terms(nt(a, ref[cut, :]), col, row[:, cut], i == j)
            at = slice(i * size, (i + 1) * size)
            row_acc[at, :] = row_acc[at, :] + by_row
            if j > i:
                col_acc[:, cut] = col_acc[:, cut] + by_col


def fold_rows(acc):
    return jnp.sum(jnp.transpose(acc[...]), axis=0, keepdims=True)


def fold_cols(acc):
    return jnp.sum(acc[...], axis=0, keepdims=True)


def fetch(copies):
    started = []
    for source, target, sem in copies:
        copy = pltpu.make_async_copy(source, target, sem)
        copy.start()
        started.append(copy)
    return started


def stage0_kernel(core_ref, meta, meta_sw, own, sw, own_out, sw_out, v_own, v_sw, col, row_acc, col_acc, sw_acc, sems):
    got = fetch([(own, v_own, sems.at[0]), (sw, v_sw, sems.at[1])])
    row_acc[...] = jnp.zeros_like(row_acc)
    col_acc[...] = jnp.zeros_like(col_acc)
    sw_acc[...] = jnp.zeros_like(sw_acc)
    col[...] = as_column(ids_row(meta))
    got[0].wait()
    own_pair(v_own, col, ids_row(meta), row_acc, col_acc)
    got[1].wait()

    @pl.when(core_ref[0] == 1)
    def _():
        pair(v_own, 0, ROWS, col, v_sw, 0, ROWS, ids_row(meta_sw), weight_of(meta_sw, 1), row_acc, 0, sw_acc, 0)

    own_out[...] = fold_rows(row_acc) + fold_cols(col_acc)
    sw_out[...] = fold_cols(sw_acc)


def stage1_kernel(
    core_ref, meta, meta_sw, meta_m, meta_p, own, sw, m0, p0, own_in, sw_in,
    own_out, sw_out, m_out, p_out,
    v_own, v_sw, v_m, v_p, m_col, p_col, own_acc, sw_acc, m_acc, p_acc, p_row_acc, sems,
):
    got = fetch([(m0, v_m, sems.at[0]), (own, v_own, sems.at[1]), (p0, v_p, sems.at[2]), (sw, v_sw, sems.at[3])])
    for acc in (own_acc, sw_acc, m_acc, p_acc, p_row_acc):
        acc[...] = jnp.zeros_like(acc)
    m_col[...] = as_column(ids_row(meta_m, 0))
    p_col[...] = as_column(ids_row(meta_p, 0))
    got[0].wait()
    got[1].wait()
    pair(v_m, 0, PART, m_col, v_own, 0, ROWS, ids_row(meta), weight_of(meta_m, 2), m_acc, 0, own_acc, 0)
    got[2].wait()
    pair(v_m, 0, PART, m_col, v_p, 0, PART, ids_row(meta_p, 0), weight_of(meta_m, 4), m_acc, 0, p_acc, 0)
    got[3].wait()

    @pl.when(core_ref[0] == 0)
    def _():
        pair(v_m, 0, PART, m_col, v_sw, 0, ROWS, ids_row(meta_sw), weight_of(meta_m, 3), m_acc, 0, sw_acc, 0)
        pair(v_p, 0, PART, p_col, v_sw, 0, ROWS, ids_row(meta_sw), weight_of(meta_sw, 1), p_row_acc, 0, sw_acc, 0)

    own_out[...] = own_in[...] + fold_cols(own_acc)
    sw_out[...] = sw_in[...] + fold_cols(sw_acc)
    m_out[...] = fold_rows(m_acc)
    p_out[...] = fold_cols(p_acc) + fold_rows(p_row_acc)


def stage2_kernel(
    core_ref, meta, meta_sw, meta_m, meta_p, meta_x, own, sw, m0, p0, x0, m1, p1, own_in, sw_in, m_in, p_in,
    own_out, sw_out, m_out, p_out, x_out,
    v_own, v_sw, v_m, v_p, v_x, m_col, p_col, own_acc, sw_acc, m_acc, p_acc, p_row_acc, x_acc, sems,
):
    first, second = pl.ds(0, PART), pl.ds(PART, PART)
    got = fetch([
        (m1, v_m.at[second, :], sems.at[0]), (own, v_own, sems.at[1]), (p0, v_p.at[first, :], sems.at[2]),
        (p1, v_p.at[second, :], sems.at[3]), (m0, v_m.at[first, :], sems.at[4]),
        (sw, v_sw, sems.at[5]), (x0, v_x, sems.at[6]),
    ])
    for acc in (own_acc, sw_acc, m_acc, p_acc, p_row_acc, x_acc):
        acc[...] = jnp.zeros_like(acc)
    m_col[...] = as_column(ids_row(meta_m))
    p_col[...] = as_column(ids_row(meta_p, 1))
    m_col1 = m_col.at[second, :]
    got[0].wait()
    got[1].wait()
    pair(v_m, PART, PART, m_col1, v_own, 0, ROWS, ids_row(meta), weight_of(meta_m, 2), m_acc, PART, own_acc, 0)
    got[2].wait()
    got[3].wait()
    w_mp = weight_of(meta_m, 4)
    pair(v_m, PART, PART, m_col1, v_p, 0, ROWS, ids_row(meta_p), w_mp, m_acc, PART, p_acc, 0)
    got[4].wait()
    pair(v_m, 0, PART, m_col, v_p, PART, PART, ids_row(meta_p, 1), w_mp, m_acc, 0, p_acc, PART)
    got[5].wait()
    got[6].wait()

    @pl.when(core_ref[0] == 0)
    def _():
        pair(v_m, PART, PART, m_col1, v_sw, 0, ROWS, ids_row(meta_sw), weight_of(meta_m, 3), m_acc, PART, sw_acc, 0)
        pair(v_p, PART, PART, p_col, v_sw, 0, ROWS, ids_row(meta_sw), weight_of(meta_sw, 1), p_row_acc, PART, sw_acc, 0)

    @pl.when(core_ref[0] == 1)
    def _():
        pair(v_m, 0, ROWS, m_col, v_x, 0, PART, ids_row(meta_x, 0), weight_of(meta_m, 3), m_acc, 0, x_acc, 0)

    own_out[...] = own_in[...] + fold_cols(own_acc)
    sw_out[...] = sw_in[...] + fold_cols(sw_acc)
    m_out[...] = fold_rows(m_acc)
    m_out[:, 0:PART] = m_out[:, 0:PART] + m_in[...]
    p_out[...] = fold_cols(p_acc) + fold_rows(p_row_acc)
    p_out[:, 0:PART] = p_out[:, 0:PART] + p_in[...]
    x_out[...] = fold_cols(x_acc)


def stage3_kernel(core_ref, meta_m, meta_x, m0, m1, x1, m_in, m_out, x_out, v_m, v_x, m_col, m_acc, x_acc, sems):
    m_out[...] = m_in[...]
    x_out[...] = jnp.zeros_like(x_out)

    @pl.when(core_ref[0] == 1)
    def _():
        first, second = pl.ds(0, PART), pl.ds(PART, PART)
        got = fetch([(m0, v_m.at[first, :], sems.at[0]), (m1, v_m.at[second, :], sems.at[1]), (x1, v_x, sems.at[2])])
        m_acc[...] = jnp.zeros_like(m_acc)
        x_acc[...] = jnp.zeros_like(x_acc)
        m_col[...] = as_column(ids_row(meta_m))
        for copy in got:
            copy.wait()
        pair(v_m, 0, ROWS, m_col, v_x, 0, PART, ids_row(meta_x, 1), weight_of(meta_m, 3), m_acc, 0, x_acc, 0)
        m_out[...] = m_in[...] + fold_rows(m_acc)
        x_out[...] = fold_cols(x_acc)


def end_kernel(land_ref, *refs):
    out_ref = refs[-1]
    load = refs[0][...]
    for ref in refs[1:-1]:
        load = load + ref[...]
    result = 1.0 / (1.0 + load)
    high = result.astype(BF16).astype(F32)
    mid = (result - high).astype(BF16).astype(F32)
    low = result - high - mid
    which = iota((8, ROWS), 0)
    parts = jnp.where(which == 0, high, jnp.where(which == 1, mid, jnp.where(which == 2, low, 0.0))).astype(BF16)
    for step in range(4):
        placed = nt(parts, one_hot(256, step * 256, land_ref[...]))
        out_ref[:, step * 256:(step + 1) * 256] = placed[0:1, :] + placed[1:2, :] + placed[2:3, :]


def vec(n):
    return jax.ShapeDtypeStruct((1, n), F32)


def rows_vmem(n):
    return pltpu.VMEM((n, WIDTH), BF16)


def call(kernel, out_shape, in_specs, scratch, tasks, args, mib=40):
    single = not isinstance(out_shape, (list, tuple))
    return pl.pallas_call(
        kernel,
        out_shape=out_shape,
        in_specs=in_specs,
        out_specs=VMEM if single else [VMEM] * len(out_shape),
        scratch_shapes=scratch,
        compiler_params=pltpu.CompilerParams(vmem_limit_bytes=mib << 20),
        cost_estimate=pl.CostEstimate(
            flops=int(tasks * 2 * ROWS * ROWS * WIDTH),
            transcendentals=int(tasks * ROWS * ROWS),
            bytes_accessed=int((1 + tasks) * 2 * ROWS * WIDTH),
        ),
    )(*args)


def move(value, devices, change, only=None):
    pairs = [
        (p, change(p))
        for p in range(devices)
        if 0 <= change(p) < devices and (only is None or p % 2 == only)
    ]
    return lax.ppermute(value, AXES, pairs)


def local(embeddings, sorted_slot, cluster_ids, block_list):
    devices = lax.axis_size(AXES)
    position = lax.axis_index(AXES)
    core = (position % 2).astype(jnp.int32).reshape(1)
    SMEM = pl.BlockSpec(memory_space=pltpu.SMEM)
    move_d = functools.partial(move, devices=devices)
    acc_rows, acc_cols = (lambda n: pltpu.VMEM((n, LANES), F32)), (lambda n: pltpu.VMEM((8, n), F32))
    sems = lambda n: pltpu.SemaphoreType.DMA((n,))

    outgoing, land_out = call(
        functools.partial(front_kernel, devices),
        [jax.ShapeDtypeStruct((ROWS, WIDTH), BF16), jax.ShapeDtypeStruct((1, ROWS), jnp.int32)],
        [VMEM, VMEM], [rows_vmem(ROWS)], 1, (embeddings, sorted_slot.reshape(1, ROWS)),
    )
    own = lax.all_to_all(outgoing, AXES, split_axis=0, concat_axis=0, tiled=True)
    land = lax.all_to_all(
        land_out.reshape(devices, ROWS // devices), AXES, split_axis=0, concat_axis=0, tiled=True
    ).reshape(1, ROWS)
    reach = position + 1 + jnp.arange(SHIFTS, dtype=jnp.int32)
    entries = jnp.pad(jnp.where(reach[None, :] < devices, block_list, 0), ((0, 0), (0, LANES - SHIFTS)))
    meta = call(
        meta_kernel, jax.ShapeDtypeStruct((1, ROWS + LANES), jnp.int32), [VMEM] * 3, [], 0.2,
        (land, cluster_ids.reshape(1, ROWS), entries),
    )
    swap = lambda p: p ^ 1
    up, down = (lambda p: p + 2), (lambda p: p - 2)
    meta_sw = move_d(meta, change=swap)
    meta_m = move_d(meta, change=up)
    meta_p = move_d(meta, change=down)
    meta_x = move_d(meta_p, change=swap, only=0)

    sw = move_d(own, change=swap)
    halves = [own[i * PART:(i + 1) * PART] for i in range(CHUNKS)]
    m = [move_d(h, change=up) for h in halves]
    p = [move_d(h, change=down) for h in halves]
    x = [move_d(h, change=swap, only=0) for h in p]

    own_s, sw_s = call(
        stage0_kernel, [vec(ROWS)] * 2, [SMEM] + [VMEM] * 2 + [ANY] * 2,
        [rows_vmem(ROWS)] * 2 + [acc_rows(ROWS)] * 2 + [acc_cols(ROWS)] * 2 + [sems(2)],
        1.6, (core, meta, meta_sw, own, sw),
    )
    own_s, sw_s, m_s, p_s = call(
        stage1_kernel, [vec(ROWS)] * 2 + [vec(PART)] * 2, [SMEM] + [VMEM] * 4 + [ANY] * 4 + [VMEM] * 2,
        [rows_vmem(ROWS)] * 2 + [rows_vmem(PART)] * 2 + [acc_rows(PART)] * 2
        + [acc_cols(ROWS)] * 2 + [acc_rows(PART), acc_cols(PART), acc_rows(PART)] + [sems(4)],
        1.7, (core, meta, meta_sw, meta_m, meta_p, own, sw, m[0], p[0], own_s, sw_s),
    )
    own_s, sw_s, m_s, p_s, x_s = call(
        stage2_kernel, [vec(ROWS)] * 4 + [vec(PART)], [SMEM] + [VMEM] * 5 + [ANY] * 7 + [VMEM] * 4,
        [rows_vmem(ROWS)] * 4 + [rows_vmem(PART)] + [acc_rows(ROWS), acc_rows(PART)]
        + [acc_cols(ROWS)] * 2 + [acc_rows(ROWS), acc_cols(ROWS), acc_rows(ROWS), acc_cols(PART)] + [sems(7)],
        2.2, (core, meta, meta_sw, meta_m, meta_p, meta_x, own, sw, m[0], p[0], x[0], m[1], p[1], own_s, sw_s, m_s, p_s),
    )
    m_s, x_s1 = call(
        stage3_kernel, [vec(ROWS), vec(PART)], [SMEM] + [VMEM] * 2 + [ANY] * 3 + [VMEM],
        [rows_vmem(ROWS), rows_vmem(PART), acc_rows(ROWS), acc_rows(ROWS), acc_cols(PART), sems(3)],
        0.5, (core, meta_m, meta_x, m[0], m[1], x[1], m_s),
    )
    x_all = jnp.concatenate([x_s, x_s1], axis=1)
    returned = [
        own_s,
        move_d(sw_s, change=swap),
        move_d(p_s, change=up),
        move_d(m_s, change=down),
        move_d(x_all, change=lambda q: q + 1, only=1),
    ]
    weights = call(end_kernel, vec(ROWS), [VMEM] * 6, [], 0.2, (land, *returned))
    return weights.reshape(ROWS)


def solution(mesh):
    in_specs = (
        P(("grp", "gr", "gc"), None),
        P(("grp", "gr", "gc")),
        P(("grp", "gr", "gc")),
        P(("grp", "gr", "gc"), None),
    )
    out_specs = P(("grp", "gr", "gc"))
    return jax.shard_map(local, mesh=mesh, in_specs=in_specs, out_specs=out_specs, check_vma=False)
```

time: 339 us -> 151 us (0.45)
  waiting for transfers between devices: 171 us -> 38.6 us
  starting transfers between devices: 93.7 us -> 48.9 us
  matrix products: 37.9 us -> 0 us
  blocking collectives: 0 us -> 33.8 us
  Pallas kernels: 0 us -> 22.2 us
  local copies, waits for them, and re-layouts: 20.9 us -> 4.66 us
  other arithmetic: 10.3 us -> 1.4 us
    ppermute x20 -> x15, waiting for transfers between devices: 145 us -> 15.8 us  [move(): return lax.ppermute(value, AXES, pairs)]
    dot_general x9 -> x0, matrix products: 37.9 us -> none  [similarity(): lax.dot_general(my_rows, their_rows, (((1,), (1,)), ((), ())), preferred_...]
    ppermute x20 -> x15, starting transfers between devices: 76.4 us -> 41.8 us  [move(): return lax.ppermute(value, AXES, pairs)]
    all_to_all x0 -> x1, blocking collectives: none -> 33.8 us  [local(): lax.all_to_all(outgoing, AXES, split_axis=0, concat_axis=0, tiled=True)]
    pallas_call x0 -> x7, Pallas kernels: none -> 22.2 us  [call(): pl.pallas_call(kernel, out_shape=out_shape, in_specs=in_specs, out_specs=...]
    all_to_all x2 -> x1, starting transfers between devices: 17.2 us -> 7.14 us  [local(): lax.all_to_all(land_out.reshape(devices, ROWS // devices), AXES, split_ax...]
    gather x2 -> x0, local copies, waits for them, and re-layouts: 9.74 us -> none  [the longest x1 5.21 us: relay_rows(): outgoing = embeddings[sending]]
    scatter x1 -> x0, local copies, waits for them, and re-layouts: 6.21 us -> none  [relay_rows(): return jnp.zeros_like(embeddings).at[landing % rows_here].set(arrived)]
  transfers between devices with their start and end apart: 22 -> 16, of which waited for: 11 -> 4; matrix products, arithmetic and copies ran while one was open for 13% -> 2% of each run, Pallas kernels for 0% -> 12%
where the time goes in v1:
time: 151 us; the launch traced here: 150 us
  starting transfers between devices  48.9 us (32%)
  waiting for transfers between devices  38.6 us (26%)
  blocking collectives  33.8 us (22%)
  Pallas kernels  22.2 us (15%)
  local copies, waits for them, and re-layouts  4.66 us (3%)
    ppermute x15, starting transfers between devices, move(): return lax.ppermute(value, AXES, pairs)  41.8 us
    all_to_all x1, blocking collectives, local(): lax.all_to_all(outgoing, AXES, split_axis=0, concat_axis=0, tiled=True)  33.8 us
    all_to_all x1, waiting for transfers between devices, local(): lax.all_to_all(land_out.reshape(devices, ROWS // devices), AXES, split_ax...  22.9 us
    pallas_call x7, Pallas kernels, call(): pl.pallas_call(kernel, out_shape=out_shape, in_specs=in_specs, out_specs=...  22.2 us
    ppermute x15, waiting for transfers between devices, move(): return lax.ppermute(value, AXES, pairs)  15.8 us
    all_to_all x1, starting transfers between devices, local(): lax.all_to_all(land_out.reshape(devices, ROWS // devices), AXES, split_ax...  7.14 us
  transfers between devices with their start and end apart: 16, of which 4 were waited for; matrix products, arithmetic and copies ran while one was open for 2% of the time, Pallas kernels for 12%

profile of v1, /device:TPU:34, one launch (start us, length us, event | category | flops | bytes accessed | tf_op | source)
XLA Modules:
  0.0 149.9 jit_solution(13103210801987263503)
XLA Ops:
  0.0 0.0 copy-start
  0.0 1.4 copy-done
  1.4 0.0 copy-start.1
  1.4 0.7 copy-done.1
  2.1 3.1 %shard_map.46 = (bf16[1024,768]{1,0:T(8,128)(2,1)S(1)}, s32[1,1024]{1,0:T(1,128)S(1)}) custom-call(bf16[1024,768]{1,0:T(8,128)(2,1)S(1)} %copy-done, s32[1,1024]{1,0:T(1,128)S(1)} %bitcast.14), custom_call_target="tpu_custom_call" | custom-call | flops 1610612736 | bytes 3145728 | tf_op jit(solution)/shard_map/pallas_call | solution.py:297
  5.2 33.8 %all_to_all.20 = bf16[64,16,768]{2,1,0:T(8,128)(2,1)S(1)} all-to-all(bf16[64,16,768]{2,1,0:T(8,128)(2,1)S(1)} %bitcast.13), channel_id=1, replica_groups=mesh['grp'=2,'gr'=8,'gc'=8] {'gr','gc'}, dimensions={0} | all-to-all | bytes 3145728 | tf_op jit(solution)/shard_map/all_to_all | solution.py:335
  39.0 0.0 copy-start.3
  39.0 0.0 copy-start.2
  39.0 0.3 collective-permute-start.4
  39.3 1.3 fusion
  40.6 4.3 %collective-permute-start.6 = (bf16[512,768]{1,0:T(8,128)(2,1)}, bf16[512,768]{1,0:T(8,128)(2,1)}, u32[]{:S(2)}, u32[]{:S(2)}) collective-permute-start(bf16[512,768]{1,0:T(8,128)(2,1)} %bitcast.6), channel_id=1, source_target_pairs={{2,0},{3,1},{4,2},{5,3},{6,4},{7,5},{8,6},{9,7},{10,8},{11,9},{12,... | collective-permute-start | bytes 2359304 | tf_op jit(solution)/shard_map/ppermute | solution.py:318
  44.8 2.4 %collective-permute-start.9 = (bf16[512,768]{1,0:T(8,128)(2,1)}, bf16[512,768]{1,0:T(8,128)(2,1)}, u32[]{:S(2)}, u32[]{:S(2)}) collective-permute-start(bf16[512,768]{1,0:T(8,128)(2,1)} %bitcast.7), channel_id=1, source_target_pairs={{2,0},{3,1},{4,2},{5,3},{6,4},{7,5},{8,6},{9,7},{10,8},{11,9},{12,... | collective-permute-start | bytes 2359304 | tf_op jit(solution)/shard_map/ppermute | solution.py:318
  47.2 0.5 broadcast.29
  47.7 0.7 reduce.6
  48.4 0.7 all_to_all.13
  49.1 7.1 %all-to-all-start = ((s32[64,1,16]{2,1,0:T(1,128)}), s32[64,1,16]{2,1,0:T(1,128)S(1)}, u32[]{:S(2)}, u32[]{:S(2)}) async-start(s32[64,1,16]{2,1,0:T(1,128)} %bitcast.1), calls=%async_computation | async-start | bytes 65536 | tf_op jit(solution)/shard_map/all_to_all | solution.py:336
  56.2 3.4 %collective-permute-start.5 = (bf16[512,768]{1,0:T(8,128)(2,1)}, bf16[512,768]{1,0:T(8,128)(2,1)}, u32[]{:S(2)}, u32[]{:S(2)}) collective-permute-start(bf16[512,768]{1,0:T(8,128)(2,1)} %bitcast.6), channel_id=1, source_target_pairs={{0,2},{1,3},{2,4},{3,5},{4,6},{5,7},{6,8},{7,9},{8,10},{9,11},{10,... | collective-permute-start | bytes 2359304 | tf_op jit(solution)/shard_map/ppermute | solution.py:318
  59.6 0.0 copy-done.3
  59.6 22.9 %all-to-all-done = s32[64,1,16]{2,1,0:T(1,128)S(1)} async-done(((s32[64,1,16]{2,1,0:T(1,128)}), s32[64,1,16]{2,1,0:T(1,128)S(1)}, u32[]{:S(2)}, u32[]{:S(2)}) %all-to-all-start) | async-done | bytes 4128 | tf_op jit(solution)/shard_map/all_to_all | solution.py:336
  82.5 0.7 reduce.7
  83.2 0.1 reshape.36.land_ref
  83.3 0.0 copy-done.2
  83.3 0.4 shard_map.47.meta
  83.7 0.2 collective-permute-start
  83.9 1.0 collective-permute-done.meta_sw
  84.9 3.4 %collective-permute-start.1 = (s32[1,1152]{1,0:T(1,128)S(1)}, s32[1,1152]{1,0:T(1,128)S(1)}, u32[]{:S(2)}, u32[]{:S(2)}) collective-permute-start(s32[1,1152]{1,0:T(1,128)S(1)} %shard_map.47.meta), channel_id=1, source_target_pairs={{0,2},{1,3},{2,4},{3,5},{4,6},{5,7},{6,8},{7,9},{8,10},{9,11},{10,... | collective-permute-start | bytes 13832 | tf_op jit(solution)/shard_map/ppermute | solution.py:318
  88.3 6.6 %collective-permute-done.1.meta_m = s32[1,1152]{1,0:T(1,128)S(1)} collective-permute-done((s32[1,1152]{1,0:T(1,128)S(1)}, s32[1,1152]{1,0:T(1,128)S(1)}, u32[]{:S(2)}, u32[]{:S(2)}) %collective-permute-start.1) | collective-permute-done | bytes 4640 | tf_op jit(solution)/shard_map/ppermute | solution.py:318
  95.0 1.9 %collective-permute-start.8 = (bf16[512,768]{1,0:T(8,128)(2,1)}, bf16[512,768]{1,0:T(8,128)(2,1)}, u32[]{:S(2)}, u32[]{:S(2)}) collective-permute-start(bf16[512,768]{1,0:T(8,128)(2,1)} %bitcast.7), channel_id=1, source_target_pairs={{0,2},{1,3},{2,4},{3,5},{4,6},{5,7},{6,8},{7,9},{8,10},{9,11},{10,... | collective-permute-start | bytes 2359304 | tf_op jit(solution)/shard_map/ppermute | solution.py:318
  96.9 0.0 collective-permute-done.6.p0
  96.9 2.2 %collective-permute-start.7 = (bf16[512,768]{1,0:T(8,128)(2,1)}, bf16[512,768]{1,0:T(8,128)(2,1)}, u32[]{:S(2)}, u32[]{:S(2)}) collective-permute-start(bf16[512,768]{1,0:T(8,128)(2,1)} %collective-permute-done.6.p0), channel_id=1, source_target_pairs={{0,1},{2,3},{4,5},{6,7},{8,9},{10,11},{12,13},{14,15},{16,17},{18,... | collective-permute-start | bytes 2359304 | tf_op jit(solution)/shard_map/ppermute | solution.py:318
  99.1 0.0 collective-permute-done.9.p1
  99.1 8.4 %collective-permute-start.2 = (s32[1,1152]{1,0:T(1,128)S(1)}, s32[1,1152]{1,0:T(1,128)S(1)}, u32[]{:S(2)}, u32[]{:S(2)}) collective-permute-start(s32[1,1152]{1,0:T(1,128)S(1)} %shard_map.47.meta), channel_id=1, source_target_pairs={{2,0},{3,1},{4,2},{5,3},{6,4},{7,5},{8,6},{9,7},{10,8},{11,9},{12,... | collective-permute-start | bytes 13832 | tf_op jit(solution)/shard_map/ppermute | solution.py:318
  107.5 0.0 collective-permute-done.4.sw
  107.5 1.3 collective-permute-start.12
  108.9 2.0 %shard_map.48 = (f32[1,1024]{1,0:T(1,128)S(1)}, f32[1,1024]{1,0:T(1,128)S(1)}) custom-call(s32[1]{0:T(128)} %bitcast.2.core_ref, s32[1,1152]{1,0:T(1,128)S(1)} %shard_map.47.meta, s32[1,1152]{1,0:T(1,128)S(1)} %collective-permute-done.meta_sw, bf16[1024,768]{1,0:T(8,128)(2,1)S(1)} %bitcast.10, bf16[1024,768]{1,0:T(8,128)(2,1)S(1)} %collective-permute-done.4.sw), custom_call_target="tpu_custom_call" | custom-call | flops 2576980480 | bytes 4089446 | tf_op jit(solution)/shard_map/pallas_call | solution.py:297
  110.9 0.0 collective-permute-done.2.meta_p
  110.9 2.3 %collective-permute-start.3 = (s32[1,1152]{1,0:T(1,128)S(1)}, s32[1,1152]{1,0:T(1,128)S(1)}, u32[]{:S(2)}, u32[]{:S(2)}) collective-permute-start(s32[1,1152]{1,0:T(1,128)S(1)} %collective-permute-done.2.meta_p), channel_id=1, source_target_pairs={{0,1},{2,3},{4,5},{6,7},{8,9},{10,11},{12,13},{14,15},{16,17},{18,... | collective-permute-start | bytes 13832 | tf_op jit(solution)/shard_map/ppermute | solution.py:318
  113.2 0.0 collective-permute-done.5.m0
  113.2 7.0 %shard_map.49 = (f32[1,1024]{1,0:T(1,128)S(1)}, f32[1,1024]{1,0:T(1,128)S(1)}, f32[1,512]{1,0:T(1,128)S(1)}, f32[1,512]{1,0:T(1,128)S(1)}) custom-call(s32[1]{0:T(128)} %bitcast.2.core_ref, s32[1,1152]{1,0:T(1,128)S(1)} %shard_map.47.meta, s32[1,1152]{1,0:T(1,128)S(1)} %collective-permute-done.meta_sw, s32[1,1152]{1,0:T(1,128)S(1)} %collective-permute-done.1.meta_m, ...), custom_call_target="tpu_custom_call" | custom-call | flops 2738041600 | bytes 4246732 | tf_op jit(solution)/shard_map/pallas_call | solution.py:297
  120.2 0.0 collective-permute-done.3.meta_x
  120.3 0.0 collective-permute-done.8.m1
  120.3 0.0 collective-permute-done.7.x0
  120.3 8.4 %shard_map.50 = (f32[1,1024]{1,0:T(1,128)S(1)}, f32[1,1024]{1,0:T(1,128)S(1)}, f32[1,1024]{1,0:T(1,128)S(1)}, f32[1,1024]{1,0:T(1,128)S(1)}, f32[1,512]{1,0:T(1,128)S(1)}) custom-call(s32[1]{0:T(128)} %bitcast.2.core_ref, s32[1,1152]{1,0:T(1,128)S(1)} %shard_map.47.meta, s32[1,1152]{1,0:T(1,128)S(1)} %collective-permute-done.meta_sw, ...), custom_call_target="tpu_custom_call" | custom-call | flops 3543347968 | bytes 5033164 | tf_op jit(solution)/shard_map/pallas_call | solution.py:297
  128.7 0.1 collective-permute-start.10
  128.8 1.9 %collective-permute-start.11 = (f32[1,1024]{1,0:T(1,128)S(1)}, f32[1,1024]{1,0:T(1,128)S(1)}, u32[]{:S(2)}, u32[]{:S(2)}) collective-permute-start(f32[1,1024]{1,0:T(1,128)S(1)} %get-tuple-element.30), channel_id=1, source_target_pairs={{0,2},{1,3},{2,4},{3,5},{4,6},{5,7},{6,8},{7,9},{8,10},{9,11},{10,... | collective-permute-start | bytes 12296 | tf_op jit(solution)/shard_map/ppermute | solution.py:318
  130.7 0.0 collective-permute-done.12.x1
  130.8 8.4 %collective-permute-start.13 = (f32[1,1024]{1,0:T(1,128)S(1)}, f32[1,1024]{1,0:T(1,128)S(1)}, u32[]{:S(2)}, u32[]{:S(2)}) collective-permute-start(f32[1,1024]{1,0:T(1,128)S(1)} %get-tuple-element.32), channel_id=1, source_target_pairs={{2,0},{3,1},{4,2},{5,3},{6,4},{7,5},{8,6},{9,7},{10,8},{11,9},{12,... | collective-permute-start | bytes 12296 | tf_op jit(solution)/shard_map/ppermute | solution.py:318
  139.2 1.3 collective-permute-start.14
  140.5 0.0 collective-permute-done.10.refs_1_
  140.6 0.0 collective-permute-done.11.refs_2_
  140.6 0.0 collective-permute-done.13.refs_3_
  140.6 8.1 %collective-permute-done.14.refs_4_ = f32[1,1024]{1,0:T(1,128)S(1)} collective-permute-done((f32[1,1024]{1,0:T(1,128)S(1)}, f32[1,1024]{1,0:T(1,128)S(1)}, u32[]{:S(2)}, u32[]{:S(2)}) %collective-permute-start.14) | collective-permute-done | bytes 4128 | tf_op jit(solution)/shard_map/ppermute | solution.py:318
  148.7 1.3 shard_map.52
  (4 shorter events, 0.1 us)
Async XLA Ops:
  0.0 1.4 copy-start
  1.4 0.7 copy-start.1
  39.0 20.6 %copy-start.3 = (s32[1,4]{1,0:T(1,128)S(1)}, s32[1,4]{1,0:T(1,128)}, u32[]{:S(2)}) copy-start(s32[1,4]{1,0:T(1,128)} %param.7) | copy-start | bytes 52
  39.0 44.3 %copy-start.2 = (s32[1024]{0:T(1024)S(1)}, s32[1024]{0:T(1024)}, u32[]{:S(2)}) copy-start(s32[1024]{0:T(1024)} %param.6) | copy-start | bytes 12292
  39.0 68.5 %collective-permute-start.4 = (bf16[1024,768]{1,0:T(8,128)(2,1)S(1)}, bf16[1024,768]{1,0:T(8,128)(2,1)S(1)}, u32[]{:S(2)}, u32[]{:S(2)}) collective-permute-start(bf16[1024,768]{1,0:T(8,128)(2,1)S(1)} %bitcast.9), channel_id=1, source_target_pairs={{0,1},{1,0},{2,3},{3,2},{4,5},{5,4},{6,7},{7,6},{8,9},{9,8},{10,11... | collective-permute-start | bytes 4718600 | tf_op jit(solution)/shard_map/ppermute | solution.py:318
  40.6 56.3 %collective-permute-start.6 = (bf16[512,768]{1,0:T(8,128)(2,1)}, bf16[512,768]{1,0:T(8,128)(2,1)}, u32[]{:S(2)}, u32[]{:S(2)}) collective-permute-start(bf16[512,768]{1,0:T(8,128)(2,1)} %bitcast.6), channel_id=1, source_target_pairs={{2,0},{3,1},{4,2},{5,3},{6,4},{7,5},{8,6},{9,7},{10,8},{11,9},{12,... | collective-permute-start | bytes 2359304 | tf_op jit(solution)/shard_map/ppermute | solution.py:318
  44.8 54.2 %collective-permute-start.9 = (bf16[512,768]{1,0:T(8,128)(2,1)}, bf16[512,768]{1,0:T(8,128)(2,1)}, u32[]{:S(2)}, u32[]{:S(2)}) collective-permute-start(bf16[512,768]{1,0:T(8,128)(2,1)} %bitcast.7), channel_id=1, source_target_pairs={{2,0},{3,1},{4,2},{5,3},{6,4},{7,5},{8,6},{9,7},{10,8},{11,9},{12,... | collective-permute-start | bytes 2359304 | tf_op jit(solution)/shard_map/ppermute | solution.py:318
  49.1 33.4 %all-to-all-start = ((s32[64,1,16]{2,1,0:T(1,128)}), s32[64,1,16]{2,1,0:T(1,128)S(1)}, u32[]{:S(2)}, u32[]{:S(2)}) async-start(s32[64,1,16]{2,1,0:T(1,128)} %bitcast.1), calls=%async_computation | async-start | bytes 65536 | tf_op jit(solution)/shard_map/all_to_all | solution.py:336
  56.2 57.0 %collective-permute-start.5 = (bf16[512,768]{1,0:T(8,128)(2,1)}, bf16[512,768]{1,0:T(8,128)(2,1)}, u32[]{:S(2)}, u32[]{:S(2)}) collective-permute-start(bf16[512,768]{1,0:T(8,128)(2,1)} %bitcast.6), channel_id=1, source_target_pairs={{0,2},{1,3},{2,4},{3,5},{4,6},{5,7},{6,8},{7,9},{8,10},{9,11},{10,... | collective-permute-start | bytes 2359304 | tf_op jit(solution)/shard_map/ppermute | solution.py:318
  83.7 1.2 collective-permute-start
  84.9 10.0 %collective-permute-start.1 = (s32[1,1152]{1,0:T(1,128)S(1)}, s32[1,1152]{1,0:T(1,128)S(1)}, u32[]{:S(2)}, u32[]{:S(2)}) collective-permute-start(s32[1,1152]{1,0:T(1,128)S(1)} %shard_map.47.meta), channel_id=1, source_target_pairs={{0,2},{1,3},{2,4},{3,5},{4,6},{5,7},{6,8},{7,9},{8,10},{9,11},{10,... | collective-permute-start | bytes 13832 | tf_op jit(solution)/shard_map/ppermute | solution.py:318
  95.0 25.3 %collective-permute-start.8 = (bf16[512,768]{1,0:T(8,128)(2,1)}, bf16[512,768]{1,0:T(8,128)(2,1)}, u32[]{:S(2)}, u32[]{:S(2)}) collective-permute-start(bf16[512,768]{1,0:T(8,128)(2,1)} %bitcast.7), channel_id=1, source_target_pairs={{0,2},{1,3},{2,4},{3,5},{4,6},{5,7},{6,8},{7,9},{8,10},{9,11},{10,... | collective-permute-start | bytes 2359304 | tf_op jit(solution)/shard_map/ppermute | solution.py:318
  96.9 23.4 %collective-permute-start.7 = (bf16[512,768]{1,0:T(8,128)(2,1)}, bf16[512,768]{1,0:T(8,128)(2,1)}, u32[]{:S(2)}, u32[]{:S(2)}) collective-permute-start(bf16[512,768]{1,0:T(8,128)(2,1)} %collective-permute-done.6.p0), channel_id=1, source_target_pairs={{0,1},{2,3},{4,5},{6,7},{8,9},{10,11},{12,13},{14,15},{16,17},{18,... | collective-permute-start | bytes 2359304 | tf_op jit(solution)/shard_map/ppermute | solution.py:318
  99.1 11.8 %collective-permute-start.2 = (s32[1,1152]{1,0:T(1,128)S(1)}, s32[1,1152]{1,0:T(1,128)S(1)}, u32[]{:S(2)}, u32[]{:S(2)}) collective-permute-start(s32[1,1152]{1,0:T(1,128)S(1)} %shard_map.47.meta), channel_id=1, source_target_pairs={{2,0},{3,1},{4,2},{5,3},{6,4},{7,5},{8,6},{9,7},{10,8},{11,9},{12,... | collective-permute-start | bytes 13832 | tf_op jit(solution)/shard_map/ppermute | solution.py:318
  107.5 23.2 %collective-permute-start.12 = (bf16[512,768]{1,0:T(8,128)(2,1)}, bf16[512,768]{1,0:T(8,128)(2,1)S(1)}, u32[]{:S(2)}, u32[]{:S(2)}) collective-permute-start(bf16[512,768]{1,0:T(8,128)(2,1)} %collective-permute-done.9.p1), channel_id=1, source_target_pairs={{0,1},{2,3},{4,5},{6,7},{8,9},{10,11},{12,13},{14,15},{16,17},{18,... | collective-permute-start | bytes 2359304 | tf_op jit(solution)/shard_map/ppermute | solution.py:318
  110.9 9.4 %collective-permute-start.3 = (s32[1,1152]{1,0:T(1,128)S(1)}, s32[1,1152]{1,0:T(1,128)S(1)}, u32[]{:S(2)}, u32[]{:S(2)}) collective-permute-start(s32[1,1152]{1,0:T(1,128)S(1)} %collective-permute-done.2.meta_p), channel_id=1, source_target_pairs={{0,1},{2,3},{4,5},{6,7},{8,9},{10,11},{12,13},{14,15},{16,17},{18,... | collective-permute-start | bytes 13832 | tf_op jit(solution)/shard_map/ppermute | solution.py:318
  128.7 11.8 %collective-permute-start.10 = (f32[1,1024]{1,0:T(1,128)S(1)}, f32[1,1024]{1,0:T(1,128)S(1)}, u32[]{:S(2)}, u32[]{:S(2)}) collective-permute-start(f32[1,1024]{1,0:T(1,128)S(1)} %get-tuple-element.29), channel_id=1, source_target_pairs={{0,1},{1,0},{2,3},{3,2},{4,5},{5,4},{6,7},{7,6},{8,9},{9,8},{10,11... | collective-permute-start | bytes 12296 | tf_op jit(solution)/shard_map/ppermute | solution.py:318
  128.8 11.8 %collective-permute-start.11 = (f32[1,1024]{1,0:T(1,128)S(1)}, f32[1,1024]{1,0:T(1,128)S(1)}, u32[]{:S(2)}, u32[]{:S(2)}) collective-permute-start(f32[1,1024]{1,0:T(1,128)S(1)} %get-tuple-element.30), channel_id=1, source_target_pairs={{0,2},{1,3},{2,4},{3,5},{4,6},{5,7},{6,8},{7,9},{8,10},{9,11},{10,... | collective-permute-start | bytes 12296 | tf_op jit(solution)/shard_map/ppermute | solution.py:318
  130.8 9.8 %collective-permute-start.13 = (f32[1,1024]{1,0:T(1,128)S(1)}, f32[1,1024]{1,0:T(1,128)S(1)}, u32[]{:S(2)}, u32[]{:S(2)}) collective-permute-start(f32[1,1024]{1,0:T(1,128)S(1)} %get-tuple-element.32), channel_id=1, source_target_pairs={{2,0},{3,1},{4,2},{5,3},{6,4},{7,5},{8,6},{9,7},{10,8},{11,9},{12,... | collective-permute-start | bytes 12296 | tf_op jit(solution)/shard_map/ppermute | solution.py:318
  139.2 9.4 %collective-permute-start.14 = (f32[1,1024]{1,0:T(1,128)S(1)}, f32[1,1024]{1,0:T(1,128)S(1)}, u32[]{:S(2)}, u32[]{:S(2)}) collective-permute-start(f32[1,1024]{1,0:T(1,128)S(1)} %pad_maximum_fusion), channel_id=1, source_target_pairs={{1,2},{3,4},{5,6},{7,8},{9,10},{11,12},{13,14},{15,16},{17,18},{19... | collective-permute-start | bytes 12296 | tf_op jit(solution)/shard_map/ppermute | solution.py:318

commit v2 on v0

v2 whole, which is shorter than its diff:
```python
import functools
import math

import jax
import jax.numpy as jnp
from jax import lax
from jax.experimental import pallas as pl
from jax.experimental.pallas import tpu as pltpu
from jax.sharding import PartitionSpec as P

SHIFTS = 4
ROWS = 1024
WIDTH = 768
LANES = 128
SIZES = (640, 384)
STARTS = tuple(sum(SIZES[:i]) for i in range(len(SIZES)))
TAIL = 16
DIGITS = 32
AXES = ("gr", "gc")

sharpness = 20.0
threshold = 0.8

F32 = jnp.float32
BF16 = jnp.bfloat16
VMEM = pl.BlockSpec(memory_space=pltpu.VMEM)
ANY = pl.BlockSpec(memory_space=pl.ANY)
HBM = pl.BlockSpec(memory_space=pltpu.HBM)
SMEM = pl.BlockSpec(memory_space=pltpu.SMEM)


def iota(shape, axis):
    return lax.broadcasted_iota(jnp.int32, shape, axis)


def one_hot(rows, first, wanted):
    hit = iota((rows, wanted.shape[1]), 0) + first == wanted
    return jnp.where(hit, 1.0, 0.0).astype(BF16)


def nt(a, b):
    return lax.dot_general(a, b, (((1,), (1,)), ((), ())), preferred_element_type=F32)


def as_column(row):
    return jnp.transpose(jnp.broadcast_to(row, (LANES, row.shape[1])))


def front_kernel(devices, slot_ref, emb_ref, out_ref, raw_ref, unit_ref, sems):
    per_pair = ROWS // devices
    size = 256
    copies = []
    for step in range(ROWS // size):
        part = pl.ds(step * size, size)
        copy = pltpu.make_async_copy(emb_ref.at[part, :], raw_ref.at[part, :], sems.at[step])
        copy.start()
        copies.append(copy)
    slot = slot_ref[...]
    target = slot // ROWS
    low = slot - target * ROWS
    goes = iota((devices, ROWS), 0) == target
    goes_b = jnp.where(goes, 1.0, 0.0).astype(BF16)
    before = jnp.where(iota((ROWS, ROWS), 0) < iota((ROWS, ROWS), 1), 1.0, 0.0).astype(BF16)
    count = jnp.dot(goes_b, before, preferred_element_type=F32)
    rank = jnp.sum(jnp.where(goes, count, 0.0), axis=0, keepdims=True)
    dest = target * per_pair + rank.astype(jnp.int32)
    high = low // DIGITS
    lane = iota((ROWS, LANES), 1)
    digits = jnp.where(
        lane == 0,
        as_column(high.astype(F32)),
        jnp.where(lane == 1, as_column((low - high * DIGITS).astype(F32)), 0.0),
    )
    unit_ref[:, WIDTH:] = digits.astype(BF16)
    for step in range(ROWS // size):
        part = pl.ds(step * size, size)
        copies[step].wait()
        values = raw_ref[part, :].astype(F32)
        mean = jnp.sum(values * values, axis=1, keepdims=True) * (1.0 / WIDTH)
        inverse = lax.rsqrt(mean + 1e-06) * (1.0 / math.sqrt(WIDTH))
        unit_ref[part, 0:WIDTH] = (values * inverse).astype(BF16)
    for step in range(ROWS // size):
        part = pl.ds(step * size, size)
        place = one_hot(size, step * size, dest)
        out_ref[part, :] = jnp.dot(place, unit_ref[...], preferred_element_type=F32).astype(BF16)


def split_kernel(got_ref, ids_ref, list_ref, *outs):
    chunks, land_ref = outs[:-1], outs[-1]
    for size, start, out in zip(SIZES, STARTS, chunks):
        out[0:size, :] = got_ref[start:start + size, 0:WIDTH]
    digits = jnp.transpose(got_ref[:, WIDTH:].astype(F32))
    land = (digits[0:1, :] * DIGITS + digits[1:2, :]).astype(jnp.int32)
    land_ref[...] = land
    ids = jnp.broadcast_to(ids_ref[...].astype(F32), (8, ROWS)).astype(BF16)
    arrived = jnp.zeros((8, ROWS), F32)
    for step in range(4):
        place = one_hot(256, step * 256, land)
        arrived = arrived + jnp.dot(ids[:, step * 256:(step + 1) * 256], place, preferred_element_type=F32)
    entries = jnp.broadcast_to(list_ref[...].astype(F32), (TAIL, LANES)).astype(BF16)
    for size, start, out in zip(SIZES, STARTS, chunks):
        own = jnp.broadcast_to(arrived[0:1, start:start + size], (TAIL, size)).astype(BF16)
        out[size:size + TAIL, 0:WIDTH - LANES] = jnp.zeros((TAIL, WIDTH - LANES), BF16)
        out[size:size + TAIL, 0:size] = own
        out[size:size + TAIL, WIDTH - LANES:] = entries


def weight_of(ref, size, shift):
    entries = ref[size:size + TAIL, WIDTH - LANES:].astype(F32)[0:1, :]
    return jnp.sum(jnp.where(iota((1, LANES), 1) == shift - 1, entries, 0.0), axis=1, keepdims=True)


def ids_row(ref, size):
    return ref[size:size + TAIL, 0:size].astype(F32)[0:1, :]


def tile_terms(scores, id_col, id_row, masked):
    rows, cols = scores.shape
    over_cols, over_rows = None, []
    for lane in range(cols // LANES):
        cut = slice(lane * LANES, (lane + 1) * LANES)
        half = jnp.tanh(scores[:, cut] * (0.5 * sharpness) - 0.5 * sharpness * threshold)
        factor = jnp.where(id_col == id_row[:, cut], 0.5, 0.25)
        term = factor * (1.0 + half)
        if masked:
            term = jnp.where(iota(term.shape, 0) == iota(term.shape, 1) + lane * LANES, 0.0, term)
        over_cols = term if over_cols is None else over_cols + term
        over_rows.append(jnp.sum(term.reshape(rows // 8, 8, LANES), axis=0))
    return over_cols, jnp.concatenate(over_rows, axis=1)


def cuts(size, width):
    return [(at, min(width, size - at)) for at in range(0, size, width)]


def pair(a_ref, a_size, a_col, b_ref, b_size, weight, row_acc, col_acc):
    b_row = ids_row(b_ref, b_size)
    height = 128

    def step(i, carry):
        at = pl.ds(pl.multiple_of(i * height, height), height)
        a = a_ref[at, :]
        col = a_col[at, :]
        total = None
        for start, width in cuts(b_size, 512):
            part = slice(start, start + width)
            by_row, by_col = tile_terms(nt(a, b_ref[part, :]), col, b_row[:, part], False)
            total = by_row if total is None else total + by_row
            col_acc[:, part] = col_acc[:, part] + weight * by_col
        row_acc[at, :] = row_acc[at, :] + weight * total
        return carry

    lax.fori_loop(0, a_size // height, step, 0)


def own_pair(ref, size, col_ref, row_acc, col_acc):
    row = ids_row(ref, size)
    for i, height in cuts(size, 256):
        a = ref[i:i + height, :]
        col = col_ref[i:i + height, :]
        for j, width in cuts(size, 256):
            if j < i:
                continue
            by_row, by_col = tile_terms(nt(a, ref[j:j + width, :]), col, row[:, j:j + width], i == j)
            row_acc[i:i + height, :] = row_acc[i:i + height, :] + by_row
            if j > i:
                col_acc[:, j:j + width] = col_acc[:, j:j + width] + by_col


ROLES = ("own", "sw", "m", "p", "x")


def stage_kernel(blocks, tasks, first, *refs):
    core_ref, refs = refs[0], refs[1:]
    sources, refs = refs[:len(blocks)], refs[len(blocks):]
    sums_in, refs = ((None,) * len(ROLES), refs) if first else (refs[:len(ROLES)], refs[len(ROLES):])
    sums_out, refs = refs[:len(ROLES)], refs[len(ROLES):]
    held, refs = dict(zip(blocks, refs[:len(blocks)])), refs[len(blocks):]
    a_sides, b_sides = sides(tasks)
    cols, refs = dict(zip(a_sides, refs[:len(a_sides)])), refs[len(a_sides):]
    row_acc, refs = dict(zip(a_sides, refs[:len(a_sides)])), refs[len(a_sides):]
    col_acc, refs = dict(zip(b_sides, refs[:len(b_sides)])), refs[len(b_sides):]
    sems = refs[0]

    waiting = {}
    for i, block in enumerate(blocks):
        waiting[block] = pltpu.make_async_copy(sources[i], held[block], sems.at[i])
        waiting[block].start()
    for acc in (*row_acc.values(), *col_acc.values()):
        acc[...] = jnp.zeros_like(acc)
    have_cols = set()

    def need(block):
        if block in waiting:
            waiting.pop(block).wait()

    for core, a, b, holder, shift in tasks:
        for block in (a, b, holder):
            if block is not None:
                need(block)
        if a not in have_cols:
            cols[a][...] = as_column(ids_row(held[a], SIZES[a[1]]))
            have_cols.add(a)

        def run(a=a, b=b, holder=holder, shift=shift):
            if a == b:
                own_pair(held[a], SIZES[a[1]], cols[a], row_acc[a], col_acc[b])
            else:
                weight = 1.0 if holder is None else weight_of(held[holder], SIZES[holder[1]], shift)
                pair(held[a], SIZES[a[1]], cols[a], held[b], SIZES[b[1]], weight, row_acc[a], col_acc[b])

        if core is None:
            run()
        else:
            pl.when(core_ref[0] == core)(run)
    for block in list(waiting):
        need(block)
    for n, role in enumerate(ROLES):
        sums_out[n][...] = jnp.zeros((1, ROWS), F32) if first else sums_in[n][...]
    for accs, fold in ((row_acc, fold_rows), (col_acc, fold_cols)):
        for (role, chunk), acc in accs.items():
            out = sums_out[ROLES.index(role)]
            at = slice(STARTS[chunk], STARTS[chunk] + SIZES[chunk])
            out[:, at] = out[:, at] + fold(acc)


def sides(tasks):
    a_sides, b_sides = [], []
    for _, a, b, _, _ in tasks:
        if a not in a_sides:
            a_sides.append(a)
        if b not in b_sides:
            b_sides.append(b)
    return a_sides, b_sides


def fold_rows(acc):
    return jnp.sum(jnp.transpose(acc[...]), axis=0, keepdims=True)


def fold_cols(acc):
    return jnp.sum(acc[...], axis=0, keepdims=True)


def run_stage(core, arrays, tasks, sums):
    blocks = []
    for _, a, b, holder, _ in tasks:
        for block in (a, b, holder):
            if block is not None and block not in blocks:
                blocks.append(block)
    a_sides, b_sides = sides(tasks)
    scratch = [pltpu.VMEM((SIZES[c] + TAIL, WIDTH), BF16) for _, c in blocks]
    scratch += [pltpu.VMEM((SIZES[c], LANES), F32) for _, c in a_sides] * 2
    scratch += [pltpu.VMEM((8, SIZES[c]), F32) for _, c in b_sides]
    scratch.append(pltpu.SemaphoreType.DMA((len(blocks),)))
    work = sum(SIZES[a[1]] * SIZES[b[1]] * (0.5 if core_of is not None else 1.0) for core_of, a, b, _, _ in tasks) / ROWS**2
    first = sums is None
    return call(
        functools.partial(stage_kernel, blocks, tasks, first), [vec(ROWS)] * len(ROLES),
        [SMEM] + [ANY] * len(blocks) + ([] if first else [VMEM] * len(ROLES)),
        scratch, work, (core, *(arrays[b] for b in blocks), *(() if first else sums)),
    )


def end_kernel(land_ref, *refs):
    out_ref = refs[-1]
    load = refs[0][...]
    for ref in refs[1:-1]:
        load = load + ref[...]
    result = 1.0 / (1.0 + load)
    high = result.astype(BF16).astype(F32)
    mid = (result - high).astype(BF16).astype(F32)
    low = result - high - mid
    which = iota((8, ROWS), 0)
    parts = jnp.where(which == 0, high, jnp.where(which == 1, mid, jnp.where(which == 2, low, 0.0))).astype(BF16)
    for step in range(4):
        placed = nt(parts, one_hot(256, step * 256, land_ref[...]))
        out_ref[:, step * 256:(step + 1) * 256] = placed[0:1, :] + placed[1:2, :] + placed[2:3, :]


def vec(n):
    return jax.ShapeDtypeStruct((1, n), F32)


def call(kernel, out_shape, in_specs, scratch, tasks, args, mib=40):
    single = not isinstance(out_shape, (list, tuple))
    return pl.pallas_call(
        kernel,
        out_shape=out_shape,
        in_specs=in_specs,
        out_specs=VMEM if single else [VMEM] * len(out_shape),
        scratch_shapes=scratch,
        compiler_params=pltpu.CompilerParams(vmem_limit_bytes=mib << 20),
        cost_estimate=pl.CostEstimate(
            flops=int(tasks * 2 * ROWS * ROWS * WIDTH),
            transcendentals=int(tasks * ROWS * ROWS),
            bytes_accessed=int((1 + tasks) * 2 * ROWS * WIDTH),
        ),
    )(*args)


def move(value, devices, change, only=None):
    pairs = [
        (p, change(p))
        for p in range(devices)
        if 0 <= change(p) < devices and (only is None or p % 2 == only)
    ]
    return lax.ppermute(value, AXES, pairs)


def local(embeddings, sorted_slot, cluster_ids, block_list):
    devices = lax.axis_size(AXES)
    position = lax.axis_index(AXES)
    core = (position % 2).astype(jnp.int32).reshape(1)
    move_d = functools.partial(move, devices=devices)
    chunks = range(len(SIZES))

    outgoing = call(
        functools.partial(front_kernel, devices),
        jax.ShapeDtypeStruct((ROWS, WIDTH + LANES), BF16), [VMEM, HBM],
        [pltpu.VMEM((ROWS, WIDTH), BF16), pltpu.VMEM((ROWS, WIDTH + LANES), BF16), pltpu.SemaphoreType.DMA((4,))],
        1, (sorted_slot.reshape(1, ROWS), embeddings),
    )
    arrived = lax.all_to_all(outgoing, AXES, split_axis=0, concat_axis=0, tiled=True)
    reach = position + 1 + jnp.arange(SHIFTS, dtype=jnp.int32)
    entries = jnp.pad(jnp.where(reach[None, :] < devices, block_list, 0), ((0, 0), (0, LANES - SHIFTS)))
    *own, land = call(
        split_kernel,
        [jax.ShapeDtypeStruct((size + TAIL, WIDTH), BF16) for size in SIZES] + [jax.ShapeDtypeStruct((1, ROWS), jnp.int32)],
        [VMEM] * 3, [], 0.3, (arrived, cluster_ids.reshape(1, ROWS), entries),
    )
    swap = lambda p: p ^ 1
    up, down = (lambda p: p + 2), (lambda p: p - 2)
    arrays = {("own", c): own[c] for c in chunks}
    for c in chunks:
        arrays["m", c] = move_d(own[c], change=up)
        arrays["p", c] = move_d(own[c], change=down)
    for c in chunks:
        arrays["sw", c] = move_d(own[c], change=swap)
    for c in chunks:
        arrays["x", c] = move_d(arrays["p", c], change=swap, only=0)

    whole = lambda role: [(role, c) for c in chunks]
    tasks = [(None, ("own", a), ("own", b), None, 0) for a in chunks for b in chunks if a <= b]
    tasks += [(1, a, b, ("sw", 0), 1) for a in whole("own") for b in whole("sw")]
    sums = run_stage(core, arrays, tasks, None)
    for c in chunks:
        m, p = ("m", c), ("p", c)
        tasks = [(None, m, b, m, 2) for b in whole("own")]
        tasks += [(None, m, ("p", d), m, 4) for d in range(c)]
        tasks += [(None, ("m", d), p, m, 4) for d in range(c + 1)]
        tasks += [(0, m, b, m, 3) for b in whole("sw")]
        tasks += [(0, p, b, ("sw", 0), 1) for b in whole("sw")]
        tasks += [(1, ("m", d), ("x", c - 1), m, 3) for d in range(c + 1) if c > 0]
        tasks += [(1, m, ("x", e), m, 3) for e in range(c - 1)]
        sums = run_stage(core, arrays, tasks, sums)
    last = chunks[-1]
    own_s, sw_s, m_s, p_s, x_s = sums
    sw_back, p_back = move_d(sw_s, change=swap), move_d(p_s, change=up)
    tasks = [(1, ("m", d), ("x", last), ("m", last), 3) for d in chunks]
    _, _, m_s, _, x_s = run_stage(core, arrays, tasks, sums)
    returned = [own_s, sw_back, p_back, move_d(m_s, change=down), move_d(x_s, change=lambda q: q + 1, only=1)]
    weights = call(end_kernel, vec(ROWS), [VMEM] * 6, [], 0.2, (land, *returned))
    return weights.reshape(ROWS)


def solution(mesh):
    in_specs = (
        P(("grp", "gr", "gc"), None),
        P(("grp", "gr", "gc")),
        P(("grp", "gr", "gc")),
        P(("grp", "gr", "gc"), None),
    )
    out_specs = P(("grp", "gr", "gc"))
    return jax.shard_map(local, mesh=mesh, in_specs=in_specs, out_specs=out_specs, check_vma=False)
```

time: 339 us -> 147 us (0.43)
  waiting for transfers between devices: 171 us -> 56.8 us
  starting transfers between devices: 93.7 us -> 42.9 us
  Pallas kernels: 0 us -> 41.9 us
  matrix products: 37.9 us -> 0 us
  local copies, waits for them, and re-layouts: 20.9 us -> 3.37 us
  other arithmetic: 10.3 us -> 0.01 us
    ppermute x20 -> x12, waiting for transfers between devices: 145 us -> 30.3 us  [move(): return lax.ppermute(value, AXES, pairs)]
    ppermute x20 -> x12, starting transfers between devices: 76.4 us -> 32.6 us  [move(): return lax.ppermute(value, AXES, pairs)]
    pallas_call x0 -> x7, Pallas kernels: none -> 41.9 us  [call(): pl.pallas_call(kernel, out_shape=out_shape, in_specs=in_specs, out_specs=...]
    dot_general x9 -> x0, matrix products: 37.9 us -> none  [similarity(): lax.dot_general(my_rows, their_rows, (((1,), (1,)), ((), ())), preferred_...]
    gather x2 -> x0, local copies, waits for them, and re-layouts: 9.74 us -> none  [the longest x1 5.21 us: relay_rows(): outgoing = embeddings[sending]]
    all_to_all x2 -> x1, starting transfers between devices: 17.2 us -> 10.3 us  [local(): lax.all_to_all(outgoing, AXES, split_axis=0, concat_axis=0, tiled=True)]
    scatter x1 -> x0, local copies, waits for them, and re-layouts: 6.21 us -> none  [relay_rows(): return jnp.zeros_like(embeddings).at[landing % rows_here].set(arrived)]
    sort x1 -> x0, other arithmetic: 5.18 us -> none  [relay_rows(): sending = jnp.argsort(sorted_slot)]
  transfers between devices with their start and end apart: 22 -> 13, of which waited for: 11 -> 4; matrix products, arithmetic and copies ran while one was open for 13% -> 0% of each run, Pallas kernels for 0% -> 25%
where the time goes in v2:
time: 147 us; the launch traced here: 145 us
  waiting for transfers between devices  56.8 us (39%)
  starting transfers between devices  42.9 us (29%)
  Pallas kernels  41.9 us (29%)
  local copies, waits for them, and re-layouts  3.37 us (2%)
    pallas_call x7, Pallas kernels, call(): pl.pallas_call(kernel, out_shape=out_shape, in_specs=in_specs, out_specs=...  41.9 us
    ppermute x12, starting transfers between devices, move(): return lax.ppermute(value, AXES, pairs)  32.6 us
    ppermute x12, waiting for transfers between devices, move(): return lax.ppermute(value, AXES, pairs)  30.3 us
    all_to_all x1, waiting for transfers between devices, local(): lax.all_to_all(outgoing, AXES, split_axis=0, concat_axis=0, tiled=True)  26.5 us
    all_to_all x1, starting transfers between devices, local(): lax.all_to_all(outgoing, AXES, split_axis=0, concat_axis=0, tiled=True)  10.3 us
    unnamed x10, local copies, waits for them, and re-layouts  3.36 us
  transfers between devices with their start and end apart: 13, of which 4 were waited for; matrix products, arithmetic and copies ran while one was open for 0% of the time, Pallas kernels for 25%

profile of v2, /device:TPU:34, one launch (start us, length us, event | category | flops | bytes accessed | tf_op | source)
XLA Modules:
  0.0 145.3 jit_solution(8310104041695685096)
XLA Ops:
  0.0 0.0 copy-start.2
  0.0 1.4 copy-done.2
  1.4 0.0 copy-start.3
  1.4 0.7 copy-done.3
  2.1 4.1 %shard_map.46 = bf16[1024,896]{1,0:T(8,128)(2,1)S(1)} custom-call(s32[1,1024]{1,0:T(1,128)S(1)} %bitcast.9, bf16[1024,768]{1,0:T(8,128)(2,1)S(1)} %copy-done.2), custom_call_target="tpu_custom_call" | custom-call | flops 1610612736 | bytes 3145728 | tf_op jit(solution)/shard_map/pallas_call | solution.py:287
  6.2 0.0 copy-start
  6.2 1.3 copy-done
  7.4 0.0 copy-start.4
  7.4 0.0 copy-start.1
  7.4 10.3 %all-to-all-start = ((bf16[64,16,896]{2,1,0:T(8,128)(2,1)}), bf16[64,16,896]{2,1,0:T(8,128)(2,1)S(1)}, u32[]{:S(2)}, u32[]{:S(2)}) async-start(bf16[64,16,896]{2,1,0:T(8,128)(2,1)} %bitcast.7), calls=%async_computation | async-start | bytes 3670016 | tf_op jit(solution)/shard_map/all_to_all | solution.py:324
  17.8 0.0 copy-done.4
  17.8 26.5 %all-to-all-done = bf16[64,16,896]{2,1,0:T(8,128)(2,1)S(1)} async-done(((bf16[64,16,896]{2,1,0:T(8,128)(2,1)}), bf16[64,16,896]{2,1,0:T(8,128)(2,1)S(1)}, u32[]{:S(2)}, u32[]{:S(2)}) %all-to-all-start) | async-done | bytes 1835040 | tf_op jit(solution)/shard_map/all_to_all | solution.py:324
  44.3 0.0 copy-done.1
  44.3 0.5 shard_map.47
  44.8 4.7 %collective-permute-start.1 = (bf16[656,768]{1,0:T(8,128)(2,1)S(1)}, bf16[656,768]{1,0:T(8,128)(2,1)}, u32[]{:S(2)}, u32[]{:S(2)}) collective-permute-start(bf16[656,768]{1,0:T(8,128)(2,1)S(1)} %get-tuple-element.27.refs_1_.refs_2_), channel_id=1, source_target_pairs={{2,0},{3,1},{4,2},{5,3},{6,4},{7,5},{8,6},{9,7},{10,8},{11,9},{12,... | collective-permute-start | bytes 3022856 | tf_op jit(solution)/shard_map/ppermute | solution.py:308
  49.5 0.1 collective-permute-start.4
  49.6 1.9 %collective-permute-start.2 = (bf16[656,768]{1,0:T(8,128)(2,1)S(1)}, bf16[656,768]{1,0:T(8,128)(2,1)S(1)}, u32[]{:S(2)}, u32[]{:S(2)}) collective-permute-start(bf16[656,768]{1,0:T(8,128)(2,1)S(1)} %get-tuple-element.27.refs_1_.refs_2_), channel_id=1, source_target_pairs={{0,2},{1,3},{2,4},{3,5},{4,6},{5,7},{6,8},{7,9},{8,10},{9,11},{10,... | collective-permute-start | bytes 3022856 | tf_op jit(solution)/shard_map/ppermute | solution.py:308
  51.5 8.4 %collective-permute-start.3 = (bf16[400,768]{1,0:T(8,128)(2,1)S(1)}, bf16[400,768]{1,0:T(8,128)(2,1)}, u32[]{:S(2)}, u32[]{:S(2)}) collective-permute-start(bf16[400,768]{1,0:T(8,128)(2,1)S(1)} %get-tuple-element.26.refs_2_.refs_3_), channel_id=1, source_target_pairs={{2,0},{3,1},{4,2},{5,3},{6,4},{7,5},{8,6},{9,7},{10,8},{11,9},{12,... | collective-permute-start | bytes 1843208 | tf_op jit(solution)/shard_map/ppermute | solution.py:308
  60.0 0.1 collective-permute-start.5
  60.1 12.1 %collective-permute-done.1.refs_4_ = bf16[656,768]{1,0:T(8,128)(2,1)} collective-permute-done((bf16[656,768]{1,0:T(8,128)(2,1)S(1)}, bf16[656,768]{1,0:T(8,128)(2,1)}, u32[]{:S(2)}, u32[]{:S(2)}) %collective-permute-start.1) | collective-permute-done | bytes 1007648 | tf_op jit(solution)/shard_map/ppermute | solution.py:308
  72.2 2.2 %collective-permute-start.6 = (bf16[656,768]{1,0:T(8,128)(2,1)}, bf16[656,768]{1,0:T(8,128)(2,1)}, u32[]{:S(2)}, u32[]{:S(2)}) collective-permute-start(bf16[656,768]{1,0:T(8,128)(2,1)} %collective-permute-done.1.refs_4_), channel_id=1, source_target_pairs={{0,1},{2,3},{4,5},{6,7},{8,9},{10,11},{12,13},{14,15},{16,17},{18,... | collective-permute-start | bytes 3022856 | tf_op jit(solution)/shard_map/ppermute | solution.py:308
  74.4 10.0 %collective-permute-done.3.refs_6_ = bf16[400,768]{1,0:T(8,128)(2,1)} collective-permute-done((bf16[400,768]{1,0:T(8,128)(2,1)S(1)}, bf16[400,768]{1,0:T(8,128)(2,1)}, u32[]{:S(2)}, u32[]{:S(2)}) %collective-permute-start.3) | collective-permute-done | bytes 614432 | tf_op jit(solution)/shard_map/ppermute | solution.py:308
  84.5 1.9 %collective-permute-start = (bf16[400,768]{1,0:T(8,128)(2,1)S(1)}, bf16[400,768]{1,0:T(8,128)(2,1)S(1)}, u32[]{:S(2)}, u32[]{:S(2)}) collective-permute-start(bf16[400,768]{1,0:T(8,128)(2,1)S(1)} %get-tuple-element.26.refs_2_.refs_3_), channel_id=1, source_target_pairs={{0,2},{1,3},{2,4},{3,5},{4,6},{5,7},{6,8},{7,9},{8,10},{9,11},{10,... | collective-permute-start | bytes 1843208 | tf_op jit(solution)/shard_map/ppermute | solution.py:308
  86.4 0.0 collective-permute-done.5.refs_4_.refs_6_.refs_8_
  86.4 1.5 %collective-permute-start.9 = (bf16[400,768]{1,0:T(8,128)(2,1)}, bf16[400,768]{1,0:T(8,128)(2,1)S(1)}, u32[]{:S(2)}, u32[]{:S(2)}) collective-permute-start(bf16[400,768]{1,0:T(8,128)(2,1)} %collective-permute-done.3.refs_6_), channel_id=1, source_target_pairs={{0,1},{2,3},{4,5},{6,7},{8,9},{10,11},{12,13},{14,15},{16,17},{18,... | collective-permute-start | bytes 1843208 | tf_op jit(solution)/shard_map/ppermute | solution.py:308
  87.9 0.0 collective-permute-done.4.refs_3_.refs_5_.refs_7_
  87.9 3.8 %shard_map.48 = (f32[1,1024]{1,0:T(1,128)S(1)}, f32[1,1024]{1,0:T(1,128)S(1)}, f32[1,1024]{1,0:T(1,128)S(1)}, f32[1,1024]{1,0:T(1,128)S(1)}, f32[1,1024]{1,0:T(1,128)S(1)}) custom-call(s32[1]{0:T(128)} %bitcast.4.refs_0_, bf16[656,768]{1,0:T(8,128)(2,1)S(1)} %get-tuple-element.27.refs_1_.refs_2_, bf16[400,768]{1,0:T(8,128)(2,1)S(1)} %get-tuple-element.26.refs_2_.refs_3_, ...), custom_call_target="tpu_custom_call" | custom-call | flops 2038431744 | bytes 3563520 | tf_op jit(solution)/shard_map/pallas_call | solution.py:287
  91.7 0.0 collective-permute-done.2.refs_1_.refs_5_
  91.7 16.7 %shard_map.49 = (f32[1,1024]{1,0:T(1,128)S(1)}, f32[1,1024]{1,0:T(1,128)S(1)}, f32[1,1024]{1,0:T(1,128)S(1)}, f32[1,1024]{1,0:T(1,128)S(1)}, f32[1,1024]{1,0:T(1,128)S(1)}) custom-call(s32[1]{0:T(128)} %bitcast.4.refs_0_, bf16[656,768]{1,0:T(8,128)(2,1)S(1)} %collective-permute-done.2.refs_1_.refs_5_, ...), custom_call_target="tpu_custom_call" | custom-call | flops 2642411520 | bytes 4153344 | tf_op jit(solution)/shard_map/pallas_call | solution.py:287
  108.3 0.0 collective-permute-done.refs_1_.refs_3_
  108.4 0.0 collective-permute-done.6.refs_9_
  108.4 14.0 %shard_map.50 = (f32[1,1024]{1,0:T(1,128)S(1)}, f32[1,1024]{1,0:T(1,128)S(1)}, f32[1,1024]{1,0:T(1,128)S(1)}, f32[1,1024]{1,0:T(1,128)S(1)}, f32[1,1024]{1,0:T(1,128)S(1)}) custom-call(s32[1]{0:T(128)} %bitcast.4.refs_0_, bf16[400,768]{1,0:T(8,128)(2,1)S(1)} %collective-permute-done.refs_1_.refs_3_, bf16[656,768]{1,0:T(8,128)(2,1)S(1)} %get-tuple-element.27.refs_1_.refs_2_, ...), custom_call_target="tpu_custom_call" | custom-call | flops 2692743168 | bytes 4202496 | tf_op jit(solution)/shard_map/pallas_call | solution.py:287
  122.3 0.1 collective-permute-start.7
  122.4 1.9 %collective-permute-start.8 = (f32[1,1024]{1,0:T(1,128)S(1)}, f32[1,1024]{1,0:T(1,128)S(1)}, u32[]{:S(2)}, u32[]{:S(2)}) collective-permute-start(f32[1,1024]{1,0:T(1,128)S(1)} %get-tuple-element.40.refs_7_), channel_id=1, source_target_pairs={{0,2},{1,3},{2,4},{3,5},{4,6},{5,7},{6,8},{7,9},{8,10},{9,11},{10,... | collective-permute-start | bytes 12296 | tf_op jit(solution)/shard_map/ppermute | solution.py:308
  124.4 0.0 collective-permute-done.9.refs_2_
  124.4 1.8 %shard_map.51 = (f32[1,1024]{1,0:T(1,128)}, f32[1,1024]{1,0:T(1,128)}, f32[1,1024]{1,0:T(1,128)S(1)}, f32[1,1024]{1,0:T(1,128)}, f32[1,1024]{1,0:T(1,128)S(1)}) custom-call(s32[1]{0:T(128)} %bitcast.4.refs_0_, bf16[656,768]{1,0:T(8,128)(2,1)S(1)} %collective-permute-done.2.refs_1_.refs_5_, bf16[400,768]{1,0:T(8,128)(2,1)S(1)} %collective-permute-done.9.refs_2_, ...), custom_call_target="tpu_custom_call" | custom-call | flops 301989888 | bytes 1867776 | tf_op jit(solution)/shard_map/pallas_call | solution.py:287
  126.1 8.4 %collective-permute-start.10 = (f32[1,1024]{1,0:T(1,128)S(1)}, f32[1,1024]{1,0:T(1,128)S(1)}, u32[]{:S(2)}, u32[]{:S(2)}) collective-permute-start(f32[1,1024]{1,0:T(1,128)S(1)} %get-tuple-element.43), channel_id=1, source_target_pairs={{2,0},{3,1},{4,2},{5,3},{6,4},{7,5},{8,6},{9,7},{10,8},{11,9},{12,... | collective-permute-start | bytes 12296 | tf_op jit(solution)/shard_map/ppermute | solution.py:308
  134.6 1.3 collective-permute-start.11
  135.9 0.0 collective-permute-done.7.refs_1_
  135.9 0.0 collective-permute-done.8.refs_2_
  135.9 0.0 collective-permute-done.10.refs_3_
  135.9 8.1 %collective-permute-done.11.refs_4_ = f32[1,1024]{1,0:T(1,128)S(1)} collective-permute-done((f32[1,1024]{1,0:T(1,128)S(1)}, f32[1,1024]{1,0:T(1,128)S(1)}, u32[]{:S(2)}, u32[]{:S(2)}) %collective-permute-start.11) | collective-permute-done | bytes 4128 | tf_op jit(solution)/shard_map/ppermute | solution.py:308
  144.0 1.3 shard_map.52
  (2 shorter events, 0.0 us)
Async XLA Ops:
  0.0 1.4 copy-start.2
  1.4 0.7 copy-start.3
  6.2 1.3 copy-start
  7.4 10.3 %copy-start.4 = (s32[1,4]{1,0:T(1,128)S(1)}, s32[1,4]{1,0:T(1,128)}, u32[]{:S(2)}) copy-start(s32[1,4]{1,0:T(1,128)} %param.7) | copy-start | bytes 52
  7.4 36.9 %copy-start.1 = (s32[1024]{0:T(1024)S(1)}, s32[1024]{0:T(1024)}, u32[]{:S(2)}) copy-start(s32[1024]{0:T(1024)} %param.6) | copy-start | bytes 12292
  7.4 36.9 %all-to-all-start = ((bf16[64,16,896]{2,1,0:T(8,128)(2,1)}), bf16[64,16,896]{2,1,0:T(8,128)(2,1)S(1)}, u32[]{:S(2)}, u32[]{:S(2)}) async-start(bf16[64,16,896]{2,1,0:T(8,128)(2,1)} %bitcast.7), calls=%async_computation | async-start | bytes 3670016 | tf_op jit(solution)/shard_map/all_to_all | solution.py:324
  44.8 27.4 %collective-permute-start.1 = (bf16[656,768]{1,0:T(8,128)(2,1)S(1)}, bf16[656,768]{1,0:T(8,128)(2,1)}, u32[]{:S(2)}, u32[]{:S(2)}) collective-permute-start(bf16[656,768]{1,0:T(8,128)(2,1)S(1)} %get-tuple-element.27.refs_1_.refs_2_), channel_id=1, source_target_pairs={{2,0},{3,1},{4,2},{5,3},{6,4},{7,5},{8,6},{9,7},{10,8},{11,9},{12,... | collective-permute-start | bytes 3022856 | tf_op jit(solution)/shard_map/ppermute | solution.py:308
  49.5 38.4 %collective-permute-start.4 = (bf16[656,768]{1,0:T(8,128)(2,1)S(1)}, bf16[656,768]{1,0:T(8,128)(2,1)}, u32[]{:S(2)}, u32[]{:S(2)}) collective-permute-start(bf16[656,768]{1,0:T(8,128)(2,1)S(1)} %get-tuple-element.27.refs_1_.refs_2_), channel_id=1, source_target_pairs={{0,1},{1,0},{2,3},{3,2},{4,5},{5,4},{6,7},{7,6},{8,9},{9,8},{10,11... | collective-permute-start | bytes 3022856 | tf_op jit(solution)/shard_map/ppermute | solution.py:308
  49.6 42.1 %collective-permute-start.2 = (bf16[656,768]{1,0:T(8,128)(2,1)S(1)}, bf16[656,768]{1,0:T(8,128)(2,1)S(1)}, u32[]{:S(2)}, u32[]{:S(2)}) collective-permute-start(bf16[656,768]{1,0:T(8,128)(2,1)S(1)} %get-tuple-element.27.refs_1_.refs_2_), channel_id=1, source_target_pairs={{0,2},{1,3},{2,4},{3,5},{4,6},{5,7},{6,8},{7,9},{8,10},{9,11},{10,... | collective-permute-start | bytes 3022856 | tf_op jit(solution)/shard_map/ppermute | solution.py:308
  51.5 32.9 %collective-permute-start.3 = (bf16[400,768]{1,0:T(8,128)(2,1)S(1)}, bf16[400,768]{1,0:T(8,128)(2,1)}, u32[]{:S(2)}, u32[]{:S(2)}) collective-permute-start(bf16[400,768]{1,0:T(8,128)(2,1)S(1)} %get-tuple-element.26.refs_2_.refs_3_), channel_id=1, source_target_pairs={{2,0},{3,1},{4,2},{5,3},{6,4},{7,5},{8,6},{9,7},{10,8},{11,9},{12,... | collective-permute-start | bytes 1843208 | tf_op jit(solution)/shard_map/ppermute | solution.py:308
  60.0 26.4 %collective-permute-start.5 = (bf16[400,768]{1,0:T(8,128)(2,1)S(1)}, bf16[400,768]{1,0:T(8,128)(2,1)}, u32[]{:S(2)}, u32[]{:S(2)}) collective-permute-start(bf16[400,768]{1,0:T(8,128)(2,1)S(1)} %get-tuple-element.26.refs_2_.refs_3_), channel_id=1, source_target_pairs={{0,1},{1,0},{2,3},{3,2},{4,5},{5,4},{6,7},{7,6},{8,9},{9,8},{10,11... | collective-permute-start | bytes 1843208 | tf_op jit(solution)/shard_map/ppermute | solution.py:308
  72.2 36.2 %collective-permute-start.6 = (bf16[656,768]{1,0:T(8,128)(2,1)}, bf16[656,768]{1,0:T(8,128)(2,1)}, u32[]{:S(2)}, u32[]{:S(2)}) collective-permute-start(bf16[656,768]{1,0:T(8,128)(2,1)} %collective-permute-done.1.refs_4_), channel_id=1, source_target_pairs={{0,1},{2,3},{4,5},{6,7},{8,9},{10,11},{12,13},{14,15},{16,17},{18,... | collective-permute-start | bytes 3022856 | tf_op jit(solution)/shard_map/ppermute | solution.py:308
  84.5 23.9 %collective-permute-start = (bf16[400,768]{1,0:T(8,128)(2,1)S(1)}, bf16[400,768]{1,0:T(8,128)(2,1)S(1)}, u32[]{:S(2)}, u32[]{:S(2)}) collective-permute-start(bf16[400,768]{1,0:T(8,128)(2,1)S(1)} %get-tuple-element.26.refs_2_.refs_3_), channel_id=1, source_target_pairs={{0,2},{1,3},{2,4},{3,5},{4,6},{5,7},{6,8},{7,9},{8,10},{9,11},{10,... | collective-permute-start | bytes 1843208 | tf_op jit(solution)/shard_map/ppermute | solution.py:308
  86.4 38.0 %collective-permute-start.9 = (bf16[400,768]{1,0:T(8,128)(2,1)}, bf16[400,768]{1,0:T(8,128)(2,1)S(1)}, u32[]{:S(2)}, u32[]{:S(2)}) collective-permute-start(bf16[400,768]{1,0:T(8,128)(2,1)} %collective-permute-done.3.refs_6_), channel_id=1, source_target_pairs={{0,1},{2,3},{4,5},{6,7},{8,9},{10,11},{12,13},{14,15},{16,17},{18,... | collective-permute-start | bytes 1843208 | tf_op jit(solution)/shard_map/ppermute | solution.py:308
  122.3 13.5 %collective-permute-start.7 = (f32[1,1024]{1,0:T(1,128)S(1)}, f32[1,1024]{1,0:T(1,128)S(1)}, u32[]{:S(2)}, u32[]{:S(2)}) collective-permute-start(f32[1,1024]{1,0:T(1,128)S(1)} %get-tuple-element.39.refs_5_), channel_id=1, source_target_pairs={{0,1},{1,0},{2,3},{3,2},{4,5},{5,4},{6,7},{7,6},{8,9},{9,8},{10,11... | collective-permute-start | bytes 12296 | tf_op jit(solution)/shard_map/ppermute | solution.py:308
  122.4 13.5 %collective-permute-start.8 = (f32[1,1024]{1,0:T(1,128)S(1)}, f32[1,1024]{1,0:T(1,128)S(1)}, u32[]{:S(2)}, u32[]{:S(2)}) collective-permute-start(f32[1,1024]{1,0:T(1,128)S(1)} %get-tuple-element.40.refs_7_), channel_id=1, source_target_pairs={{0,2},{1,3},{2,4},{3,5},{4,6},{5,7},{6,8},{7,9},{8,10},{9,11},{10,... | collective-permute-start | bytes 12296 | tf_op jit(solution)/shard_map/ppermute | solution.py:308
  126.1 9.8 %collective-permute-start.10 = (f32[1,1024]{1,0:T(1,128)S(1)}, f32[1,1024]{1,0:T(1,128)S(1)}, u32[]{:S(2)}, u32[]{:S(2)}) collective-permute-start(f32[1,1024]{1,0:T(1,128)S(1)} %get-tuple-element.43), channel_id=1, source_target_pairs={{2,0},{3,1},{4,2},{5,3},{6,4},{7,5},{8,6},{9,7},{10,8},{11,9},{12,... | collective-permute-start | bytes 12296 | tf_op jit(solution)/shard_map/ppermute | solution.py:308
  134.6 9.4 %collective-permute-start.11 = (f32[1,1024]{1,0:T(1,128)S(1)}, f32[1,1024]{1,0:T(1,128)S(1)}, u32[]{:S(2)}, u32[]{:S(2)}) collective-permute-start(f32[1,1024]{1,0:T(1,128)S(1)} %get-tuple-element.44), channel_id=1, source_target_pairs={{1,2},{3,4},{5,6},{7,8},{9,10},{11,12},{13,14},{15,16},{17,18},{19... | collective-permute-start | bytes 12296 | tf_op jit(solution)/shard_map/ppermute | solution.py:308

commit v3 on v2

--- a/solution.py
+++ b/solution.py
@@ -12,7 +12,8 @@
 ROWS = 1024
 WIDTH = 768
 LANES = 128
-SIZES = (640, 384)
+HINT = 20
+SIZES = (768, 256)
 STARTS = tuple(sum(SIZES[:i]) for i in range(len(SIZES)))
 TAIL = 16
 DIGITS = 32
@@ -46,21 +47,23 @@
     return jnp.transpose(jnp.broadcast_to(row, (LANES, row.shape[1])))
 
 
-def front_kernel(devices, slot_ref, emb_ref, out_ref, raw_ref, unit_ref, sems):
+def front_kernel(devices, slot_hbm, emb_ref, out_hbm, slot_ref, raw_ref, unit_ref, out_ref, sems):
     per_pair = ROWS // devices
     size = 256
+    parts = [pl.ds(at, size) for at in range(0, ROWS, size)]
+    slots = pltpu.make_async_copy(slot_hbm, slot_ref, sems.at[len(parts)])
+    slots.start()
     copies = []
-    for step in range(ROWS // size):
-        part = pl.ds(step * size, size)
-        copy = pltpu.make_async_copy(emb_ref.at[part, :], raw_ref.at[part, :], sems.at[step])
-        copy.start()
-        copies.append(copy)
+    for n, part in enumerate(parts):
+        copies.append(pltpu.make_async_copy(emb_ref.at[part, :], raw_ref.at[part, :], sems.at[n]))
+        copies[n].start()
+    before = jnp.where(iota((ROWS, ROWS), 0) < iota((ROWS, ROWS), 1), 1.0, 0.0).astype(BF16)
+    slots.wait()
     slot = slot_ref[...]
     target = slot // ROWS
     low = slot - target * ROWS
     goes = iota((devices, ROWS), 0) == target
     goes_b = jnp.where(goes, 1.0, 0.0).astype(BF16)
-    before = jnp.where(iota((ROWS, ROWS), 0) < iota((ROWS, ROWS), 1), 1.0, 0.0).astype(BF16)
     count = jnp.dot(goes_b, before, preferred_element_type=F32)
     rank = jnp.sum(jnp.where(goes, count, 0.0), axis=0, keepdims=True)
     dest = target * per_pair + rank.astype(jnp.int32)
@@ -72,17 +75,20 @@
         jnp.where(lane == 1, as_column((low - high * DIGITS).astype(F32)), 0.0),
     )
     unit_ref[:, WIDTH:] = digits.astype(BF16)
-    for step in range(ROWS // size):
-        part = pl.ds(step * size, size)
-        copies[step].wait()
+    for n, part in enumerate(parts):
+        copies[n].wait()
         values = raw_ref[part, :].astype(F32)
         mean = jnp.sum(values * values, axis=1, keepdims=True) * (1.0 / WIDTH)
         inverse = lax.rsqrt(mean + 1e-06) * (1.0 / math.sqrt(WIDTH))
         unit_ref[part, 0:WIDTH] = (values * inverse).astype(BF16)
-    for step in range(ROWS // size):
-        part = pl.ds(step * size, size)
-        place = one_hot(size, step * size, dest)
+    back = []
+    for n, part in enumerate(parts):
+        place = one_hot(size, n * size, dest)
         out_ref[part, :] = jnp.dot(place, unit_ref[...], preferred_element_type=F32).astype(BF16)
+        back.append(pltpu.make_async_copy(out_ref.at[part, :], out_hbm.at[part, :], sems.at[n]))
+        back[n].start()
+    for copy in back:
+        copy.wait()
 
 
 def split_kernel(got_ref, ids_ref, list_ref, *outs):
@@ -97,16 +103,17 @@
     for step in range(4):
         place = one_hot(256, step * 256, land)
         arrived = arrived + jnp.dot(ids[:, step * 256:(step + 1) * 256], place, preferred_element_type=F32)
-    entries = jnp.broadcast_to(list_ref[...].astype(F32), (TAIL, LANES)).astype(BF16)
+    entries = list_ref[...].astype(F32)
     for size, start, out in zip(SIZES, STARTS, chunks):
-        own = jnp.broadcast_to(arrived[0:1, start:start + size], (TAIL, size)).astype(BF16)
-        out[size:size + TAIL, 0:WIDTH - LANES] = jnp.zeros((TAIL, WIDTH - LANES), BF16)
-        out[size:size + TAIL, 0:size] = own
-        out[size:size + TAIL, WIDTH - LANES:] = entries
+        first = iota((TAIL, LANES), 0) == 0
+        for at in range(0, WIDTH, LANES):
+            lanes = slice(at, at + LANES)
+            own = arrived[0:1, start + at:start + at + LANES] if at < size else jnp.zeros((1, LANES), F32)
+            out[size:size + TAIL, lanes] = jnp.where(first, own, entries).astype(BF16)
 
 
 def weight_of(ref, size, shift):
-    entries = ref[size:size + TAIL, WIDTH - LANES:].astype(F32)[0:1, :]
+    entries = ref[size:size + TAIL, 0:LANES].astype(F32)[1:2, :]
     return jnp.sum(jnp.where(iota((1, LANES), 1) == shift - 1, entries, 0.0), axis=1, keepdims=True)
 
 
@@ -135,22 +142,16 @@
 
 def pair(a_ref, a_size, a_col, b_ref, b_size, weight, row_acc, col_acc):
     b_row = ids_row(b_ref, b_size)
-    height = 128
-
-    def step(i, carry):
-        at = pl.ds(pl.multiple_of(i * height, height), height)
-        a = a_ref[at, :]
-        col = a_col[at, :]
-        total = None
-        for start, width in cuts(b_size, 512):
-            part = slice(start, start + width)
-            by_row, by_col = tile_terms(nt(a, b_ref[part, :]), col, b_row[:, part], False)
-            total = by_row if total is None else total + by_row
-            col_acc[:, part] = col_acc[:, part] + weight * by_col
-        row_acc[at, :] = row_acc[at, :] + weight * total
-        return carry
-
-    lax.fori_loop(0, a_size // height, step, 0)
+    for j, width in cuts(b_size, 256):
+        part = slice(j, j + width)
+        b = b_ref[part, :]
+        down = None
+        for i, height in cuts(a_size, 256):
+            at = slice(i, i + height)
+            by_row, by_col = tile_terms(nt(a_ref[at, :], b), a_col[at, :], b_row[:, part], False)
+            row_acc[at, :] = row_acc[at, :] + weight * by_row
+            down = by_col if down is None else down + by_col
+        col_acc[:, part] = col_acc[:, part] + weight * down
 
 
 def own_pair(ref, size, col_ref, row_acc, col_acc):
@@ -282,19 +283,19 @@
     return jax.ShapeDtypeStruct((1, n), F32)
 
 
-def call(kernel, out_shape, in_specs, scratch, tasks, args, mib=40):
+def call(kernel, out_shape, in_specs, scratch, tasks, args, mib=40, out_spec=VMEM):
     single = not isinstance(out_shape, (list, tuple))
     return pl.pallas_call(
         kernel,
         out_shape=out_shape,
         in_specs=in_specs,
-        out_specs=VMEM if single else [VMEM] * len(out_shape),
+        out_specs=out_spec if single else [out_spec] * len(out_shape),
         scratch_shapes=scratch,
         compiler_params=pltpu.CompilerParams(vmem_limit_bytes=mib << 20),
         cost_estimate=pl.CostEstimate(
-            flops=int(tasks * 2 * ROWS * ROWS * WIDTH),
-            transcendentals=int(tasks * ROWS * ROWS),
-            bytes_accessed=int((1 + tasks) * 2 * ROWS * WIDTH),
+            flops=int(HINT * tasks * 2 * ROWS * ROWS * WIDTH),
+            transcendentals=int(HINT * tasks * ROWS * ROWS),
+            bytes_accessed=int(HINT * (1 + tasks) * 2 * ROWS * WIDTH),
         ),
     )(*args)
 
@@ -317,9 +318,10 @@
 
     outgoing = call(
         functools.partial(front_kernel, devices),
-        jax.ShapeDtypeStruct((ROWS, WIDTH + LANES), BF16), [VMEM, HBM],
-        [pltpu.VMEM((ROWS, WIDTH), BF16), pltpu.VMEM((ROWS, WIDTH + LANES), BF16), pltpu.SemaphoreType.DMA((4,))],
-        1, (sorted_slot.reshape(1, ROWS), embeddings),
+        jax.ShapeDtypeStruct((ROWS, WIDTH + LANES), BF16), [ANY] * 2,
+        [pltpu.VMEM((1, ROWS), jnp.int32), pltpu.VMEM((ROWS, WIDTH), BF16)]
+        + [pltpu.VMEM((ROWS, WIDTH + LANES), BF16)] * 2 + [pltpu.SemaphoreType.DMA((5,))],
+        1, (sorted_slot.reshape(1, ROWS), embeddings), 62, ANY,
     )
     arrived = lax.all_to_all(outgoing, AXES, split_axis=0, concat_axis=0, tiled=True)
     reach = position + 1 + jnp.arange(SHIFTS, dtype=jnp.int32)
@@ -333,19 +335,23 @@
     up, down = (lambda p: p + 2), (lambda p: p - 2)
     arrays = {("own", c): own[c] for c in chunks}
     for c in chunks:
-        arrays["m", c] = move_d(own[c], change=up)
-        arrays["p", c] = move_d(own[c], change=down)
-    for c in chunks:
         arrays["sw", c] = move_d(own[c], change=swap)
     for c in chunks:
-        arrays["x", c] = move_d(arrays["p", c], change=swap, only=0)
+        sent = own[c]
+        if c > 0:
+            sent = lax.optimization_barrier((sent, *(arrays["sw", d] for d in chunks)))[0]
+        arrays["m", c] = move_d(sent, change=up)
+        arrays["p", c] = move_d(sent, change=down)
 
     whole = lambda role: [(role, c) for c in chunks]
     tasks = [(None, ("own", a), ("own", b), None, 0) for a in chunks for b in chunks if a <= b]
-    tasks += [(1, a, b, ("sw", 0), 1) for a in whole("own") for b in whole("sw")]
     sums = run_stage(core, arrays, tasks, None)
+    tasks = [(1, a, b, ("sw", 0), 1) for a in whole("own") for b in whole("sw")]
+    sums = run_stage(core, arrays, tasks, sums)
     for c in chunks:
         m, p = ("m", c), ("p", c)
+        relayed = lax.optimization_barrier((arrays[p], *sums))[0]
+        arrays["x", c] = move_d(relayed, change=swap, only=0)
         tasks = [(None, m, b, m, 2) for b in whole("own")]
         tasks += [(None, m, ("p", d), m, 4) for d in range(c)]
         tasks += [(None, ("m", d), p, m, 4) for d in range(c + 1)]

time: 147 us -> 124 us (0.84)
  Pallas kernels: 41.9 us -> 27.8 us
  waiting for transfers between devices: 56.8 us -> 52.5 us
  local copies, waits for them, and re-layouts: 3.37 us -> 0.02 us
    pallas_call x7 -> x8, Pallas kernels: 41.9 us -> 27.8 us  [call(): pl.pallas_call(kernel, out_shape=out_shape, in_specs=in_specs, out_specs=...]
    ppermute x12, waiting for transfers between devices: 30.3 us -> 26 us  [move(): return lax.ppermute(value, AXES, pairs)]
    unnamed x10 -> x4, local copies, waits for them, and re-layouts: 3.36 us -> 0.01 us
  transfers between devices with their start and end apart: 13 -> 13, of which waited for: 4 -> 4; matrix products, arithmetic and copies ran while one was open for 0% -> 0% of each run, Pallas kernels for 25% -> 17%
where the time goes in v3:
time: 124 us; the launch traced here: 123 us
  waiting for transfers between devices  52.5 us (42%)
  starting transfers between devices  42.1 us (34%)
  Pallas kernels  27.8 us (22%)
    ppermute x12, starting transfers between devices, move(): return lax.ppermute(value, AXES, pairs)  31.9 us
    pallas_call x8, Pallas kernels, call(): pl.pallas_call(kernel, out_shape=out_shape, in_specs=in_specs, out_specs=...  27.8 us
    all_to_all x1, waiting for transfers between devices, local(): lax.all_to_all(outgoing, AXES, split_axis=0, concat_axis=0, tiled=True)  26.5 us
    ppermute x12, waiting for transfers between devices, move(): return lax.ppermute(value, AXES, pairs)  26 us
    all_to_all x1, starting transfers between devices, local(): lax.all_to_all(outgoing, AXES, split_axis=0, concat_axis=0, tiled=True)  10.2 us
  transfers between devices with their start and end apart: 13, of which 4 were waited for; matrix products, arithmetic and copies ran while one was open for 0% of the time, Pallas kernels for 17%

profile of v3, /device:TPU:34, one launch (start us, length us, event | category | flops | bytes accessed | tf_op | source)
XLA Modules:
  0.0 122.7 jit_solution(13758194448361114408)
XLA Ops:
  0.0 4.7 %shard_map.46 = bf16[1024,896]{1,0:T(8,128)(2,1)} custom-call(s32[1,1024]{1,0:T(1,128)} %bitcast.9, bf16[1024,768]{1,0:T(8,128)(2,1)} %emb_ref.1), custom_call_target="tpu_custom_call" | custom-call | flops 32212254720 | bytes 62914560 | tf_op jit(solution)/shard_map/pallas_call | solution.py:288
  4.8 0.0 copy-start.1
  4.8 0.0 copy-start
  4.8 10.2 %all-to-all-start = ((bf16[64,16,896]{2,1,0:T(8,128)(2,1)}), bf16[64,16,896]{2,1,0:T(8,128)(2,1)S(1)}, u32[]{:S(2)}, u32[]{:S(2)}) async-start(bf16[64,16,896]{2,1,0:T(8,128)(2,1)} %bitcast.8), calls=%async_computation | async-start | bytes 3670016 | tf_op jit(solution)/shard_map/all_to_all | solution.py:326
  15.0 0.0 copy-done.1
  15.0 26.5 %all-to-all-done = bf16[64,16,896]{2,1,0:T(8,128)(2,1)S(1)} async-done(((bf16[64,16,896]{2,1,0:T(8,128)(2,1)}), bf16[64,16,896]{2,1,0:T(8,128)(2,1)S(1)}, u32[]{:S(2)}, u32[]{:S(2)}) %all-to-all-start) | async-done | bytes 1835040 | tf_op jit(solution)/shard_map/all_to_all | solution.py:326
  41.5 0.0 copy-done
  41.5 0.5 shard_map.47
  42.0 0.4 collective-permute-start
  42.4 4.4 %collective-permute-start.3 = (bf16[784,768]{1,0:T(8,128)(2,1)S(1)}, bf16[784,768]{1,0:T(8,128)(2,1)S(1)}, u32[]{:S(2)}, u32[]{:S(2)}) collective-permute-start(bf16[784,768]{1,0:T(8,128)(2,1)S(1)} %get-tuple-element.35.refs_1_.refs_2_), channel_id=1, source_target_pairs={{2,0},{3,1},{4,2},{5,3},{6,4},{7,5},{8,6},{9,7},{10,8},{11,9},{12,... | collective-permute-start | bytes 3612680 | tf_op jit(solution)/shard_map/ppermute | solution.py:309
  46.8 1.9 %collective-permute-start.4 = (bf16[784,768]{1,0:T(8,128)(2,1)S(1)}, bf16[784,768]{1,0:T(8,128)(2,1)S(1)}, u32[]{:S(2)}, u32[]{:S(2)}) collective-permute-start(bf16[784,768]{1,0:T(8,128)(2,1)S(1)} %get-tuple-element.35.refs_1_.refs_2_), channel_id=1, source_target_pairs={{0,2},{1,3},{2,4},{3,5},{4,6},{5,7},{6,8},{7,9},{8,10},{9,11},{10,... | collective-permute-start | bytes 3612680 | tf_op jit(solution)/shard_map/ppermute | solution.py:309
  48.7 0.3 collective-permute-start.1
  49.0 2.2 %shard_map.48 = (f32[1,1024]{1,0:T(1,128)S(1)}, f32[1,1024]{1,0:T(1,128)S(1)}, f32[1,1024]{1,0:T(1,128)S(1)}, f32[1,1024]{1,0:T(1,128)S(1)}, f32[1,1024]{1,0:T(1,128)S(1)}) custom-call(s32[1]{0:T(128)} %bitcast.4.refs_0_, bf16[784,768]{1,0:T(8,128)(2,1)S(1)} %get-tuple-element.35.refs_1_.refs_2_, bf16[272,768]{1,0:T(8,128)(2,1)S(1)} %get-tuple-element.36.refs_2_.refs_4_.refs_3_), custom_call_target="tpu_custom_call" | custom-call | flops 26172456960 | bytes 57016320 | tf_op jit(solution)/shard_map/pallas_call | solution.py:288
  51.2 0.0 collective-permute-done.1.refs_3_.refs_6_.refs_8_
  51.2 0.0 collective-permute-done.refs_2_.refs_5_.refs_7_
  51.2 2.1 %collective-permute-start.2 = (bf16[272,768]{1,0:T(8,128)(2,1)S(1)}, bf16[272,768]{1,0:T(8,128)(2,1)S(1)}, u32[]{:S(2)}, u32[]{:S(2)}) collective-permute-start(bf16[272,768]{1,0:T(8,128)(2,1)S(1)} %get-tuple-element.36.refs_2_.refs_4_.refs_3_), channel_id=1, source_target_pairs={{0,2},{1,3},{2,4},{3,5},{4,6},{5,7},{6,8},{7,9},{8,10},{9,11},{10,... | collective-permute-start | bytes 1253384 | tf_op jit(solution)/shard_map/ppermute | solution.py:309
  53.4 8.2 %collective-permute-start.5 = (bf16[272,768]{1,0:T(8,128)(2,1)S(1)}, bf16[272,768]{1,0:T(8,128)(2,1)S(1)}, u32[]{:S(2)}, u32[]{:S(2)}) collective-permute-start(bf16[272,768]{1,0:T(8,128)(2,1)S(1)} %get-tuple-element.36.refs_2_.refs_4_.refs_3_), channel_id=1, source_target_pairs={{2,0},{3,1},{4,2},{5,3},{6,4},{7,5},{8,6},{9,7},{10,8},{11,9},{12,... | collective-permute-start | bytes 1253384 | tf_op jit(solution)/shard_map/ppermute | solution.py:309
  61.6 1.5 %shard_map.49 = (f32[1,1024]{1,0:T(1,128)S(1)}, f32[1,1024]{1,0:T(1,128)S(1)}, f32[1,1024]{1,0:T(1,128)S(1)}, f32[1,1024]{1,0:T(1,128)S(1)}, f32[1,1024]{1,0:T(1,128)S(1)}) custom-call(s32[1]{0:T(128)} %bitcast.4.refs_0_, bf16[784,768]{1,0:T(8,128)(2,1)S(1)} %get-tuple-element.35.refs_1_.refs_2_, ...), custom_call_target="tpu_custom_call" | custom-call | flops 16106127360 | bytes 47185920 | tf_op jit(solution)/shard_map/pallas_call | solution.py:288
  63.2 10.5 %collective-permute-done.3.refs_4_ = bf16[784,768]{1,0:T(8,128)(2,1)S(1)} collective-permute-done((bf16[784,768]{1,0:T(8,128)(2,1)S(1)}, bf16[784,768]{1,0:T(8,128)(2,1)S(1)}, u32[]{:S(2)}, u32[]{:S(2)}) %collective-permute-start.3) | collective-permute-done | bytes 1204256 | tf_op jit(solution)/shard_map/ppermute | solution.py:309
  73.6 1.5 %collective-permute-start.6 = (bf16[784,768]{1,0:T(8,128)(2,1)S(1)}, bf16[784,768]{1,0:T(8,128)(2,1)S(1)}, u32[]{:S(2)}, u32[]{:S(2)}) collective-permute-start(bf16[784,768]{1,0:T(8,128)(2,1)S(1)} %collective-permute-done.3.refs_4_), channel_id=1, source_target_pairs={{0,1},{2,3},{4,5},{6,7},{8,9},{10,11},{12,13},{14,15},{16,17},{18,... | collective-permute-start | bytes 3612680 | tf_op jit(solution)/shard_map/ppermute | solution.py:309
  75.2 7.4 %collective-permute-done.4.refs_1_.refs_5_ = bf16[784,768]{1,0:T(8,128)(2,1)S(1)} collective-permute-done((bf16[784,768]{1,0:T(8,128)(2,1)S(1)}, bf16[784,768]{1,0:T(8,128)(2,1)S(1)}, u32[]{:S(2)}, u32[]{:S(2)}) %collective-permute-start.4) | collective-permute-done | bytes 1204256 | tf_op jit(solution)/shard_map/ppermute | solution.py:309
  82.5 8.8 %shard_map.50 = (f32[1,1024]{1,0:T(1,128)S(1)}, f32[1,1024]{1,0:T(1,128)S(1)}, f32[1,1024]{1,0:T(1,128)S(1)}, f32[1,1024]{1,0:T(1,128)S(1)}, f32[1,1024]{1,0:T(1,128)S(1)}) custom-call(s32[1]{0:T(128)} %bitcast.4.refs_0_, bf16[784,768]{1,0:T(8,128)(2,1)S(1)} %collective-permute-done.4.refs_1_.refs_5_, ...), custom_call_target="tpu_custom_call" | custom-call | flops 66437775360 | bytes 96337920 | tf_op jit(solution)/shard_map/pallas_call | solution.py:288
  91.3 0.0 collective-permute-done.5.refs_6_
  91.3 1.3 %collective-permute-start.9 = (bf16[272,768]{1,0:T(8,128)(2,1)S(1)}, bf16[272,768]{1,0:T(8,128)(2,1)S(1)}, u32[]{:S(2)}, u32[]{:S(2)}) collective-permute-start(bf16[272,768]{1,0:T(8,128)(2,1)S(1)} %collective-permute-done.5.refs_6_), channel_id=1, source_target_pairs={{0,1},{2,3},{4,5},{6,7},{8,9},{10,11},{12,13},{14,15},{16,17},{18,... | collective-permute-start | bytes 1253384 | tf_op jit(solution)/shard_map/ppermute | solution.py:309
  92.6 0.0 collective-permute-done.2.refs_1_.refs_3_
  92.6 0.0 collective-permute-done.6.refs_9_
  92.7 7.0 %shard_map.51 = (f32[1,1024]{1,0:T(1,128)S(1)}, f32[1,1024]{1,0:T(1,128)S(1)}, f32[1,1024]{1,0:T(1,128)S(1)}, f32[1,1024]{1,0:T(1,128)S(1)}, f32[1,1024]{1,0:T(1,128)S(1)}) custom-call(s32[1]{0:T(128)} %bitcast.4.refs_0_, bf16[272,768]{1,0:T(8,128)(2,1)S(1)} %collective-permute-done.2.refs_1_.refs_3_, ...), custom_call_target="tpu_custom_call" | custom-call | flops 42278584320 | bytes 72744960 | tf_op jit(solution)/shard_map/pallas_call | solution.py:288
  99.7 0.1 collective-permute-start.7
  99.8 1.9 %collective-permute-start.8 = (f32[1,1024]{1,0:T(1,128)S(1)}, f32[1,1024]{1,0:T(1,128)S(1)}, u32[]{:S(2)}, u32[]{:S(2)}) collective-permute-start(f32[1,1024]{1,0:T(1,128)S(1)} %get-tuple-element.55.refs_7_), channel_id=1, source_target_pairs={{0,2},{1,3},{2,4},{3,5},{4,6},{5,7},{6,8},{7,9},{8,10},{9,11},{10,... | collective-permute-start | bytes 12296 | tf_op jit(solution)/shard_map/ppermute | solution.py:309
  101.7 0.0 collective-permute-done.9.refs_2_
  101.7 1.8 %shard_map.52 = (f32[1,1024]{1,0:T(1,128)}, f32[1,1024]{1,0:T(1,128)}, f32[1,1024]{1,0:T(1,128)S(1)}, f32[1,1024]{1,0:T(1,128)}, f32[1,1024]{1,0:T(1,128)S(1)}) custom-call(s32[1]{0:T(128)} %bitcast.4.refs_0_, bf16[784,768]{1,0:T(8,128)(2,1)S(1)} %collective-permute-done.4.refs_1_.refs_5_, bf16[272,768]{1,0:T(8,128)(2,1)S(1)} %collective-permute-done.9.refs_2_, ...), custom_call_target="tpu_custom_call" | custom-call | flops 4026531840 | bytes 35389440 | tf_op jit(solution)/shard_map/pallas_call | solution.py:288
  103.5 8.4 %collective-permute-start.10 = (f32[1,1024]{1,0:T(1,128)S(1)}, f32[1,1024]{1,0:T(1,128)S(1)}, u32[]{:S(2)}, u32[]{:S(2)}) collective-permute-start(f32[1,1024]{1,0:T(1,128)S(1)} %get-tuple-element.59), channel_id=1, source_target_pairs={{2,0},{3,1},{4,2},{5,3},{6,4},{7,5},{8,6},{9,7},{10,8},{11,9},{12,... | collective-permute-start | bytes 12296 | tf_op jit(solution)/shard_map/ppermute | solution.py:309
  112.0 1.3 %collective-permute-start.11 = (f32[1,1024]{1,0:T(1,128)S(1)}, f32[1,1024]{1,0:T(1,128)S(1)}, u32[]{:S(2)}, u32[]{:S(2)}) collective-permute-start(f32[1,1024]{1,0:T(1,128)S(1)} %get-tuple-element.60), channel_id=1, source_target_pairs={{1,2},{3,4},{5,6},{7,8},{9,10},{11,12},{13,14},{15,16},{17,18},{19... | collective-permute-start | bytes 12296 | tf_op jit(solution)/shard_map/ppermute | solution.py:309
  113.3 0.0 collective-permute-done.7.refs_1_
  113.3 0.0 collective-permute-done.8.refs_2_
  113.3 0.0 collective-permute-done.10.refs_3_
  113.3 8.1 %collective-permute-done.11.refs_4_ = f32[1,1024]{1,0:T(1,128)S(1)} collective-permute-done((f32[1,1024]{1,0:T(1,128)S(1)}, f32[1,1024]{1,0:T(1,128)S(1)}, u32[]{:S(2)}, u32[]{:S(2)}) %collective-permute-start.11) | collective-permute-done | bytes 4128 | tf_op jit(solution)/shard_map/ppermute | solution.py:309
  121.4 1.3 %shard_map.53 = f32[1,1024]{1,0:T(1,128)} custom-call(s32[1,1024]{1,0:T(1,128)S(1)} %get-tuple-element.33.land_ref, f32[1,1024]{1,0:T(1,128)S(1)} %get-tuple-element.53.refs_4_.refs_0_, f32[1,1024]{1,0:T(1,128)S(1)} %collective-permute-done.7.refs_1_, f32[1,1024]{1,0:T(1,128)S(1)} %collective-permute-done.8.refs_2_, ...), custom_call_target="tpu_custom_call" | custom-call | flops 6442450944 | bytes 37748736 | tf_op jit(solution)/shard_map/pallas_call | solution.py:288
  (2 shorter events, 0.0 us)
Async XLA Ops:
  4.8 10.2 %copy-start.1 = (s32[1,4]{1,0:T(1,128)S(1)}, s32[1,4]{1,0:T(1,128)}, u32[]{:S(2)}) copy-start(s32[1,4]{1,0:T(1,128)} %param.7) | copy-start | bytes 52
  4.8 36.8 %copy-start = (s32[1024]{0:T(1024)S(1)}, s32[1024]{0:T(1024)}, u32[]{:S(2)}) copy-start(s32[1024]{0:T(1024)} %param.6) | copy-start | bytes 12292
  4.8 36.8 %all-to-all-start = ((bf16[64,16,896]{2,1,0:T(8,128)(2,1)}), bf16[64,16,896]{2,1,0:T(8,128)(2,1)S(1)}, u32[]{:S(2)}, u32[]{:S(2)}) async-start(bf16[64,16,896]{2,1,0:T(8,128)(2,1)} %bitcast.8), calls=%async_computation | async-start | bytes 3670016 | tf_op jit(solution)/shard_map/all_to_all | solution.py:326
  42.0 9.2 %collective-permute-start = (bf16[784,768]{1,0:T(8,128)(2,1)S(1)}, bf16[784,768]{1,0:T(8,128)(2,1)S(1)}, u32[]{:S(2)}, u32[]{:S(2)}) collective-permute-start(bf16[784,768]{1,0:T(8,128)(2,1)S(1)} %get-tuple-element.35.refs_1_.refs_2_), channel_id=1, source_target_pairs={{0,1},{1,0},{2,3},{3,2},{4,5},{5,4},{6,7},{7,6},{8,9},{9,8},{10,11... | collective-permute-start | bytes 3612680 | tf_op jit(solution)/shard_map/ppermute | solution.py:309
  42.4 31.2 %collective-permute-start.3 = (bf16[784,768]{1,0:T(8,128)(2,1)S(1)}, bf16[784,768]{1,0:T(8,128)(2,1)S(1)}, u32[]{:S(2)}, u32[]{:S(2)}) collective-permute-start(bf16[784,768]{1,0:T(8,128)(2,1)S(1)} %get-tuple-element.35.refs_1_.refs_2_), channel_id=1, source_target_pairs={{2,0},{3,1},{4,2},{5,3},{6,4},{7,5},{8,6},{9,7},{10,8},{11,9},{12,... | collective-permute-start | bytes 3612680 | tf_op jit(solution)/shard_map/ppermute | solution.py:309
  46.8 35.7 %collective-permute-start.4 = (bf16[784,768]{1,0:T(8,128)(2,1)S(1)}, bf16[784,768]{1,0:T(8,128)(2,1)S(1)}, u32[]{:S(2)}, u32[]{:S(2)}) collective-permute-start(bf16[784,768]{1,0:T(8,128)(2,1)S(1)} %get-tuple-element.35.refs_1_.refs_2_), channel_id=1, source_target_pairs={{0,2},{1,3},{2,4},{3,5},{4,6},{5,7},{6,8},{7,9},{8,10},{9,11},{10,... | collective-permute-start | bytes 3612680 | tf_op jit(solution)/shard_map/ppermute | solution.py:309
  48.7 2.5 %collective-permute-start.1 = (bf16[272,768]{1,0:T(8,128)(2,1)S(1)}, bf16[272,768]{1,0:T(8,128)(2,1)S(1)}, u32[]{:S(2)}, u32[]{:S(2)}) collective-permute-start(bf16[272,768]{1,0:T(8,128)(2,1)S(1)} %get-tuple-element.36.refs_2_.refs_4_.refs_3_), channel_id=1, source_target_pairs={{0,1},{1,0},{2,3},{3,2},{4,5},{5,4},{6,7},{7,6},{8,9},{9,8},{10,11... | collective-permute-start | bytes 1253384 | tf_op jit(solution)/shard_map/ppermute | solution.py:309
  51.2 41.4 %collective-permute-start.2 = (bf16[272,768]{1,0:T(8,128)(2,1)S(1)}, bf16[272,768]{1,0:T(8,128)(2,1)S(1)}, u32[]{:S(2)}, u32[]{:S(2)}) collective-permute-start(bf16[272,768]{1,0:T(8,128)(2,1)S(1)} %get-tuple-element.36.refs_2_.refs_4_.refs_3_), channel_id=1, source_target_pairs={{0,2},{1,3},{2,4},{3,5},{4,6},{5,7},{6,8},{7,9},{8,10},{9,11},{10,... | collective-permute-start | bytes 1253384 | tf_op jit(solution)/shard_map/ppermute | solution.py:309
  53.4 37.9 %collective-permute-start.5 = (bf16[272,768]{1,0:T(8,128)(2,1)S(1)}, bf16[272,768]{1,0:T(8,128)(2,1)S(1)}, u32[]{:S(2)}, u32[]{:S(2)}) collective-permute-start(bf16[272,768]{1,0:T(8,128)(2,1)S(1)} %get-tuple-element.36.refs_2_.refs_4_.refs_3_), channel_id=1, source_target_pairs={{2,0},{3,1},{4,2},{5,3},{6,4},{7,5},{8,6},{9,7},{10,8},{11,9},{12,... | collective-permute-start | bytes 1253384 | tf_op jit(solution)/shard_map/ppermute | solution.py:309
  73.6 19.0 %collective-permute-start.6 = (bf16[784,768]{1,0:T(8,128)(2,1)S(1)}, bf16[784,768]{1,0:T(8,128)(2,1)S(1)}, u32[]{:S(2)}, u32[]{:S(2)}) collective-permute-start(bf16[784,768]{1,0:T(8,128)(2,1)S(1)} %collective-permute-done.3.refs_4_), channel_id=1, source_target_pairs={{0,1},{2,3},{4,5},{6,7},{8,9},{10,11},{12,13},{14,15},{16,17},{18,... | collective-permute-start | bytes 3612680 | tf_op jit(solution)/shard_map/ppermute | solution.py:309
  91.3 10.4 %collective-permute-start.9 = (bf16[272,768]{1,0:T(8,128)(2,1)S(1)}, bf16[272,768]{1,0:T(8,128)(2,1)S(1)}, u32[]{:S(2)}, u32[]{:S(2)}) collective-permute-start(bf16[272,768]{1,0:T(8,128)(2,1)S(1)} %collective-permute-done.5.refs_6_), channel_id=1, source_target_pairs={{0,1},{2,3},{4,5},{6,7},{8,9},{10,11},{12,13},{14,15},{16,17},{18,... | collective-permute-start | bytes 1253384 | tf_op jit(solution)/shard_map/ppermute | solution.py:309
  99.7 13.6 %collective-permute-start.7 = (f32[1,1024]{1,0:T(1,128)S(1)}, f32[1,1024]{1,0:T(1,128)S(1)}, u32[]{:S(2)}, u32[]{:S(2)}) collective-permute-start(f32[1,1024]{1,0:T(1,128)S(1)} %get-tuple-element.54.refs_5_), channel_id=1, source_target_pairs={{0,1},{1,0},{2,3},{3,2},{4,5},{5,4},{6,7},{7,6},{8,9},{9,8},{10,11... | collective-permute-start | bytes 12296 | tf_op jit(solution)/shard_map/ppermute | solution.py:309
  99.8 13.5 %collective-permute-start.8 = (f32[1,1024]{1,0:T(1,128)S(1)}, f32[1,1024]{1,0:T(1,128)S(1)}, u32[]{:S(2)}, u32[]{:S(2)}) collective-permute-start(f32[1,1024]{1,0:T(1,128)S(1)} %get-tuple-element.55.refs_7_), channel_id=1, source_target_pairs={{0,2},{1,3},{2,4},{3,5},{4,6},{5,7},{6,8},{7,9},{8,10},{9,11},{10,... | collective-permute-start | bytes 12296 | tf_op jit(solution)/shard_map/ppermute | solution.py:309
  103.5 9.8 %collective-permute-start.10 = (f32[1,1024]{1,0:T(1,128)S(1)}, f32[1,1024]{1,0:T(1,128)S(1)}, u32[]{:S(2)}, u32[]{:S(2)}) collective-permute-start(f32[1,1024]{1,0:T(1,128)S(1)} %get-tuple-element.59), channel_id=1, source_target_pairs={{2,0},{3,1},{4,2},{5,3},{6,4},{7,5},{8,6},{9,7},{10,8},{11,9},{12,... | collective-permute-start | bytes 12296 | tf_op jit(solution)/shard_map/ppermute | solution.py:309
  112.0 9.4 %collective-permute-start.11 = (f32[1,1024]{1,0:T(1,128)S(1)}, f32[1,1024]{1,0:T(1,128)S(1)}, u32[]{:S(2)}, u32[]{:S(2)}) collective-permute-start(f32[1,1024]{1,0:T(1,128)S(1)} %get-tuple-element.60), channel_id=1, source_target_pairs={{1,2},{3,4},{5,6},{7,8},{9,10},{11,12},{13,14},{15,16},{17,18},{19... | collective-permute-start | bytes 12296 | tf_op jit(solution)/shard_map/ppermute | solution.py:309

commit v4 on v3

v4 whole, which is shorter than its diff:
```python
import functools
import math

import jax
import jax.numpy as jnp
from jax import lax
from jax.experimental import pallas as pl
from jax.experimental.pallas import tpu as pltpu
from jax.sharding import PartitionSpec as P

SHIFTS = 4
ROWS = 1024
WIDTH = 768
LANES = 128
HINT = 20
COPIES = 3
APART = 2
PER_PAIR = 16
PIECES = WIDTH // LANES
MESSAGE = (COPIES * PIECES + 1) * PER_PAIR
TAIL = 16
DIGITS = 32
AXES = ("gr", "gc")

sharpness = 20.0
threshold = 0.8

F32 = jnp.float32
BF16 = jnp.bfloat16
VMEM = pl.BlockSpec(memory_space=pltpu.VMEM)
ANY = pl.BlockSpec(memory_space=pl.ANY)
SMEM = pl.BlockSpec(memory_space=pltpu.SMEM)


def iota(shape, axis):
    return lax.broadcasted_iota(jnp.int32, shape, axis)


def one_hot(rows, first, wanted):
    hit = iota((rows, wanted.shape[1]), 0) + first == wanted
    return jnp.where(hit, 1.0, 0.0).astype(BF16)


def nt(a, b):
    return lax.dot_general(a, b, (((1,), (1,)), ((), ())), preferred_element_type=F32)


def as_column(row):
    return jnp.transpose(jnp.broadcast_to(row, (LANES, row.shape[1])))


def front_kernel(devices, slot_hbm, emb_ref, out_hbm, slot_ref, raw_ref, unit_ref, digit_ref, out_ref, sems):
    size = 256
    parts = [pl.ds(at, size) for at in range(0, ROWS, size)]
    slots = pltpu.make_async_copy(slot_hbm, slot_ref, sems.at[len(parts)])
    slots.start()
    copies = []
    for n, part in enumerate(parts):
        copies.append(pltpu.make_async_copy(emb_ref.at[part, :], raw_ref.at[part, :], sems.at[n]))
        copies[n].start()
    before = jnp.where(iota((ROWS, ROWS), 0) < iota((ROWS, ROWS), 1), 1.0, 0.0).astype(BF16)
    slots.wait()
    slot = slot_ref[...]
    target = slot // ROWS
    low = slot - target * ROWS
    goes = iota((devices, ROWS), 0) == target
    goes_b = jnp.where(goes, 1.0, 0.0).astype(BF16)
    count = jnp.dot(goes_b, before, preferred_element_type=F32)
    rank = jnp.sum(jnp.where(goes, count, 0.0), axis=0, keepdims=True)
    dest = target * PER_PAIR + rank.astype(jnp.int32)
    high = low // DIGITS
    even = iota((ROWS, LANES), 1) % 2 == 0
    digits = jnp.where(even, as_column(high.astype(F32)), as_column((low - high * DIGITS).astype(F32)))
    unit_ref[:, WIDTH:] = digits.astype(BF16)
    for n, part in enumerate(parts):
        copies[n].wait()
        values = raw_ref[part, :].astype(F32)
        mean = jnp.sum(values * values, axis=1, keepdims=True) * (1.0 / WIDTH)
        inverse = lax.rsqrt(mean + 1e-06) * (1.0 / math.sqrt(WIDTH))
        unit_ref[part, 0:WIDTH] = (values * inverse).astype(BF16)
    for n, part in enumerate(parts):
        place = one_hot(size, n * size, dest)
        placed = jnp.dot(place, unit_ref[...], preferred_element_type=F32).astype(BF16)
        digit_ref[part, :] = placed[:, WIDTH:]
        for i in range(size // PER_PAIR):
            block = n * (size // PER_PAIR) + i
            rows = placed[i * PER_PAIR:(i + 1) * PER_PAIR, :]
            for copy in range(COPIES):
                at = (block - APART * copy) % devices * MESSAGE + copy * PIECES * PER_PAIR
                for piece in range(PIECES):
                    out_ref[at + piece * PER_PAIR:at + (piece + 1) * PER_PAIR, :] = rows[:, piece * LANES:(piece + 1) * LANES]
    lane = iota((PER_PAIR, LANES), 1) // 2
    for device in range(devices):
        tile = digit_ref[device * PER_PAIR:(device + 1) * PER_PAIR, :]
        for copy in range(1, COPIES):
            at = (device + APART * copy) % devices * PER_PAIR
            tile = jnp.where(lane == copy, digit_ref[at:at + PER_PAIR, :], tile)
        out_ref[(device + 1) * MESSAGE - PER_PAIR:(device + 1) * MESSAGE, :] = tile
    back = []
    for n in range(len(parts)):
        rows = devices * MESSAGE // len(parts)
        back.append(pltpu.make_async_copy(out_ref.at[pl.ds(n * rows, rows), :], out_hbm.at[pl.ds(n * rows, rows), :], sems.at[n]))
        back[n].start()
    for copy in back:
        copy.wait()


def gather_block(got_ref, copy, write):
    for piece in range(PIECES):
        at = (copy * PIECES + piece) * PER_PAIR
        write(slice(piece * LANES, (piece + 1) * LANES), got_ref[:, at:at + PER_PAIR, :].reshape(ROWS, LANES))


def arrival_slots(got_ref):
    digits = got_ref[:, MESSAGE - PER_PAIR:MESSAGE, :].reshape(ROWS, LANES)
    digits = jnp.transpose(digits.astype(F32))[0:8, :]
    return [
        (digits[2 * c:2 * c + 1, :] * DIGITS + digits[2 * c + 1:2 * c + 2, :]).astype(jnp.int32) for c in range(COPIES)
    ]


def arrival_ids(ids, land):
    ids = jnp.broadcast_to(ids.astype(F32), (8, ROWS)).astype(BF16)
    arrived = jnp.zeros((8, ROWS), F32)
    for at in range(0, ROWS, 256):
        place = one_hot(256, at, land)
        arrived = arrived + jnp.dot(ids[:, at:at + 256], place, preferred_element_type=F32)
    return arrived[0:1, :]


def split_kernel(got_ref, ids_ref, list_ref, out_ref, land_ref):
    def write(lanes, rows):
        out_ref[0:ROWS, lanes] = rows

    gather_block(got_ref, 0, write)
    land = arrival_slots(got_ref)[0]
    land_ref[...] = land
    ids = arrival_ids(ids_ref[...], land)
    entries = list_ref[...].astype(F32)
    row = iota((TAIL, LANES), 0)
    for at in range(0, WIDTH, LANES):
        rest = ids[:, at + WIDTH:at + WIDTH + LANES] if at + WIDTH < ROWS else jnp.zeros((1, LANES), F32)
        tail = jnp.where(row == 0, ids[:, at:at + LANES], jnp.where(row == 1, rest, entries))
        out_ref[ROWS:ROWS + TAIL, at:at + LANES] = tail.astype(BF16)


def weight_of(ref, shift):
    entries = ref[ROWS:ROWS + TAIL, 0:LANES].astype(F32)[2:3, :]
    return jnp.sum(jnp.where(iota((1, LANES), 1) == shift - 1, entries, 0.0), axis=1, keepdims=True)


def ids_row(ref):
    tail = ref[ROWS:ROWS + TAIL, :].astype(F32)
    return jnp.concatenate([tail[0:1, :], tail[1:2, 0:ROWS - WIDTH]], axis=1)


def tile_terms(scores, id_col, id_row, masked):
    rows, cols = scores.shape
    over_cols, over_rows = None, []
    for lane in range(cols // LANES):
        cut = slice(lane * LANES, (lane + 1) * LANES)
        half = jnp.tanh(scores[:, cut] * (0.5 * sharpness) - 0.5 * sharpness * threshold)
        factor = jnp.where(id_col == id_row[:, cut], 0.5, 0.25)
        term = factor * (1.0 + half)
        if masked:
            term = jnp.where(iota(term.shape, 0) == iota(term.shape, 1) + lane * LANES, 0.0, term)
        over_cols = term if over_cols is None else over_cols + term
        over_rows.append(jnp.sum(term.reshape(rows // 8, 8, LANES), axis=0))
    return over_cols, jnp.concatenate(over_rows, axis=1)


SIZE = 256
CUTS = [slice(at, at + SIZE) for at in range(0, ROWS, SIZE)]


def pair(a_ref, a_col, b_of, b_row, weight, row_acc):
    over_rows = []
    for part in CUTS:
        b = b_of(part)
        down = None
        for at in CUTS:
            by_row, by_col = tile_terms(nt(a_ref[at, :], b), a_col[at, :], b_row[:, part], False)
            row_acc[at, :] = row_acc[at, :] + weight * by_row
            down = by_col if down is None else down + by_col
        over_rows.append(weight * down)
    return jnp.sum(jnp.concatenate(over_rows, axis=1), axis=0, keepdims=True)


def own_pair(ref, a_col, row, row_acc, col_acc):
    for i, at in enumerate(CUTS):
        a = ref[at, :]
        for j, part in enumerate(CUTS):
            if j < i:
                continue
            by_row, by_col = tile_terms(nt(a, ref[part, :]), a_col[at, :], row[:, part], i == j)
            row_acc[at, :] = row_acc[at, :] + by_row
            if j > i:
                col_acc[:, part] = col_acc[:, part] + by_col


def fold_rows(acc):
    return jnp.sum(jnp.transpose(acc[...]), axis=0, keepdims=True)


def first_kernel(got_ref, own_ref, *refs):
    ids_refs, (blocks_ref, ids_out, sums_ref, col, row_acc, col_acc) = refs[:COPIES - 1], refs[COPIES - 1:]
    blocks_ref[0] = own_ref[0:ROWS, :]
    row = ids_row(own_ref)
    ids_out[0] = row
    col[...] = as_column(row)
    row_acc[...] = jnp.zeros_like(row_acc)
    col_acc[...] = jnp.zeros_like(col_acc)
    own_pair(own_ref, col, row, row_acc, col_acc)
    lands = arrival_slots(got_ref)
    for c in range(1, COPIES):

        def write(lanes, rows, c=c):
            blocks_ref[c, :, lanes] = rows

        gather_block(got_ref, c, write)
        far = arrival_ids(ids_refs[c - 1][...], lands[c])
        ids_out[c] = far
        sums_ref[c] = pair(
            own_ref, col, lambda part, c=c: blocks_ref[c, part, :], far, weight_of(own_ref, APART * c), row_acc
        )
    sums_ref[0] = fold_rows(row_acc) + jnp.sum(col_acc[...], axis=0, keepdims=True)


def second_kernel(core_ref, blocks_ref, ids_ref, sums_ref, sw_ref, *refs):
    outs, (total, col, row_acc) = refs[:COPIES + 1], refs[COPIES + 1:]
    total[...] = sums_ref[...]
    col[...] = as_column(ids_row(sw_ref))
    row_acc[...] = jnp.zeros_like(row_acc)
    for n in range(2):
        which = 1 - core_ref[0] + n
        down = pair(
            sw_ref, col, lambda part: blocks_ref[which, part, :], ids_ref[which], weight_of(sw_ref, 1 + 2 * n), row_acc
        )
        total[which] = total[which] + down
    for c in range(COPIES):
        outs[c][...] = total[c]
    outs[COPIES][...] = fold_rows(row_acc)


def end_kernel(land_ref, *refs):
    out_ref = refs[-1]
    load = refs[0][...]
    for ref in refs[1:-1]:
        load = load + ref[...]
    result = 1.0 / (1.0 + load)
    high = result.astype(BF16).astype(F32)
    mid = (result - high).astype(BF16).astype(F32)
    low = result - high - mid
    which = iota((8, ROWS), 0)
    parts = jnp.where(which == 0, high, jnp.where(which == 1, mid, jnp.where(which == 2, low, 0.0))).astype(BF16)
    for step in range(4):
        placed = nt(parts, one_hot(256, step * 256, land_ref[...]))
        out_ref[:, step * 256:(step + 1) * 256] = placed[0:1, :] + placed[1:2, :] + placed[2:3, :]


def vec(n):
    return jax.ShapeDtypeStruct((1, n), F32)


def call(kernel, out_shape, in_specs, scratch, tasks, args, mib=40, out_spec=VMEM):
    single = not isinstance(out_shape, (list, tuple))
    return pl.pallas_call(
        kernel,
        out_shape=out_shape,
        in_specs=in_specs,
        out_specs=out_spec if single else [out_spec] * len(out_shape),
        scratch_shapes=scratch,
        compiler_params=pltpu.CompilerParams(vmem_limit_bytes=mib << 20),
        cost_estimate=pl.CostEstimate(
            flops=int(HINT * tasks * 2 * ROWS * ROWS * WIDTH),
            transcendentals=int(HINT * tasks * ROWS * ROWS),
            bytes_accessed=int(HINT * (1 + tasks) * 2 * ROWS * WIDTH),
        ),
    )(*args)


def move(value, devices, change, only=None):
    pairs = [
        (p, change(p))
        for p in range(devices)
        if 0 <= change(p) < devices and (only is None or p % 2 == only)
    ]
    return lax.ppermute(value, AXES, pairs)


def local(embeddings, sorted_slot, cluster_ids, block_list):
    devices = lax.axis_size(AXES)
    position = lax.axis_index(AXES)
    core = (position % 2).astype(jnp.int32).reshape(1)
    move_d = functools.partial(move, devices=devices)
    scratch = pltpu.VMEM

    outgoing = call(
        functools.partial(front_kernel, devices),
        jax.ShapeDtypeStruct((devices * MESSAGE, LANES), BF16), [ANY] * 2,
        [scratch((1, ROWS), jnp.int32), scratch((ROWS, WIDTH), BF16), scratch((ROWS, WIDTH + LANES), BF16)]
        + [scratch((ROWS, LANES), BF16), scratch((devices * MESSAGE, LANES), BF16), pltpu.SemaphoreType.DMA((5,))],
        1, (sorted_slot.reshape(1, ROWS), embeddings), 62, ANY,
    )
    arrived = lax.all_to_all(outgoing, AXES, split_axis=0, concat_axis=0, tiled=True)
    got = arrived.reshape(devices, MESSAGE, LANES)
    ids = cluster_ids.reshape(1, ROWS)
    far_ids = [move_d(ids, change=lambda p, c=c: p - APART * c) for c in range(1, COPIES)]
    reach = position + 1 + jnp.arange(SHIFTS, dtype=jnp.int32)
    entries = jnp.pad(jnp.where(reach[None, :] < devices, block_list, 0), ((0, 0), (0, LANES - SHIFTS)))
    own, land = call(
        split_kernel,
        [jax.ShapeDtypeStruct((ROWS + TAIL, WIDTH), BF16), jax.ShapeDtypeStruct((1, ROWS), jnp.int32)],
        [VMEM] * 3, [], 0.3, (got, ids, entries), 16,
    )
    sw = move_d(own, change=lambda p: p ^ 1)
    blocks, block_ids, sums = call(
        first_kernel,
        [jax.ShapeDtypeStruct((COPIES, ROWS, WIDTH), BF16)] + [jax.ShapeDtypeStruct((COPIES, 1, ROWS), F32)] * 2,
        [VMEM] * (COPIES + 1), [scratch((ROWS, LANES), F32)] * 2 + [scratch((8, ROWS), F32)],
        2.6, (got, own, *far_ids), 24,
    )
    sums = call(
        second_kernel, [vec(ROWS)] * (COPIES + 1), [SMEM] + [VMEM] * 4,
        [scratch((COPIES, 1, ROWS), F32)] + [scratch((ROWS, LANES), F32)] * 2,
        2, (core, blocks, block_ids, sums, sw), 24,
    )
    returned = [sums[0], move_d(sums[COPIES], change=lambda p: p ^ 1)]
    returned += [move_d(sums[c], change=lambda p, c=c: p + APART * c) for c in range(1, COPIES)]
    weights = call(end_kernel, vec(ROWS), [VMEM] * (COPIES + 2), [], 0.2, (land, *returned))
    return weights.reshape(ROWS)


def solution(mesh):
    in_specs = (
        P(("grp", "gr", "gc"), None),
        P(("grp", "gr", "gc")),
        P(("grp", "gr", "gc")),
        P(("grp", "gr", "gc"), None),
    )
    out_specs = P(("grp", "gr", "gc"))
    return jax.shard_map(local, mesh=mesh, in_specs=in_specs, out_specs=out_specs, check_vma=False)
```

time: 124 us -> 111 us (0.90); the launches traced: 123 us -> 111 us
  starting transfers between devices: 42.1 us -> 28.5 us
  waiting for transfers between devices: 52.5 us -> 57.9 us
  Pallas kernels: 27.8 us -> 24.4 us
    all_to_all x1, waiting for transfers between devices: 26.5 us -> 49.5 us  [local(): lax.all_to_all(outgoing, AXES, split_axis=0, concat_axis=0, tiled=True)]
    ppermute x12 -> x6, waiting for transfers between devices: 26 us -> 8.38 us  [move(): return lax.ppermute(value, AXES, pairs)]
    ppermute x12 -> x6, starting transfers between devices: 31.9 us -> 18.1 us  [move(): return lax.ppermute(value, AXES, pairs)]
    pallas_call x8 -> x5, Pallas kernels: 27.8 us -> 24.4 us  [call(): pl.pallas_call(kernel, out_shape=out_shape, in_specs=in_specs, out_specs=...]
  transfers between devices with their start and end apart: 13 -> 7, of which waited for: 4 -> 3; matrix products, arithmetic and copies ran while one was open for 0% -> 0% of each run, Pallas kernels for 17% -> 11%
where the time goes in v4:
time: 111 us
  waiting for transfers between devices  57.9 us (52%)
  starting transfers between devices  28.5 us (26%)
  Pallas kernels  24.4 us (22%)
    all_to_all x1, waiting for transfers between devices, local(): lax.all_to_all(outgoing, AXES, split_axis=0, concat_axis=0, tiled=True)  49.5 us
    pallas_call x5, Pallas kernels, call(): pl.pallas_call(kernel, out_shape=out_shape, in_specs=in_specs, out_specs=...  24.4 us
    ppermute x6, starting transfers between devices, move(): return lax.ppermute(value, AXES, pairs)  18.1 us
    all_to_all x1, starting transfers between devices, local(): lax.all_to_all(outgoing, AXES, split_axis=0, concat_axis=0, tiled=True)  10.4 us
    ppermute x6, waiting for transfers between devices, move(): return lax.ppermute(value, AXES, pairs)  8.38 us
  transfers between devices with their start and end apart: 7, of which 3 were waited for; matrix products, arithmetic and copies ran while one was open for 0% of the time, Pallas kernels for 11%

profile of v4, /device:TPU:34, one launch (start us, length us, event | category | flops | bytes accessed | tf_op | source)
XLA Modules:
  0.0 110.9 jit_solution(18020257997957605492)
XLA Ops:
  0.0 6.3 %shard_map.46 = bf16[19456,128]{1,0:T(8,128)(2,1)} custom-call(s32[1,1024]{1,0:T(1,128)} %bitcast.9, bf16[1024,768]{1,0:T(8,128)(2,1)} %emb_ref.1), custom_call_target="tpu_custom_call" | custom-call | flops 32212254720 | bytes 62914560 | tf_op jit(solution)/shard_map/pallas_call | solution.py:267
  6.3 0.0 copy-start
  6.3 0.0 copy-start.1
  6.3 10.4 %all-to-all-start = ((bf16[64,304,128]{2,1,0:T(8,128)(2,1)}), bf16[64,304,128]{2,1,0:T(8,128)(2,1)}, u32[]{:S(2)}, u32[]{:S(2)}) async-start(bf16[64,304,128]{2,1,0:T(8,128)(2,1)} %bitcast.8), calls=%async_computation | async-start | bytes 9961472 | tf_op jit(solution)/shard_map/all_to_all | solution.py:305
  16.7 0.0 copy-done
  16.7 7.0 %collective-permute-start = (s32[1,1024]{1,0:T(1,128)S(1)}, s32[1,1024]{1,0:T(1,128)S(1)}, u32[]{:S(2)}, u32[]{:S(2)}) collective-permute-start(s32[1,1024]{1,0:T(1,128)S(1)} %bitcast.5), channel_id=1, source_target_pairs={{2,0},{3,1},{4,2},{5,3},{6,4},{7,5},{8,6},{9,7},{10,8},{11,9},{12,... | collective-permute-start | bytes 12296 | tf_op jit(solution)/shard_map/ppermute | solution.py:288
  23.7 2.8 %collective-permute-start.1 = (s32[1,1024]{1,0:T(1,128)S(1)}, s32[1,1024]{1,0:T(1,128)S(1)}, u32[]{:S(2)}, u32[]{:S(2)}) collective-permute-start(s32[1,1024]{1,0:T(1,128)S(1)} %bitcast.6), channel_id=1, source_target_pairs={{4,0},{5,1},{6,2},{7,3},{8,4},{9,5},{10,6},{11,7},{12,8},{13,9},{1... | collective-permute-start | bytes 12296 | tf_op jit(solution)/shard_map/ppermute | solution.py:288
  26.5 0.0 copy-done.1
  26.5 49.5 %all-to-all-done.got_ref = bf16[64,304,128]{2,1,0:T(8,128)(2,1)} async-done(((bf16[64,304,128]{2,1,0:T(8,128)(2,1)}), bf16[64,304,128]{2,1,0:T(8,128)(2,1)}, u32[]{:S(2)}, u32[]{:S(2)}) %all-to-all-start) | async-done | bytes 4980768 | tf_op jit(solution)/shard_map/all_to_all | solution.py:305
  76.0 3.1 %shard_map.47 = (bf16[1040,768]{1,0:T(8,128)(2,1)S(1)}, s32[1,1024]{1,0:T(1,128)S(1)}) custom-call(bf16[64,304,128]{2,1,0:T(8,128)(2,1)} %all-to-all-done.got_ref, s32[1,1024]{1,0:T(1,128)S(1)} %bitcast.7, s32[1,128]{1,0:T(1,128)S(1)} %pad.4.list_ref), custom_call_target="tpu_custom_call" | custom-call | flops 9663676416 | bytes 40894464 | tf_op jit(solution)/shard_map/pallas_call | solution.py:267
  79.2 2.2 %collective-permute-start.2 = (bf16[1040,768]{1,0:T(8,128)(2,1)S(1)}, bf16[1040,768]{1,0:T(8,128)(2,1)S(1)}, u32[]{:S(2)}, u32[]{:S(2)}) collective-permute-start(bf16[1040,768]{1,0:T(8,128)(2,1)S(1)} %get-tuple-element.15.own_ref), channel_id=1, source_target_pairs={{0,1},{1,0},{2,3},{3,2},{4,5},{5,4},{6,7},{7,6},{8,9},{9,8},{10,11... | collective-permute-start | bytes 4792328 | tf_op jit(solution)/shard_map/ppermute | solution.py:288
  81.4 0.0 collective-permute-done.refs_0_
  81.4 0.0 collective-permute-done.1.refs_1_
  81.4 9.4 %shard_map.48 = (bf16[3,1024,768]{2,1,0:T(8,128)(2,1)S(1)}, f32[3,1,1024]{2,1,0:T(1,128)S(1)}, f32[3,1,1024]{2,1,0:T(1,128)S(1)}) custom-call(bf16[64,304,128]{2,1,0:T(8,128)(2,1)} %all-to-all-done.got_ref, bf16[1040,768]{1,0:T(8,128)(2,1)S(1)} %get-tuple-element.15.own_ref, s32[1,1024]{1,0:T(1,128)S(1)} %collective-permute-done.refs_0_, ...), custom_call_target="tpu_custom_call" | custom-call | flops 83751862272 | bytes 113246208 | tf_op jit(solution)/shard_map/pallas_call | solution.py:267
  90.9 0.0 collective-permute-done.2.sw_ref
  90.9 4.3 %shard_map.49 = (f32[1,1024]{1,0:T(1,128)S(1)}, f32[1,1024]{1,0:T(1,128)S(1)}, f32[1,1024]{1,0:T(1,128)S(1)}, f32[1,1024]{1,0:T(1,128)S(1)}) custom-call(s32[1]{0:T(128)} %bitcast.3.core_ref, bf16[3,1024,768]{2,1,0:T(8,128)(2,1)S(1)} %get-tuple-element.16.blocks_ref, f32[3,1,1024]{2,1,0:T(1,128)S(1)} %get-tuple-element.17.ids_ref, ...), custom_call_target="tpu_custom_call" | custom-call | flops 64424509440 | bytes 94371840 | tf_op jit(solution)/shard_map/pallas_call | solution.py:267
  95.1 0.1 collective-permute-start.3
  95.2 4.1 %collective-permute-start.4 = (f32[1,1024]{1,0:T(1,128)S(1)}, f32[1,1024]{1,0:T(1,128)S(1)}, u32[]{:S(2)}, u32[]{:S(2)}) collective-permute-start(f32[1,1024]{1,0:T(1,128)S(1)} %get-tuple-element.21), channel_id=1, source_target_pairs={{0,2},{1,3},{2,4},{3,5},{4,6},{5,7},{6,8},{7,9},{8,10},{9,11},{10,... | collective-permute-start | bytes 12296 | tf_op jit(solution)/shard_map/ppermute | solution.py:288
  99.4 1.9 %collective-permute-start.5 = (f32[1,1024]{1,0:T(1,128)S(1)}, f32[1,1024]{1,0:T(1,128)S(1)}, u32[]{:S(2)}, u32[]{:S(2)}) collective-permute-start(f32[1,1024]{1,0:T(1,128)S(1)} %get-tuple-element.22), channel_id=1, source_target_pairs={{0,4},{1,5},{2,6},{3,7},{4,8},{5,9},{6,10},{7,11},{8,12},{9,13},{1... | collective-permute-start | bytes 12296 | tf_op jit(solution)/shard_map/ppermute | solution.py:288
  101.3 0.0 collective-permute-done.3.refs_1_
  101.3 3.9 %collective-permute-done.4.refs_2_ = f32[1,1024]{1,0:T(1,128)S(1)} collective-permute-done((f32[1,1024]{1,0:T(1,128)S(1)}, f32[1,1024]{1,0:T(1,128)S(1)}, u32[]{:S(2)}, u32[]{:S(2)}) %collective-permute-start.4) | collective-permute-done | bytes 4128 | tf_op jit(solution)/shard_map/ppermute | solution.py:288
  105.2 4.4 %collective-permute-done.5.refs_3_ = f32[1,1024]{1,0:T(1,128)S(1)} collective-permute-done((f32[1,1024]{1,0:T(1,128)S(1)}, f32[1,1024]{1,0:T(1,128)S(1)}, u32[]{:S(2)}, u32[]{:S(2)}) %collective-permute-start.5) | collective-permute-done | bytes 4128 | tf_op jit(solution)/shard_map/ppermute | solution.py:288
  109.7 1.3 %shard_map.50 = f32[1,1024]{1,0:T(1,128)} custom-call(s32[1,1024]{1,0:T(1,128)S(1)} %get-tuple-element.14.land_ref, f32[1,1024]{1,0:T(1,128)S(1)} %get-tuple-element.19.refs_0_, f32[1,1024]{1,0:T(1,128)S(1)} %collective-permute-done.3.refs_1_, f32[1,1024]{1,0:T(1,128)S(1)} %collective-permute-done.4.refs_2_, f32[1,1024]{1,0:T(1,128)S(1)} %collective-permute-done.5.refs_3_), custom_call_target="tpu_custom_call" | custom-call | flops 6442450944 | bytes 37748736 | tf_op jit(solution)/shard_map/pallas_call | solution.py:267
  (2 shorter events, 0.0 us)
Async XLA Ops:
  6.3 10.4 %copy-start = (s32[1024]{0:T(1024)S(1)}, s32[1024]{0:T(1024)}, u32[]{:S(2)}) copy-start(s32[1024]{0:T(1024)} %param.6) | copy-start | bytes 12292
  6.3 20.2 %copy-start.1 = (s32[1,4]{1,0:T(1,128)S(1)}, s32[1,4]{1,0:T(1,128)}, u32[]{:S(2)}) copy-start(s32[1,4]{1,0:T(1,128)} %param.7) | copy-start | bytes 52
  6.3 69.7 %all-to-all-start = ((bf16[64,304,128]{2,1,0:T(8,128)(2,1)}), bf16[64,304,128]{2,1,0:T(8,128)(2,1)}, u32[]{:S(2)}, u32[]{:S(2)}) async-start(bf16[64,304,128]{2,1,0:T(8,128)(2,1)} %bitcast.8), calls=%async_computation | async-start | bytes 9961472 | tf_op jit(solution)/shard_map/all_to_all | solution.py:305
  16.7 64.7 %collective-permute-start = (s32[1,1024]{1,0:T(1,128)S(1)}, s32[1,1024]{1,0:T(1,128)S(1)}, u32[]{:S(2)}, u32[]{:S(2)}) collective-permute-start(s32[1,1024]{1,0:T(1,128)S(1)} %bitcast.5), channel_id=1, source_target_pairs={{2,0},{3,1},{4,2},{5,3},{6,4},{7,5},{8,6},{9,7},{10,8},{11,9},{12,... | collective-permute-start | bytes 12296 | tf_op jit(solution)/shard_map/ppermute | solution.py:288
  23.7 57.7 %collective-permute-start.1 = (s32[1,1024]{1,0:T(1,128)S(1)}, s32[1,1024]{1,0:T(1,128)S(1)}, u32[]{:S(2)}, u32[]{:S(2)}) collective-permute-start(s32[1,1024]{1,0:T(1,128)S(1)} %bitcast.6), channel_id=1, source_target_pairs={{4,0},{5,1},{6,2},{7,3},{8,4},{9,5},{10,6},{11,7},{12,8},{13,9},{1... | collective-permute-start | bytes 12296 | tf_op jit(solution)/shard_map/ppermute | solution.py:288
  79.2 11.7 %collective-permute-start.2 = (bf16[1040,768]{1,0:T(8,128)(2,1)S(1)}, bf16[1040,768]{1,0:T(8,128)(2,1)S(1)}, u32[]{:S(2)}, u32[]{:S(2)}) collective-permute-start(bf16[1040,768]{1,0:T(8,128)(2,1)S(1)} %get-tuple-element.15.own_ref), channel_id=1, source_target_pairs={{0,1},{1,0},{2,3},{3,2},{4,5},{5,4},{6,7},{7,6},{8,9},{9,8},{10,11... | collective-permute-start | bytes 4792328 | tf_op jit(solution)/shard_map/ppermute | solution.py:288
  95.1 6.2 %collective-permute-start.3 = (f32[1,1024]{1,0:T(1,128)S(1)}, f32[1,1024]{1,0:T(1,128)S(1)}, u32[]{:S(2)}, u32[]{:S(2)}) collective-permute-start(f32[1,1024]{1,0:T(1,128)S(1)} %get-tuple-element.20), channel_id=1, source_target_pairs={{0,1},{1,0},{2,3},{3,2},{4,5},{5,4},{6,7},{7,6},{8,9},{9,8},{10,11... | collective-permute-start | bytes 12296 | tf_op jit(solution)/shard_map/ppermute | solution.py:288
  95.2 10.0 %collective-permute-start.4 = (f32[1,1024]{1,0:T(1,128)S(1)}, f32[1,1024]{1,0:T(1,128)S(1)}, u32[]{:S(2)}, u32[]{:S(2)}) collective-permute-start(f32[1,1024]{1,0:T(1,128)S(1)} %get-tuple-element.21), channel_id=1, source_target_pairs={{0,2},{1,3},{2,4},{3,5},{4,6},{5,7},{6,8},{7,9},{8,10},{9,11},{10,... | collective-permute-start | bytes 12296 | tf_op jit(solution)/shard_map/ppermute | solution.py:288
  99.4 10.3 %collective-permute-start.5 = (f32[1,1024]{1,0:T(1,128)S(1)}, f32[1,1024]{1,0:T(1,128)S(1)}, u32[]{:S(2)}, u32[]{:S(2)}) collective-permute-start(f32[1,1024]{1,0:T(1,128)S(1)} %get-tuple-element.22), channel_id=1, source_target_pairs={{0,4},{1,5},{2,6},{3,7},{4,8},{5,9},{6,10},{7,11},{8,12},{9,13},{1... | collective-permute-start | bytes 12296 | tf_op jit(solution)/shard_map/ppermute | solution.py:288

commit v5 on v4

--- a/solution.py
+++ b/solution.py
@@ -78,45 +78,61 @@
         mean = jnp.sum(values * values, axis=1, keepdims=True) * (1.0 / WIDTH)
         inverse = lax.rsqrt(mean + 1e-06) * (1.0 / math.sqrt(WIDTH))
         unit_ref[part, 0:WIDTH] = (values * inverse).astype(BF16)
+    reach = APART * (COPIES - 1)
+    per_part = size // PER_PAIR
+    back = []
+
+    def send(first, count):
+        for device in range(first, first + count):
+            tile = digit_ref[device * PER_PAIR:(device + 1) * PER_PAIR, :]
+            for copy in range(1, COPIES):
+                at = (device + APART * copy) % devices * PER_PAIR
+                tile = jnp.where(lane == copy, digit_ref[at:at + PER_PAIR, :], tile)
+            out_ref[(device + 1) * MESSAGE - PER_PAIR:(device + 1) * MESSAGE, :] = tile
+        rows = pl.ds(first * MESSAGE, count * MESSAGE)
+        back.append(pltpu.make_async_copy(out_ref.at[rows, :], out_hbm.at[rows, :], sems.at[len(back)]))
+        back[-1].start()
+
+    lane = iota((PER_PAIR, LANES), 1) // 2
     for n, part in enumerate(parts):
         place = one_hot(size, n * size, dest)
         placed = jnp.dot(place, unit_ref[...], preferred_element_type=F32).astype(BF16)
         digit_ref[part, :] = placed[:, WIDTH:]
-        for i in range(size // PER_PAIR):
-            block = n * (size // PER_PAIR) + i
+        for i in range(per_part):
+            block = n * per_part + i
             rows = placed[i * PER_PAIR:(i + 1) * PER_PAIR, :]
             for copy in range(COPIES):
                 at = (block - APART * copy) % devices * MESSAGE + copy * PIECES * PER_PAIR
                 for piece in range(PIECES):
                     out_ref[at + piece * PER_PAIR:at + (piece + 1) * PER_PAIR, :] = rows[:, piece * LANES:(piece + 1) * LANES]
-    lane = iota((PER_PAIR, LANES), 1) // 2
-    for device in range(devices):
-        tile = digit_ref[device * PER_PAIR:(device + 1) * PER_PAIR, :]
-        for copy in range(1, COPIES):
-            at = (device + APART * copy) % devices * PER_PAIR
-            tile = jnp.where(lane == copy, digit_ref[at:at + PER_PAIR, :], tile)
-        out_ref[(device + 1) * MESSAGE - PER_PAIR:(device + 1) * MESSAGE, :] = tile
-    back = []
-    for n in range(len(parts)):
-        rows = devices * MESSAGE // len(parts)
-        back.append(pltpu.make_async_copy(out_ref.at[pl.ds(n * rows, rows), :], out_hbm.at[pl.ds(n * rows, rows), :], sems.at[n]))
-        back[n].start()
+        if n == 0:
+            send(0, per_part - reach)
+        else:
+            send(n * per_part - reach, per_part)
+    send(devices - reach, reach)
     for copy in back:
         copy.wait()
 
 
-def gather_block(got_ref, copy, write):
+def tiles(got_hbm, copy, target, sem):
+    started = []
     for piece in range(PIECES):
         at = (copy * PIECES + piece) * PER_PAIR
-        write(slice(piece * LANES, (piece + 1) * LANES), got_ref[:, at:at + PER_PAIR, :].reshape(ROWS, LANES))
-
-
-def arrival_slots(got_ref):
-    digits = got_ref[:, MESSAGE - PER_PAIR:MESSAGE, :].reshape(ROWS, LANES)
-    digits = jnp.transpose(digits.astype(F32))[0:8, :]
-    return [
-        (digits[2 * c:2 * c + 1, :] * DIGITS + digits[2 * c + 1:2 * c + 2, :]).astype(jnp.int32) for c in range(COPIES)
-    ]
+        lanes = pl.ds(piece * LANES, LANES)
+        started.append(pltpu.make_async_copy(got_hbm.at[:, pl.ds(at, PER_PAIR), :], target.at[:, :, lanes], sem.at[piece]))
+        started[-1].start()
+    return started
+
+
+def slot_tiles(got_hbm, target, sem):
+    copy = pltpu.make_async_copy(got_hbm.at[:, pl.ds(MESSAGE - PER_PAIR, PER_PAIR), :], target, sem)
+    copy.start()
+    return copy
+
+
+def arrival_slots(digits, copies):
+    digits = jnp.transpose(digits.reshape(ROWS, LANES).astype(F32))[0:8, :]
+    return [(digits[2 * c:2 * c + 1, :] * DIGITS + digits[2 * c + 1:2 * c + 2, :]).astype(jnp.int32) for c in copies]
 
 
 def arrival_ids(ids, land):
@@ -128,12 +144,11 @@
     return arrived[0:1, :]
 
 
-def split_kernel(got_ref, ids_ref, list_ref, out_ref, land_ref):
-    def write(lanes, rows):
-        out_ref[0:ROWS, lanes] = rows
-
-    gather_block(got_ref, 0, write)
-    land = arrival_slots(got_ref)[0]
+def split_kernel(got_hbm, ids_ref, list_ref, out_ref, land_ref, digit_ref, row_ref, sems):
+    slots = slot_tiles(got_hbm, digit_ref, sems.at[PIECES])
+    rows = tiles(got_hbm, 0, row_ref, sems)
+    slots.wait()
+    land = arrival_slots(digit_ref[...], (0,))[0]
     land_ref[...] = land
     ids = arrival_ids(ids_ref[...], land)
     entries = list_ref[...].astype(F32)
@@ -142,6 +157,9 @@
         rest = ids[:, at + WIDTH:at + WIDTH + LANES] if at + WIDTH < ROWS else jnp.zeros((1, LANES), F32)
         tail = jnp.where(row == 0, ids[:, at:at + LANES], jnp.where(row == 1, rest, entries))
         out_ref[ROWS:ROWS + TAIL, at:at + LANES] = tail.astype(BF16)
+    for copy in rows:
+        copy.wait()
+    out_ref[0:ROWS, :] = row_ref[...].reshape(ROWS, WIDTH)
 
 
 def weight_of(ref, shift):
@@ -202,28 +220,34 @@
     return jnp.sum(jnp.transpose(acc[...]), axis=0, keepdims=True)
 
 
-def first_kernel(got_ref, own_ref, *refs):
-    ids_refs, (blocks_ref, ids_out, sums_ref, col, row_acc, col_acc) = refs[:COPIES - 1], refs[COPIES - 1:]
-    blocks_ref[0] = own_ref[0:ROWS, :]
+def first_kernel(devices, got_hbm, own_ref, *refs):
+    ids_refs, (blocks_ref, ids_out, sums_ref, col, row_acc, col_acc, digit_ref, sems) = refs[:COPIES - 1], refs[COPIES - 1:]
+    slots = slot_tiles(got_hbm, digit_ref, sems.at[0, PIECES])
+    rows = [tiles(got_hbm, c, blocks_ref.at[c], sems.at[c]) for c in range(1, COPIES)]
+    blocks_ref[0] = own_ref[0:ROWS, :].reshape(devices, PER_PAIR, WIDTH)
     row = ids_row(own_ref)
     ids_out[0] = row
     col[...] = as_column(row)
     row_acc[...] = jnp.zeros_like(row_acc)
     col_acc[...] = jnp.zeros_like(col_acc)
     own_pair(own_ref, col, row, row_acc, col_acc)
-    lands = arrival_slots(got_ref)
+    slots.wait()
+    lands = arrival_slots(digit_ref[...], range(1, COPIES))
     for c in range(1, COPIES):
-
-        def write(lanes, rows, c=c):
-            blocks_ref[c, :, lanes] = rows
-
-        gather_block(got_ref, c, write)
-        far = arrival_ids(ids_refs[c - 1][...], lands[c])
+        far = arrival_ids(ids_refs[c - 1][...], lands[c - 1])
         ids_out[c] = far
-        sums_ref[c] = pair(
-            own_ref, col, lambda part, c=c: blocks_ref[c, part, :], far, weight_of(own_ref, APART * c), row_acc
-        )
+        for copy in rows[c - 1]:
+            copy.wait()
+        sums_ref[c] = pair(own_ref, col, block_part(blocks_ref, c), far, weight_of(own_ref, APART * c), row_acc)
     sums_ref[0] = fold_rows(row_acc) + jnp.sum(col_acc[...], axis=0, keepdims=True)
+
+
+def block_part(blocks_ref, which):
+    def part(rows):
+        at = pl.ds(rows.start // PER_PAIR, SIZE // PER_PAIR)
+        return blocks_ref[which, at, :, :].reshape(SIZE, WIDTH)
+
+    return part
 
 
 def second_kernel(core_ref, blocks_ref, ids_ref, sums_ref, sw_ref, *refs):
@@ -234,7 +258,7 @@
     for n in range(2):
         which = 1 - core_ref[0] + n
         down = pair(
-            sw_ref, col, lambda part: blocks_ref[which, part, :], ids_ref[which], weight_of(sw_ref, 1 + 2 * n), row_acc
+            sw_ref, col, block_part(blocks_ref, which), ids_ref[which], weight_of(sw_ref, 1 + 2 * n), row_acc
         )
         total[which] = total[which] + down
     for c in range(COPIES):
@@ -308,22 +332,26 @@
     far_ids = [move_d(ids, change=lambda p, c=c: p - APART * c) for c in range(1, COPIES)]
     reach = position + 1 + jnp.arange(SHIFTS, dtype=jnp.int32)
     entries = jnp.pad(jnp.where(reach[None, :] < devices, block_list, 0), ((0, 0), (0, LANES - SHIFTS)))
+    tile_rows = lambda width: pltpu.VMEM((devices, PER_PAIR, width), BF16)
+    sems = pltpu.SemaphoreType.DMA
     own, land = call(
         split_kernel,
         [jax.ShapeDtypeStruct((ROWS + TAIL, WIDTH), BF16), jax.ShapeDtypeStruct((1, ROWS), jnp.int32)],
-        [VMEM] * 3, [], 0.3, (got, ids, entries), 16,
+        [ANY, VMEM, VMEM], [tile_rows(LANES), tile_rows(WIDTH), sems((PIECES + 1,))], 0.3, (got, ids, entries), 16,
     )
     sw = move_d(own, change=lambda p: p ^ 1)
     blocks, block_ids, sums = call(
-        first_kernel,
-        [jax.ShapeDtypeStruct((COPIES, ROWS, WIDTH), BF16)] + [jax.ShapeDtypeStruct((COPIES, 1, ROWS), F32)] * 2,
-        [VMEM] * (COPIES + 1), [scratch((ROWS, LANES), F32)] * 2 + [scratch((8, ROWS), F32)],
-        2.6, (got, own, *far_ids), 24,
+        functools.partial(first_kernel, devices),
+        [jax.ShapeDtypeStruct((COPIES, devices, PER_PAIR, WIDTH), BF16)]
+        + [jax.ShapeDtypeStruct((COPIES, 1, ROWS), F32)] * 2,
+        [ANY] + [VMEM] * COPIES,
+        [scratch((ROWS, LANES), F32)] * 2 + [scratch((8, ROWS), F32), tile_rows(LANES), sems((COPIES, PIECES + 1))],
+        2.6, (got, own, *far_ids), 16,
     )
     sums = call(
         second_kernel, [vec(ROWS)] * (COPIES + 1), [SMEM] + [VMEM] * 4,
         [scratch((COPIES, 1, ROWS), F32)] + [scratch((ROWS, LANES), F32)] * 2,
-        2, (core, blocks, block_ids, sums, sw), 24,
+        2, (core, blocks, block_ids, sums, sw), 16,
     )
     returned = [sums[0], move_d(sums[COPIES], change=lambda p: p ^ 1)]
     returned += [move_d(sums[c], change=lambda p, c=c: p + APART * c) for c in range(1, COPIES)]

time: 111 us -> 106 us (0.955)
  Pallas kernels: 24.4 us -> 19 us
    pallas_call x5, Pallas kernels: 24.4 us -> 19 us  [call(): pl.pallas_call(kernel, out_shape=out_shape, in_specs=in_specs, out_specs=...]
  transfers between devices with their start and end apart: 7 -> 7, of which waited for: 3 -> 3; matrix products, arithmetic and copies ran while one was open for 0% -> 0% of each run, Pallas kernels for 11% -> 8%
where the time goes in v5:
time: 106 us
  waiting for transfers between devices  57.9 us (55%)
  starting transfers between devices  28.5 us (27%)
  Pallas kernels  19 us (18%)
    all_to_all x1, waiting for transfers between devices, local(): lax.all_to_all(outgoing, AXES, split_axis=0, concat_axis=0, tiled=True)  49.5 us
    pallas_call x5, Pallas kernels, call(): pl.pallas_call(kernel, out_shape=out_shape, in_specs=in_specs, out_specs=...  19 us
    ppermute x6, starting transfers between devices, move(): return lax.ppermute(value, AXES, pairs)  18.2 us
    all_to_all x1, starting transfers between devices, local(): lax.all_to_all(outgoing, AXES, split_axis=0, concat_axis=0, tiled=True)  10.4 us
    ppermute x6, waiting for transfers between devices, move(): return lax.ppermute(value, AXES, pairs)  8.38 us
  transfers between devices with their start and end apart: 7, of which 3 were waited for; matrix products, arithmetic and copies ran while one was open for 0% of the time, Pallas kernels for 8%

profile of v5, /device:TPU:34, one launch (start us, length us, event | category | flops | bytes accessed | tf_op | source)
XLA Modules:
  0.0 105.6 jit_solution(12110144803903166228)
XLA Ops:
  0.0 5.3 %shard_map.46 = bf16[19456,128]{1,0:T(8,128)(2,1)} custom-call(s32[1,1024]{1,0:T(1,128)} %bitcast.9, bf16[1024,768]{1,0:T(8,128)(2,1)} %emb_ref.1), custom_call_target="tpu_custom_call" | custom-call | flops 32212254720 | bytes 62914560 | tf_op jit(solution)/shard_map/pallas_call | solution.py:291
  5.3 0.0 copy-start
  5.3 0.0 copy-start.1
  5.3 10.4 %all-to-all-start = ((bf16[64,304,128]{2,1,0:T(8,128)(2,1)}), bf16[64,304,128]{2,1,0:T(8,128)(2,1)}, u32[]{:S(2)}, u32[]{:S(2)}) async-start(bf16[64,304,128]{2,1,0:T(8,128)(2,1)} %bitcast.8), calls=%async_computation | async-start | bytes 9961472 | tf_op jit(solution)/shard_map/all_to_all | solution.py:329
  15.7 0.0 copy-done
  15.7 7.0 %collective-permute-start = (s32[1,1024]{1,0:T(1,128)S(1)}, s32[1,1024]{1,0:T(1,128)S(1)}, u32[]{:S(2)}, u32[]{:S(2)}) collective-permute-start(s32[1,1024]{1,0:T(1,128)S(1)} %bitcast.5), channel_id=1, source_target_pairs={{2,0},{3,1},{4,2},{5,3},{6,4},{7,5},{8,6},{9,7},{10,8},{11,9},{12,... | collective-permute-start | bytes 12296 | tf_op jit(solution)/shard_map/ppermute | solution.py:312
  22.7 2.8 %collective-permute-start.1 = (s32[1,1024]{1,0:T(1,128)S(1)}, s32[1,1024]{1,0:T(1,128)S(1)}, u32[]{:S(2)}, u32[]{:S(2)}) collective-permute-start(s32[1,1024]{1,0:T(1,128)S(1)} %bitcast.6), channel_id=1, source_target_pairs={{4,0},{5,1},{6,2},{7,3},{8,4},{9,5},{10,6},{11,7},{12,8},{13,9},{1... | collective-permute-start | bytes 12296 | tf_op jit(solution)/shard_map/ppermute | solution.py:312
  25.4 0.0 copy-done.1
  25.5 49.5 %all-to-all-done.got_hbm = bf16[64,304,128]{2,1,0:T(8,128)(2,1)} async-done(((bf16[64,304,128]{2,1,0:T(8,128)(2,1)}), bf16[64,304,128]{2,1,0:T(8,128)(2,1)}, u32[]{:S(2)}, u32[]{:S(2)}) %all-to-all-start) | async-done | bytes 4980768 | tf_op jit(solution)/shard_map/all_to_all | solution.py:329
  75.0 1.6 %shard_map.47 = (bf16[1040,768]{1,0:T(8,128)(2,1)S(1)}, s32[1,1024]{1,0:T(1,128)S(1)}) custom-call(bf16[64,304,128]{2,1,0:T(8,128)(2,1)} %all-to-all-done.got_hbm, s32[1,1024]{1,0:T(1,128)S(1)} %bitcast.7, s32[1,128]{1,0:T(1,128)S(1)} %pad.4.list_ref), custom_call_target="tpu_custom_call" | custom-call | flops 9663676416 | bytes 40894464 | tf_op jit(solution)/shard_map/pallas_call | solution.py:291
  76.6 2.3 %collective-permute-start.2 = (bf16[1040,768]{1,0:T(8,128)(2,1)S(1)}, bf16[1040,768]{1,0:T(8,128)(2,1)S(1)}, u32[]{:S(2)}, u32[]{:S(2)}) collective-permute-start(bf16[1040,768]{1,0:T(8,128)(2,1)S(1)} %get-tuple-element.15.own_ref), channel_id=1, source_target_pairs={{0,1},{1,0},{2,3},{3,2},{4,5},{5,4},{6,7},{7,6},{8,9},{9,8},{10,11... | collective-permute-start | bytes 4792328 | tf_op jit(solution)/shard_map/ppermute | solution.py:312
  78.9 0.0 collective-permute-done.refs_0_
  78.9 0.0 collective-permute-done.1.refs_1_
  78.9 6.7 %shard_map.48 = (bf16[3,64,16,768]{3,2,1,0:T(8,128)(2,1)S(1)}, f32[3,1,1024]{2,1,0:T(1,128)S(1)}, f32[3,1,1024]{2,1,0:T(1,128)S(1)}) custom-call(bf16[64,304,128]{2,1,0:T(8,128)(2,1)} %all-to-all-done.got_hbm, bf16[1040,768]{1,0:T(8,128)(2,1)S(1)} %get-tuple-element.15.own_ref, s32[1,1024]{1,0:T(1,128)S(1)} %collective-permute-done.refs_0_, ...), custom_call_target="tpu_custom_call" | custom-call | flops 83751862272 | bytes 113246208 | tf_op jit(solution)/shard_map/pallas_call | solution.py:291
  85.5 0.0 collective-permute-done.2.sw_ref
  85.6 4.2 %shard_map.49 = (f32[1,1024]{1,0:T(1,128)S(1)}, f32[1,1024]{1,0:T(1,128)S(1)}, f32[1,1024]{1,0:T(1,128)S(1)}, f32[1,1024]{1,0:T(1,128)S(1)}) custom-call(s32[1]{0:T(128)} %bitcast.3.core_ref, bf16[3,64,16,768]{3,2,1,0:T(8,128)(2,1)S(1)} %get-tuple-element.16.blocks_ref, f32[3,1,1024]{2,1,0:T(1,128)S(1)} %get-tuple-element.17.ids_ref, ...), custom_call_target="tpu_custom_call" | custom-call | flops 64424509440 | bytes 94371840 | tf_op jit(solution)/shard_map/pallas_call | solution.py:291
  89.8 0.1 collective-permute-start.3
  89.9 4.1 %collective-permute-start.4 = (f32[1,1024]{1,0:T(1,128)S(1)}, f32[1,1024]{1,0:T(1,128)S(1)}, u32[]{:S(2)}, u32[]{:S(2)}) collective-permute-start(f32[1,1024]{1,0:T(1,128)S(1)} %get-tuple-element.21), channel_id=1, source_target_pairs={{0,2},{1,3},{2,4},{3,5},{4,6},{5,7},{6,8},{7,9},{8,10},{9,11},{10,... | collective-permute-start | bytes 12296 | tf_op jit(solution)/shard_map/ppermute | solution.py:312
  94.1 1.9 %collective-permute-start.5 = (f32[1,1024]{1,0:T(1,128)S(1)}, f32[1,1024]{1,0:T(1,128)S(1)}, u32[]{:S(2)}, u32[]{:S(2)}) collective-permute-start(f32[1,1024]{1,0:T(1,128)S(1)} %get-tuple-element.22), channel_id=1, source_target_pairs={{0,4},{1,5},{2,6},{3,7},{4,8},{5,9},{6,10},{7,11},{8,12},{9,13},{1... | collective-permute-start | bytes 12296 | tf_op jit(solution)/shard_map/ppermute | solution.py:312
  96.0 0.0 collective-permute-done.3.refs_1_
  96.0 3.9 %collective-permute-done.4.refs_2_ = f32[1,1024]{1,0:T(1,128)S(1)} collective-permute-done((f32[1,1024]{1,0:T(1,128)S(1)}, f32[1,1024]{1,0:T(1,128)S(1)}, u32[]{:S(2)}, u32[]{:S(2)}) %collective-permute-start.4) | collective-permute-done | bytes 4128 | tf_op jit(solution)/shard_map/ppermute | solution.py:312
  99.9 4.5 %collective-permute-done.5.refs_3_ = f32[1,1024]{1,0:T(1,128)S(1)} collective-permute-done((f32[1,1024]{1,0:T(1,128)S(1)}, f32[1,1024]{1,0:T(1,128)S(1)}, u32[]{:S(2)}, u32[]{:S(2)}) %collective-permute-start.5) | collective-permute-done | bytes 4128 | tf_op jit(solution)/shard_map/ppermute | solution.py:312
  104.4 1.3 %shard_map.50 = f32[1,1024]{1,0:T(1,128)} custom-call(s32[1,1024]{1,0:T(1,128)S(1)} %get-tuple-element.14.land_ref, f32[1,1024]{1,0:T(1,128)S(1)} %get-tuple-element.19.refs_0_, f32[1,1024]{1,0:T(1,128)S(1)} %collective-permute-done.3.refs_1_, f32[1,1024]{1,0:T(1,128)S(1)} %collective-permute-done.4.refs_2_, f32[1,1024]{1,0:T(1,128)S(1)} %collective-permute-done.5.refs_3_), custom_call_target="tpu_custom_call" | custom-call | flops 6442450944 | bytes 37748736 | tf_op jit(solution)/shard_map/pallas_call | solution.py:291
  (2 shorter events, 0.0 us)
Async XLA Ops:
  5.3 10.4 %copy-start = (s32[1024]{0:T(1024)S(1)}, s32[1024]{0:T(1024)}, u32[]{:S(2)}) copy-start(s32[1024]{0:T(1024)} %param.6) | copy-start | bytes 12292
  5.3 20.2 %copy-start.1 = (s32[1,4]{1,0:T(1,128)S(1)}, s32[1,4]{1,0:T(1,128)}, u32[]{:S(2)}) copy-start(s32[1,4]{1,0:T(1,128)} %param.7) | copy-start | bytes 52
  5.3 69.7 %all-to-all-start = ((bf16[64,304,128]{2,1,0:T(8,128)(2,1)}), bf16[64,304,128]{2,1,0:T(8,128)(2,1)}, u32[]{:S(2)}, u32[]{:S(2)}) async-start(bf16[64,304,128]{2,1,0:T(8,128)(2,1)} %bitcast.8), calls=%async_computation | async-start | bytes 9961472 | tf_op jit(solution)/shard_map/all_to_all | solution.py:329
  15.7 63.2 %collective-permute-start = (s32[1,1024]{1,0:T(1,128)S(1)}, s32[1,1024]{1,0:T(1,128)S(1)}, u32[]{:S(2)}, u32[]{:S(2)}) collective-permute-start(s32[1,1024]{1,0:T(1,128)S(1)} %bitcast.5), channel_id=1, source_target_pairs={{2,0},{3,1},{4,2},{5,3},{6,4},{7,5},{8,6},{9,7},{10,8},{11,9},{12,... | collective-permute-start | bytes 12296 | tf_op jit(solution)/shard_map/ppermute | solution.py:312
  22.7 56.2 %collective-permute-start.1 = (s32[1,1024]{1,0:T(1,128)S(1)}, s32[1,1024]{1,0:T(1,128)S(1)}, u32[]{:S(2)}, u32[]{:S(2)}) collective-permute-start(s32[1,1024]{1,0:T(1,128)S(1)} %bitcast.6), channel_id=1, source_target_pairs={{4,0},{5,1},{6,2},{7,3},{8,4},{9,5},{10,6},{11,7},{12,8},{13,9},{1... | collective-permute-start | bytes 12296 | tf_op jit(solution)/shard_map/ppermute | solution.py:312
  76.6 8.9 %collective-permute-start.2 = (bf16[1040,768]{1,0:T(8,128)(2,1)S(1)}, bf16[1040,768]{1,0:T(8,128)(2,1)S(1)}, u32[]{:S(2)}, u32[]{:S(2)}) collective-permute-start(bf16[1040,768]{1,0:T(8,128)(2,1)S(1)} %get-tuple-element.15.own_ref), channel_id=1, source_target_pairs={{0,1},{1,0},{2,3},{3,2},{4,5},{5,4},{6,7},{7,6},{8,9},{9,8},{10,11... | collective-permute-start | bytes 4792328 | tf_op jit(solution)/shard_map/ppermute | solution.py:312
  89.8 6.2 %collective-permute-start.3 = (f32[1,1024]{1,0:T(1,128)S(1)}, f32[1,1024]{1,0:T(1,128)S(1)}, u32[]{:S(2)}, u32[]{:S(2)}) collective-permute-start(f32[1,1024]{1,0:T(1,128)S(1)} %get-tuple-element.20), channel_id=1, source_target_pairs={{0,1},{1,0},{2,3},{3,2},{4,5},{5,4},{6,7},{7,6},{8,9},{9,8},{10,11... | collective-permute-start | bytes 12296 | tf_op jit(solution)/shard_map/ppermute | solution.py:312
  89.9 10.0 %collective-permute-start.4 = (f32[1,1024]{1,0:T(1,128)S(1)}, f32[1,1024]{1,0:T(1,128)S(1)}, u32[]{:S(2)}, u32[]{:S(2)}) collective-permute-start(f32[1,1024]{1,0:T(1,128)S(1)} %get-tuple-element.21), channel_id=1, source_target_pairs={{0,2},{1,3},{2,4},{3,5},{4,6},{5,7},{6,8},{7,9},{8,10},{9,11},{10,... | collective-permute-start | bytes 12296 | tf_op jit(solution)/shard_map/ppermute | solution.py:312
  94.1 10.3 %collective-permute-start.5 = (f32[1,1024]{1,0:T(1,128)S(1)}, f32[1,1024]{1,0:T(1,128)S(1)}, u32[]{:S(2)}, u32[]{:S(2)}) collective-permute-start(f32[1,1024]{1,0:T(1,128)S(1)} %get-tuple-element.22), channel_id=1, source_target_pairs={{0,4},{1,5},{2,6},{3,7},{4,8},{5,9},{6,10},{7,11},{8,12},{9,13},{1... | collective-permute-start | bytes 12296 | tf_op jit(solution)/shard_map/ppermute | solution.py:312
